TPU v7x, 32 devices: a whole 2x2x4 slice. The times are simulated.
32 devices in a mesh: dp: 4 (over y, core), lat: 8 (over z, x).
Axes of the slice: x: 2, y: 2, z: 4, core: 2. Of those that a mesh axis runs over, the one named last changes fastest.
Arguments:
- tokens: bfloat16 [2, 4, 8, 180, 768], P(None, 'dp', 'lat'), may hold values from -6 to 6
- boxes: int32 [2, 4, 2], P(None, 'dp'), may hold values from 4 to 180, as said below
- patch_mask: int32 [2, 4, 8, 180], P(None, 'dp', 'lat'), may hold values 0 or 1
- pre_gain: float32 [768], replicated, may hold values from 0.25 to 1.75
- pre_shift: float32 [768], replicated, may hold values from -3 to 3
- filter_inner: bfloat16 [2, 8, 96, 96], replicated, may hold values from -0.4375 to 0.4375
- filter_inner_bias: float32 [2, 8, 96], replicated, may hold values from -3 to 3
- filter_outer: bfloat16 [2, 8, 96, 96], replicated, may hold values from -0.4375 to 0.4375
- filter_outer_bias: float32 [2, 8, 96], replicated, may hold values from -3 to 3
- post_gain: float32 [768], replicated, may hold values from 0.25 to 1.75
- post_shift: float32 [768], replicated, may hold values from -3 to 3
- expand_weight: bfloat16 [768, 3072], replicated, may hold values from -0.21875 to 0.21875
- expand_bias: float32 [3072], replicated, may hold values from -3 to 3
- reduce_weight: bfloat16 [3072, 768], replicated, may hold values from -0.109375 to 0.109375
- reduce_bias: float32 [768], replicated, may hold values from -3 to 3
- cotangent: bfloat16 [2, 4, 8, 180, 768], P(None, 'dp', 'lat'), may hold values from -6 to 6
Outputs:
- block_out: bfloat16 [2, 4, 8, 180, 768], P(None, 'dp', 'lat')
- grad_tokens: float32 [2, 4, 8, 180, 768], P(None, 'dp', 'lat')
- grad_pre_gain: float32 [768], replicated
- grad_pre_shift: float32 [768], replicated
- grad_filter_inner: float32 [2, 8, 96, 96], replicated
- grad_filter_inner_bias: float32 [2, 8, 96], replicated
- grad_filter_outer: float32 [2, 8, 96, 96], replicated
- grad_filter_outer_bias: float32 [2, 8, 96], replicated
- grad_post_gain: float32 [768], replicated
- grad_post_shift: float32 [768], replicated
- grad_expand_weight: float32 [768, 3072], P(None, ('dp', 'lat'))
- grad_expand_bias: float32 [3072], replicated
- grad_reduce_weight: float32 [3072, 768], P(('dp', 'lat'))
- grad_reduce_bias: float32 [768], replicated
Inputs may be any that keep to these rules, and one draw needn't show every extreme that they name: boxes[m,c,0] lies between 4 and 8, boxes[m,c,1] between 90 and 180. For each crop index c, at least one of the 2 micro-batches m has boxes[m,c] equal to the full box of 8 rows and 180 columns.
All inputs are finite; a program needn't handle non-finite values. No bound on the sum of `patch_mask` on one device may be relied on, other than what follows from the above.
Results may differ from a plain program's by a relative error of at most 0.013.
The roundings to bfloat16 on the way count: a program that leaves them out, or rounds other values in their place, can miss the bound.
Values may be sent and summed in bfloat16 or wider, within the bound.
No kernel may reach another device: no remote copies, remote signals or barrier semaphores. Data moves between devices by JAX's collectives and lax.ppermute only.
A program may use at most 192 MiB of HBM per device.

v0:
```python
import functools
import math

import jax
import jax.numpy as jnp
import ml_dtypes
import numpy as np
from jax import lax
from jax.experimental import pallas as pl
from jax.experimental.pallas import tpu as pltpu
from jax.sharding import PartitionSpec as P

MODES = 64
shrink_level = 0.01
epsilon = 1e-05
inv_root_two = 1.0 / math.sqrt(2.0)
inv_root_tau = 1.0 / math.sqrt(2.0 * math.pi)
f32 = jnp.float32
bf16 = jnp.bfloat16


def table_pair(out_count, in_count, length):
    phase = np.arange(out_count)[:, None] * np.arange(in_count)[None, :] % length
    angle = phase.astype(np.float32) * np.float32(2.0 * math.pi / length)
    return np.cos(angle).astype(np.float32), np.sin(angle).astype(np.float32)


def low(values):
    return values.astype(np.float32).astype(ml_dtypes.bfloat16)


def make_tables(lon_cells, lat_count, block_size, chunk):
    lon_factor = np.float32(1.0 / math.sqrt(lon_cells))
    cosine, sine = table_pair(MODES, lon_cells, lon_cells)
    weight = np.where(np.arange(MODES) == 0, 1.0, 2.0).astype(np.float32)[:, None]
    forward = low(np.concatenate([cosine, -sine]) * lon_factor)
    inverse = low(np.concatenate([cosine * weight, -sine * weight]) * lon_factor)
    cosine, sine = table_pair(lat_count, lat_count, lat_count)
    lat_factor = np.float32(1.0 / math.sqrt(lat_count))
    same = np.eye(chunk, dtype=np.float32)
    cosine = np.kron(low(cosine * lat_factor).astype(np.float32), same)
    sine = np.kron(low(sine * lat_factor).astype(np.float32), same)
    turn_fwd = low(np.concatenate([cosine, sine], axis=1))
    turn_inv = low(np.concatenate([cosine, -sine], axis=1))
    eye, none = np.eye(block_size), np.zeros((block_size, block_size))
    swap = low(np.block([[none, -eye], [eye, none]]))
    return dict(
        fwd=forward, fwd_t=forward.T.copy(), inv=inverse, inv_t=inverse.T.copy(),
        turn_fwd=turn_fwd, turn_inv=turn_inv, swap=swap,
    )


def dot(a, b, ca, cb):
    return lax.dot_general(a, b, (((ca,), (cb,)), ((), ())), preferred_element_type=f32)


def row_mean(values):
    return jnp.sum(values, axis=-1, keepdims=True) * (1.0 / values.shape[-1])


def norm_parts(values):
    centered = values - row_mean(values)
    inv_scale = lax.rsqrt(row_mean(centered * centered) + epsilon)
    return centered * inv_scale, inv_scale


def norm_back(grad_normed, unit_values, inv_scale, gain):
    grad_unit = grad_normed * gain
    plain, cross = row_mean(grad_unit), row_mean(grad_unit * unit_values)
    return inv_scale * (grad_unit - plain - unit_values * cross)


def gelu_pair(values):
    half = 0.5 * (1.0 + lax.erf(values * inv_root_two))
    return values * half, half + values * jnp.exp(-0.5 * values * values) * inv_root_tau


def shrink_pair(values):
    inverse = lax.rsqrt(values * values + shrink_level * shrink_level)
    slope = 1.0 - shrink_level * shrink_level * shrink_level * inverse * inverse * inverse
    return values - shrink_level * values * inverse, slope


def valid_row(box_ref, row_ref, hole_ref, lat_rows, cells):
    item = pl.program_id(0)
    crop, row = item // lat_rows, row_ref[0] + item % lat_rows
    limit = jnp.where(row < box_ref[2 * crop], box_ref[2 * crop + 1], 0)
    column = lax.broadcasted_iota(jnp.int32, (1, cells), 1)
    return jnp.where((column < limit) & (hole_ref[0] > 0), 1.0, 0.0)


def as_column(row):
    cells = row.shape[1]
    down = lax.broadcasted_iota(jnp.int32, (cells, cells), 0)
    along = lax.broadcasted_iota(jnp.int32, (cells, cells), 1)
    return jnp.sum(jnp.where(down == along, row, 0.0), axis=1, keepdims=True)


def put_modes(send_ref, spectrum, block_size, sub):
    spectrum = spectrum.astype(bf16)
    own = MODES // sub
    for block in range(spectrum.shape[1] // block_size):
        cut = spectrum[:, block * block_size : (block + 1) * block_size]
        both = jnp.concatenate([cut[:MODES], cut[MODES:]], axis=1)
        for j in range(sub):
            send_ref[block * sub + j, 0] = both[j * own : (j + 1) * own]


def get_modes(recv_ref, block_size, sub):
    groups = recv_ref.shape[0]
    real, imag = [], []
    for block in range(groups // sub):
        parts = [recv_ref[block * sub + j, 0] for j in range(sub)]
        both = parts[0] if sub == 1 else jnp.concatenate(parts, axis=0)
        real.append(both[:, :block_size])
        imag.append(both[:, block_size:])
    real, imag = jnp.concatenate(real, axis=1), jnp.concatenate(imag, axis=1)
    return jnp.concatenate([real, imag], axis=0)


def turn_rows(src_ref, dst_ref, table, swap, chunk):
    lat_count, points, wide = src_ref.shape
    for at in range(0, points, chunk):
        piece = src_ref[:, at : at + chunk, :].reshape(lat_count * chunk, wide)
        other = dot(piece, swap, 1, 0).astype(bf16)
        out = dot(table, jnp.concatenate([piece, other], axis=0), 1, 0)
        dst_ref[:, at : at + chunk, :] = out.astype(bf16).reshape(lat_count, chunk, wide)


def pre_kernel(
    lat_rows, block_size, sub,
    box_ref, row_ref, token_ref, cot_ref, hole_ref, gain_ref, shift_ref, table_ref,
    send_ref, cot_pad_ref,
):
    cells = token_ref.shape[1]
    valid = valid_row(box_ref, row_ref, hole_ref, lat_rows, cells)
    unit, _ = norm_parts(token_ref[0].astype(f32))
    normed = (unit * gain_ref[...] + shift_ref[...]).astype(bf16)
    table = (table_ref[...].astype(f32) * valid).astype(bf16)
    put_modes(send_ref, dot(table, normed, 1, 0), block_size, sub)
    pad = cot_pad_ref.shape[1] - cells
    cot_pad_ref[0, :cells] = cot_ref[0]
    if pad:
        cot_pad_ref[0, cells:] = jnp.zeros((pad, cot_ref.shape[2]), bf16)


def filter_kernel(
    chunk,
    recv_ref, inner_ref, inner_bias_ref, outer_ref, outer_bias_ref, turn_fwd_ref, turn_inv_ref, swap_ref,
    send_ref, spec_ref, hid_ref, slope_ref, shrunk_ref, filt_ref,
):
    turn_rows(recv_ref, spec_ref, turn_fwd_ref[...], swap_ref[...], chunk)
    for p in range(spec_ref.shape[0]):
        pre = dot(spec_ref[p], inner_ref[...], 1, 0) + inner_bias_ref[...]
        hid, slope = gelu_pair(pre)
        hid = hid.astype(bf16)
        hid_ref[p] = hid
        slope_ref[p] = slope
        mid = dot(hid, outer_ref[...], 1, 0) + outer_bias_ref[...]
        filt, shrunk = shrink_pair(mid)
        filt_ref[p] = filt.astype(bf16)
        shrunk_ref[p] = shrunk
    turn_rows(filt_ref, send_ref, turn_inv_ref[...], swap_ref[...], chunk)


def mix_kernel(
    lat_rows, block_size, sub,
    box_ref, row_ref, recv_ref, token_ref, hole_ref, gain_ref, shift_ref,
    post_gain_ref, post_shift_ref, table_ref,
    mixed_ref, post_ref,
):
    cells = token_ref.shape[1]
    valid = as_column(valid_row(box_ref, row_ref, hole_ref, lat_rows, cells))
    tokens = token_ref[0].astype(f32)
    unit, _ = norm_parts(tokens)
    normed = unit * gain_ref[...] + shift_ref[...]
    filtered = dot(table_ref[...], get_modes(recv_ref, block_size, sub), 1, 0)
    mixed = tokens + normed + valid * filtered
    mixed_ref[0] = mixed
    unit, _ = norm_parts(mixed)
    post_ref[0, :cells] = (unit * post_gain_ref[...] + post_shift_ref[...]).astype(bf16)
    pad = post_ref.shape[1] - cells
    if pad:
        post_ref[0, cells:] = jnp.zeros((pad, token_ref.shape[2]), bf16)


def feed_kernel(
    core_ref, post_own_ref, post_other_ref, cot_own_ref, cot_other_ref,
    expand_ref, expand_bias_ref, reduce_ref,
    group_a_ref, group_b_ref, group_c_ref, bias_grad_ref,
    out_own_ref, out_other_ref, grad_own_ref, grad_other_ref,
    post_ref, cot_ref, out_ref, grad_ref,
):
    step = pl.program_id(0)
    rows = post_own_ref.shape[0]

    @pl.when(step == 0)
    def _():
        post_ref[:rows] = post_own_ref[...]
        post_ref[rows:] = post_other_ref[...]
        cot_ref[:rows] = cot_own_ref[...]
        cot_ref[rows:] = cot_other_ref[...]
        out_ref[...] = jnp.zeros_like(out_ref)
        grad_ref[...] = jnp.zeros_like(grad_ref)

    expand, reduce = expand_ref[...], reduce_ref[...]
    post, cot = post_ref[...], cot_ref[...]
    hidden, slope = gelu_pair(dot(post, expand, 1, 0) + expand_bias_ref[...])
    hidden = hidden.astype(bf16)
    grad = (dot(cot, reduce, 1, 1) * slope).astype(bf16)
    bias_grad_ref[...] = jnp.sum(grad.astype(f32), axis=0, keepdims=True)
    out_ref[...] += dot(hidden, reduce, 1, 0)
    grad_ref[...] += dot(grad, expand, 1, 1)
    grad_expand = dot(grad, post, 0, 0).astype(bf16)
    grad_reduce = dot(hidden, cot, 0, 0).astype(bf16)
    lanes = group_a_ref.shape[1] // 2
    for at, group_ref in enumerate((group_a_ref, group_b_ref, group_c_ref)):
        group_ref[:, :lanes] = grad_expand[:, at * lanes : (at + 1) * lanes]
        group_ref[:, lanes:] = grad_reduce[:, at * lanes : (at + 1) * lanes]

    @pl.when(step == pl.num_programs(0) - 1)
    def _():
        out_own_ref[...] = out_ref[:rows]
        out_other_ref[...] = out_ref[rows:].astype(bf16)
        grad_own_ref[...] = grad_ref[:rows]
        grad_other_ref[...] = grad_ref[rows:].astype(bf16)


def add_sum(ref, value):
    value = jnp.sum(value, axis=0, keepdims=True)

    @pl.when(pl.program_id(0) == 0)
    def _():
        ref[...] = value

    @pl.when(pl.program_id(0) > 0)
    def _():
        ref[...] += value


def post_kernel(
    lat_rows, block_size, sub,
    box_ref, row_ref, mixed_ref, out_own_ref, out_other_ref, grad_own_ref, grad_other_ref,
    cot_ref, hole_ref, gain_ref, bias_ref, table_ref,
    result_ref, grad_mixed_ref, send_ref, gain_grad_ref, shift_grad_ref, bias_grad_ref,
):
    cells = mixed_ref.shape[1]
    valid = valid_row(box_ref, row_ref, hole_ref, lat_rows, cells)
    mixed = mixed_ref[0]
    out = out_own_ref[0, :cells] + out_other_ref[0, :cells].astype(f32)
    result_ref[0] = (mixed + (out + bias_ref[...])).astype(bf16)
    grad = grad_own_ref[0, :cells] + grad_other_ref[0, :cells].astype(f32)
    unit, inv_scale = norm_parts(mixed)
    add_sum(gain_grad_ref, grad * unit)
    add_sum(shift_grad_ref, grad)
    cot = cot_ref[0].astype(f32)
    add_sum(bias_grad_ref, cot)
    grad_mixed = cot + norm_back(grad, unit, inv_scale, gain_ref[...])
    grad_mixed_ref[0] = grad_mixed
    table = (table_ref[...].astype(f32) * valid).astype(bf16)
    put_modes(send_ref, dot(table, grad_mixed.astype(bf16), 1, 0), block_size, sub)


def filter_back_kernel(
    chunk,
    recv_ref, spec_ref, hid_ref, slope_ref, shrunk_ref, inner_ref, outer_ref,
    turn_fwd_ref, turn_inv_ref, swap_ref,
    send_ref, weight_grad_ref, bias_grad_ref,
    turned_ref, grad_mid_ref, grad_pre_ref,
):
    lat_count, points, wide = recv_ref.shape
    turn_rows(recv_ref, turned_ref, turn_fwd_ref[...], swap_ref[...], chunk)
    inner_bias = jnp.zeros((1, wide), f32)
    outer_bias = jnp.zeros((1, wide), f32)
    for p in range(lat_count):
        grad_mid = (turned_ref[p].astype(f32) * shrunk_ref[p]).astype(bf16)
        grad_mid_ref[p] = grad_mid
        outer_bias += jnp.sum(grad_mid.astype(f32), axis=0, keepdims=True)
        grad_pre = (dot(grad_mid, outer_ref[...], 1, 1) * slope_ref[p]).astype(bf16)
        grad_pre_ref[p] = grad_pre
        inner_bias += jnp.sum(grad_pre.astype(f32), axis=0, keepdims=True)
        turned_ref[p] = dot(grad_pre, inner_ref[...], 1, 1).astype(bf16)
    turn_rows(turned_ref, send_ref, turn_inv_ref[...], swap_ref[...], chunk)
    bias_grad_ref[0:1] = inner_bias
    bias_grad_ref[1:2] = outer_bias
    flat = (lat_count * points, wide)
    half = wide // 2
    pairs = ((spec_ref, grad_pre_ref), (hid_ref, grad_mid_ref))
    for at, (left, right) in enumerate(pairs):
        grad = dot(left[...].reshape(flat), right[...].reshape(flat), 0, 0)
        weight_grad_ref[at, 0] = grad[:half, :half] + grad[half:, half:]
        weight_grad_ref[at, 1] = grad[:half, half:] - grad[half:, :half]


def last_kernel(
    lat_rows, block_size, sub,
    box_ref, row_ref, recv_ref, token_ref, grad_mixed_ref, hole_ref, gain_ref, table_ref,
    result_ref, gain_grad_ref, shift_grad_ref,
):
    cells = token_ref.shape[1]
    valid = as_column(valid_row(box_ref, row_ref, hole_ref, lat_rows, cells))
    grad_masked = dot(table_ref[...], get_modes(recv_ref, block_size, sub), 1, 0)
    grad_mixed = grad_mixed_ref[0]
    grad = grad_mixed + valid * grad_masked
    unit, inv_scale = norm_parts(token_ref[0].astype(f32))
    add_sum(gain_grad_ref, grad * unit)
    add_sum(shift_grad_ref, grad)
    result_ref[0] = grad_mixed + norm_back(grad, unit, inv_scale, gain_ref[...])


def call(kernel, grid, in_specs, out_specs, out_shape, args, prefetch=0, scratch=(), flops=0):
    moved = sum(a.size * a.dtype.itemsize for a in args)
    moved += sum(math.prod(s.shape) * np.dtype(s.dtype).itemsize for s in out_shape)
    return pl.pallas_call(
        kernel,
        out_shape=out_shape,
        grid_spec=pltpu.PrefetchScalarGridSpec(
            num_scalar_prefetch=prefetch,
            grid=grid,
            in_specs=in_specs,
            out_specs=out_specs,
            scratch_shapes=scratch,
        ),
        compiler_params=pltpu.CompilerParams(
            dimension_semantics=("arbitrary",), vmem_limit_bytes=48 << 20
        ),
        cost_estimate=pl.CostEstimate(flops=int(flops), bytes_accessed=int(moved), transcendentals=0),
    )(*args)


def shape(dims, dtype):
    return jax.ShapeDtypeStruct(tuple(dims), dtype)


def item_spec(dims):
    rest = (0,) * (len(dims) - 1)
    return pl.BlockSpec((1,) + tuple(dims[1:]), lambda i, *_: (i,) + rest)


def mode_spec(dims):
    return pl.BlockSpec((dims[0], 1) + tuple(dims[2:]), lambda i, *_: (0, i, 0, 0))


def whole_spec(dims):
    rest = (0,) * len(dims)
    return pl.BlockSpec(tuple(dims), lambda *_: rest)


def pair_swap(operand, axis_name, bit):
    size = lax.axis_size(axis_name)
    return lax.ppermute(operand, axis_name, [(i, i ^ bit) for i in range(size)])


def axis_bits(axis_name):
    size = lax.axis_size(axis_name)
    return [1 << i for i in range(size.bit_length() - 1)]


def all_sum(vector):
    for axis_name in ("dp", "lat"):
        for bit in axis_bits(axis_name):
            vector = vector + pair_swap(vector, axis_name, bit)
    return vector


def halving_scatter(part, names, order):
    for step in order:
        dim = names.index(step)
        axis_name, bit = step
        own = (lax.axis_index(axis_name) // bit) % 2
        keep = lax.dynamic_slice_in_dim(part, own, 1, dim).astype(f32)
        away = lax.dynamic_slice_in_dim(part, 1 - own, 1, dim).astype(bf16)
        dims = away.shape
        away = pair_swap(away.reshape(-1, dims[-1]), axis_name, bit).reshape(dims)
        part = keep + away.astype(f32)
        if step != order[-1]:
            part = part.astype(bf16)
    return part.reshape(part.shape[-2:])


def body(
    tokens,
    boxes,
    patch_mask,
    pre_gain,
    pre_shift,
    filter_inner,
    filter_inner_bias,
    filter_outer,
    filter_outer_bias,
    post_gain,
    post_shift,
    expand_weight,
    expand_bias,
    reduce_weight,
    reduce_bias,
    cotangent,
):
    micro_count, crop_count, lat_rows, cells, width = tokens.shape
    groups = lax.axis_size("lat")
    lat_count = lat_rows * groups
    block_count, block_size = filter_inner.shape[1:3]
    sub = groups // block_count
    modes_own = MODES // sub
    crops = micro_count * crop_count
    items = crops * lat_rows
    points = crops * modes_own
    wide = 2 * block_size
    padded = -(-cells // 16) * 16
    rows = items * padded
    chunk = 16
    hidden_width = expand_weight.shape[1]
    dp_size = lax.axis_size("dp")
    lat_index, dp_index = lax.axis_index("lat"), lax.axis_index("dp")
    own_block = lat_index // sub
    tables = {k: jnp.asarray(v) for k, v in make_tables(cells, lat_count, block_size, chunk).items()}

    box = boxes.reshape(-1)
    own_row = (lat_index * lat_rows).astype(jnp.int32).reshape(1)
    core = (dp_index % 2).astype(jnp.int32).reshape(1)
    token_items = tokens.reshape(items, cells, width)
    cot_items = cotangent.reshape(items, cells, width)
    holes = patch_mask.reshape(items, 1, cells)
    gain_pre, shift_pre = pre_gain.reshape(1, width), pre_shift.reshape(1, width)
    gain_post, shift_post = post_gain.reshape(1, width), post_shift.reshape(1, width)
    row_item, hole_item = (items, cells, width), (items, 1, cells)
    pad_item = (items, padded, width)
    mode_dims = (groups, items, modes_own, wide)
    vector = (1, width)
    names = (lat_rows, block_size, sub)
    lon_flops = 2 * items * 2 * MODES * cells * width

    def exchange(both, by_rows):
        if by_rows:
            both = both.reshape(groups, crops, lat_rows, modes_own, wide).swapaxes(1, 2)
            both = both.reshape(groups, lat_rows * points, wide)
            both = lax.all_to_all(both, "lat", 0, 0, tiled=True)
            return both.reshape(lat_count, points, wide)
        both = lax.all_to_all(both.reshape(groups, lat_rows * points, wide), "lat", 0, 0, tiled=True)
        both = both.reshape(groups, lat_rows, crops, modes_own, wide).swapaxes(1, 2)
        return both.reshape(mode_dims)

    def own_matrix(matrix):
        pair = lax.dynamic_index_in_dim(matrix, own_block, 1, keepdims=False)
        top = jnp.concatenate([pair[0], pair[1]], axis=1)
        under = jnp.concatenate([-pair[1], pair[0]], axis=1)
        return jnp.concatenate([top, under], axis=0)

    def own_bias(bias):
        return lax.dynamic_index_in_dim(bias, own_block, 1, keepdims=False).reshape(1, wide)

    args = (box, own_row, token_items, cot_items, holes, gain_pre, shift_pre, tables["fwd"])
    send, cot_pad = call(
        functools.partial(pre_kernel, *names),
        (items,),
        [item_spec(row_item), item_spec(row_item), item_spec(hole_item)]
        + [whole_spec(a.shape) for a in args[5:]],
        [mode_spec(mode_dims), item_spec(pad_item)],
        [shape(mode_dims, bf16), shape(pad_item, bf16)],
        args,
        prefetch=2,
        flops=lon_flops,
    )
    cot_pad = cot_pad.reshape(rows, width)
    cot_other = pair_swap(cot_pad, "dp", 1)
    recv = exchange(send, True)

    spectrum = (lat_count, points, wide)
    filter_flops = 4 * lat_count * points * wide * wide
    inner, outer = own_matrix(filter_inner), own_matrix(filter_outer)
    args = (
        recv, inner, own_bias(filter_inner_bias), outer, own_bias(filter_outer_bias),
        tables["turn_fwd"], tables["turn_inv"], tables["swap"],
    )
    send, spec, hid, slope, shrunk = call(
        functools.partial(filter_kernel, chunk),
        (1,),
        [whole_spec(a.shape) for a in args],
        [whole_spec(spectrum)] * 5,
        [shape(spectrum, t) for t in (bf16, bf16, bf16, f32, f32)],
        args,
        scratch=[pltpu.VMEM(spectrum, bf16)],
        flops=filter_flops,
    )
    recv = exchange(send, False)

    args = (
        box, own_row, recv, token_items, holes, gain_pre, shift_pre, gain_post, shift_post,
        tables["inv_t"],
    )
    mixed, post = call(
        functools.partial(mix_kernel, *names),
        (items,),
        [mode_spec(mode_dims), item_spec(row_item), item_spec(hole_item)]
        + [whole_spec(a.shape) for a in args[5:]],
        [item_spec(row_item), item_spec(pad_item)],
        [shape(row_item, f32), shape(pad_item, bf16)],
        args,
        prefetch=2,
        flops=lon_flops,
    )
    post = post.reshape(rows, width)
    post_other = pair_swap(post, "dp", 1)

    run = hidden_width // dp_size
    tile = next(t for t in (256, 384, 128, run) if run % t == 0)
    per_run = run // tile
    hidden_own = hidden_width // 2
    lanes = width // 3

    def column(j, core_ref):
        return ((j // per_run) * 2 + core_ref[0]) * per_run + j % per_run

    args = (
        core, post, post_other, cot_pad, cot_other,
        expand_weight, expand_bias.reshape(1, hidden_width), reduce_weight,
    )
    group_spec = pl.BlockSpec((tile, 2 * lanes), lambda j, _: (j, 0))
    flat = (rows, width)
    *parts, grad_expand_b, out_own, out_other, grad_own, grad_other = call(
        feed_kernel,
        (hidden_own // tile,),
        [whole_spec(flat)] * 4
        + [
            pl.BlockSpec((width, tile), lambda j, c: (0, column(j, c))),
            pl.BlockSpec((1, tile), lambda j, c: (0, column(j, c))),
            pl.BlockSpec((tile, width), lambda j, c: (column(j, c), 0)),
        ],
        [group_spec] * 3
        + [pl.BlockSpec((1, tile), lambda j, _: (0, j))]
        + [whole_spec(flat)] * 4,
        [shape((hidden_own, 2 * lanes), bf16)] * 3
        + [shape((1, hidden_own), f32)]
        + [shape(flat, t) for t in (f32, bf16, f32, bf16)],
        args,
        prefetch=1,
        scratch=[pltpu.VMEM((2 * rows, width), t) for t in (bf16, bf16, f32, f32)],
        flops=6 * 2 * 2 * rows * width * hidden_own,
    )
    grad_other = pair_swap(grad_other, "dp", 1).reshape(pad_item)
    out_other = pair_swap(out_other, "dp", 1).reshape(pad_item)

    args = (
        box, own_row, mixed, out_own.reshape(pad_item), out_other, grad_own.reshape(pad_item),
        grad_other, cot_items, holes, gain_post, reduce_bias.reshape(1, width), tables["inv"],
    )
    result, grad_mixed, send, grad_post_g, grad_post_s, grad_reduce_b = call(
        functools.partial(post_kernel, *names),
        (items,),
        [item_spec(row_item)] + [item_spec(pad_item)] * 4
        + [item_spec(row_item), item_spec(hole_item)]
        + [whole_spec(a.shape) for a in args[9:]],
        [item_spec(row_item), item_spec(row_item), mode_spec(mode_dims)] + [whole_spec(vector)] * 3,
        [shape(row_item, bf16), shape(row_item, f32), shape(mode_dims, bf16)] + [shape(vector, f32)] * 3,
        args,
        prefetch=2,
        flops=lon_flops,
    )
    recv = exchange(send, True)

    lat_bits = [("lat", b) for b in axis_bits("lat")]
    dp_bits = [("dp", b) for b in axis_bits("dp")[1:]]
    orders = (
        dp_bits + lat_bits,
        lat_bits + dp_bits,
        lat_bits[1:2] + dp_bits + lat_bits[:1] + lat_bits[2:],
    )
    bit_names = dp_bits[::-1] + lat_bits[::-1]
    own_rows = hidden_width // (dp_size * groups)
    summed = []
    for part, order in zip(parts, orders):
        part = part.reshape([2] * len(bit_names) + [own_rows, 2 * lanes])
        summed.append(halving_scatter(part, bit_names, order))
    expand_part = jnp.concatenate([s[:, :lanes] for s in summed], axis=1).T
    reduce_part = jnp.concatenate([s[:, lanes:] for s in summed], axis=1)

    args = (
        recv, spec, hid, slope, shrunk, inner, outer,
        tables["turn_fwd"], tables["turn_inv"], tables["swap"],
    )
    weight_dims = (2, 2, block_size, block_size)
    send, filters, filter_bias = call(
        functools.partial(filter_back_kernel, chunk),
        (1,),
        [whole_spec(a.shape) for a in args],
        [whole_spec(spectrum), whole_spec(weight_dims), whole_spec((2, wide))],
        [shape(spectrum, bf16), shape(weight_dims, f32), shape((2, wide), f32)],
        args,
        scratch=[pltpu.VMEM(spectrum, bf16)] * 3,
        flops=2 * filter_flops,
    )
    recv = exchange(send, False)

    args = (
        box, own_row, recv, token_items, grad_mixed, holes, gain_pre, tables["fwd_t"],
    )
    grad_tokens, grad_pre_g, grad_pre_s = call(
        functools.partial(last_kernel, *names),
        (items,),
        [mode_spec(mode_dims), item_spec(row_item), item_spec(row_item), item_spec(hole_item)]
        + [whole_spec(a.shape) for a in args[6:]],
        [item_spec(row_item)] + [whole_spec(vector)] * 2,
        [shape(row_item, f32)] + [shape(vector, f32)] * 2,
        args,
        prefetch=2,
        flops=lon_flops,
    )

    filters = filters.reshape(-1, block_size)
    for bit in axis_bits("dp"):
        filters = filters + pair_swap(filters, "dp", bit)
    for bit in [b for b in axis_bits("lat") if b < sub]:
        filters = filters + pair_swap(filters, "lat", bit)
    filters = jnp.broadcast_to(filters.astype(bf16), (groups,) + filters.shape)
    filters = lax.all_to_all(filters, "lat", 0, 0, tiled=True)[::sub].astype(f32)
    filters = filters.reshape((block_count,) + weight_dims).transpose(1, 2, 0, 3, 4)

    def place(bias):
        spread = jnp.zeros((2, block_count, block_size), f32)
        return lax.dynamic_update_slice_in_dim(
            spread, bias.reshape(2, 1, block_size), own_block, 1
        ).reshape(-1)

    spread = jnp.zeros((dp_size // 2, 2, run), f32)
    spread = lax.dynamic_update_slice_in_dim(
        spread, grad_expand_b.reshape(dp_size // 2, 1, run), core[0], 1
    )
    small = [
        grad_pre_g.reshape(-1),
        grad_pre_s.reshape(-1),
        place(filter_bias[0]),
        place(filter_bias[1]),
        grad_post_g.reshape(-1),
        grad_post_s.reshape(-1),
        spread.reshape(-1),
        grad_reduce_b.reshape(-1),
    ]
    lengths = [v.shape[0] for v in small]
    total = all_sum(jnp.concatenate(small).reshape(-1, 128)).reshape(-1)
    split, at = [], 0
    for length in lengths:
        split.append(total[at : at + length])
        at += length
    return (
        result.reshape(tokens.shape),
        grad_tokens.reshape(tokens.shape),
        split[0],
        split[1],
        filters[0],
        split[2].reshape(2, block_count, block_size),
        filters[1],
        split[3].reshape(2, block_count, block_size),
        split[4],
        split[5],
        expand_part,
        split[6],
        reduce_part,
        split[7],
    )


def solution(mesh):
    rows = P(None, "dp", "lat", None, None)
    in_specs = (rows, P(None, "dp", None), P(None, "dp", "lat", None)) + (P(),) * 12 + (rows,)
    out_specs = (
        (rows, rows)
        + (P(),) * 8
        + (P(None, ("dp", "lat")), P(), P(("dp", "lat"), None), P())
    )
    return jax.shard_map(body, mesh=mesh, in_specs=in_specs, out_specs=out_specs, check_vma=False)
```

profile of v0, /device:TPU:0, one launch (start us, length us, event | category | flops | bytes accessed | tf_op | source)
XLA Modules:
  0.0 193.3 jit_solution(11693126803224009326)
XLA Ops:
  8.8 7.3 %all-to-all-start = ((bf16[8,128,192]{1,2,0:T(8,128)(2,1)}), bf16[8,128,192]{1,2,0:T(8,128)(2,1)S(1)}, u32[]{:S(2)}, u32[]{:S(2)}) async-start(bf16[8,128,192]{1,2,0:T(8,128)(2,1)} %copy.53), calls=%async_computation | async-start | bytes 786432 | tf_op jit(solution)/shard_map/all_to_all | solution.py:437
  18.7 9.0 %all-to-all-done = bf16[8,128,192]{1,2,0:T(8,128)(2,1)S(1)} async-done(((bf16[8,128,192]{1,2,0:T(8,128)(2,1)}), bf16[8,128,192]{1,2,0:T(8,128)(2,1)S(1)}, u32[]{:S(2)}, u32[]{:S(2)}) %all-to-all-start) | async-done | bytes 393248 | tf_op jit(solution)/shard_map/all_to_all | solution.py:437
  34.6 3.8 %all-to-all-start.1 = ((bf16[8,128,192]{1,2,0:T(8,128)(2,1)}), bf16[8,128,192]{1,2,0:T(8,128)(2,1)S(1)}, u32[]{:S(2)}, u32[]{:S(2)}) async-start(bf16[8,128,192]{1,2,0:T(8,128)(2,1)} %copy.55), calls=%async_computation.1 | async-start | bytes 786432 | tf_op jit(solution)/shard_map/all_to_all | solution.py:439
  38.5 11.5 %all-to-all-done.1 = bf16[8,128,192]{1,2,0:T(8,128)(2,1)S(1)} async-done(((bf16[8,128,192]{1,2,0:T(8,128)(2,1)}), bf16[8,128,192]{1,2,0:T(8,128)(2,1)S(1)}, u32[]{:S(2)}, u32[]{:S(2)}) %all-to-all-start.1) | async-done | bytes 393248 | tf_op jit(solution)/shard_map/all_to_all | solution.py:439
  50.2 2.6 %shard_map.328 = (f32[2,180,768]{2,1,0:T(8,128)S(1)}, bf16[2,192,768]{2,1,0:T(8,128)(2,1)}) custom-call(s32[4]{0:T(128)S(1)} %reshape.356.box_ref, s32[1]{0:T(128)} %bitcast.row_ref, bf16[8,2,64,192]{3,2,1,0:T(8,128)(2,1)S(1)} %bitcast.112, bf16[2,180,768]{2,1,0:T(8,128)(2,1)S(1)} %get-tuple-element.136.token_ref, s32[2,1,180]{2,1,0:T(1,128)S(1)} %bitcast.121, ...), custom_call_target="tpu_custom_call" | custom-call | flops 70778880 | bytes 2701748 | tf_op jit(solution)/shard_map/pallas_call | solution.py:314
  52.9 2.2 %collective-permute-done.post_other_ref = bf16[384,768]{1,0:T(8,128)(2,1)S(1)} collective-permute-done((bf16[384,768]{1,0:T(8,128)(2,1)}, bf16[384,768]{1,0:T(8,128)(2,1)S(1)}, u32[]{:S(2)}, u32[]{:S(2)}) %collective-permute-start) | collective-permute-done | bytes 589856 | tf_op jit(solution)/shard_map/ppermute | solution.py:351
  56.1 17.6 %shard_map.329 = (bf16[1536,512]{1,0:T(8,128)(2,1)}, bf16[1536,512]{1,0:T(8,128)(2,1)}, bf16[1536,512]{1,0:T(8,128)(2,1)}, f32[1,1536]{1,0:T(1,128)S(1)}, f32[38...) custom-call(s32[1]{0:T(128)} %bitcast.10.core_ref, ...), custom_call_target="tpu_custom_call" | custom-call | flops 10871635968 | bytes 20072452 | tf_op jit(solution)/shard_map/pallas_call | solution.py:314
  79.3 2.1 %constant_dynamic-slice_fusion.5 = bf16[2,2,2,1,96,512]{5,4,3,2,1,0:T(8,128)(2,1)} fusion(bf16[2,2,2,2,96,512]{5,4,3,2,1,0:T(8,128)(2,1)} %bitcast.131, s32[]{:T(128)S(6)} %select_n.121), kind=kLoop, calls=%fused_computation.46 | loop fusion | bytes 1572868 | tf_op jit(solution)/shard_map/dynamic_slice | solution.py:372
  81.9 2.1 %constant_dynamic-slice_fusion.8 = bf16[1,2,2,2,96,512]{5,4,3,2,1,0:T(8,128)(2,1)} fusion(bf16[2,2,2,2,96,512]{5,4,3,2,1,0:T(8,128)(2,1)} %bitcast.129, s32[]{:T(128)S(6)} %select_n.118), kind=kLoop, calls=%fused_computation.49 | loop fusion | bytes 1572868 | tf_op jit(solution)/shard_map/dynamic_slice | solution.py:372
  86.2 3.9 %shard_map.330 = (bf16[2,180,768]{2,1,0:T(8,128)(2,1)S(1)}, f32[2,180,768]{2,1,0:T(8,128)S(1)}, bf16[8,2,64,192]{3,2,1,0:T(8,128)(2,1)S(1)}, f32[1,768]{1,0:T(1,...) custom-call(s32[4]{0:T(128)S(1)} %reshape.356.box_ref, s32[1]{0:T(128)} %bitcast.row_ref, ...), custom_call_target="tpu_custom_call" | custom-call | flops 70778880 | bytes 7312820 | tf_op jit(solution)/shard_map/pallas_call | solution.py:314
  93.3 4.3 %all-to-all-start.2 = ((bf16[8,128,192]{1,2,0:T(8,128)(2,1)}), bf16[8,128,192]{1,2,0:T(8,128)(2,1)}, u32[]{:S(2)}, u32[]{:S(2)}) async-start(bf16[8,128,192]{1,2,0:T(8,128)(2,1)} %copy.57), calls=%async_computation.2 | async-start | bytes 786432 | tf_op jit(solution)/shard_map/all_to_all | solution.py:437
  106.9 2.5 %collective-permute-start.12 = (bf16[384,512]{1,0:T(8,128)(2,1)S(1)}, bf16[384,512]{1,0:T(8,128)(2,1)S(1)}, u32[]{:S(2)}, u32[]{:S(2)}) collective-permute-start(bf16[384,512]{1,0:T(8,128)(2,1)S(1)} %bitcast.139), channel_id=1, source_target_pairs={{0,1},{1,0},{2,3},{3,2},{4,5},{5,4},{6,7},{7,6},{8,9},{9,8},{10,11... | collective-permute-start | bytes 1179656 | tf_op jit(solution)/shard_map/ppermute | solution.py:351
  109.4 2.5 %collective-permute-done.20 = bf16[384,512]{1,0:T(8,128)(2,1)S(1)} collective-permute-done((bf16[384,512]{1,0:T(8,128)(2,1)S(1)}, bf16[384,512]{1,0:T(8,128)(2,1)S(1)}, u32[]{:S(2)}, u32[]{:S(2)}) %collective-permute-start.20) | collective-permute-done | bytes 393248 | tf_op jit(solution)/shard_map/ppermute | solution.py:351
  124.9 2.1 %shard_map.331 = (bf16[8,128,192]{2,1,0:T(8,128)(2,1)S(1)}, f32[2,2,96,96]{3,2,1,0:T(8,128)S(1)}, f32[2,192]{1,0:T(2,128)S(1)}) custom-call(bf16[8,128,192]{2,1,0:T(8,128)(2,1)S(1)} %copy.58.recv_ref, bf16[8,128,192]{2,1,0:T(8,128)(2,1)S(1)} %copy-done.10, bf16[8,128,192]{2,1,0:T(8,128)(2,1)S(1)} %copy-done.12, f32[8,128,192]{2,1,0:T(8,128)S(1)} %copy-done.5, ...), custom_call_target="tpu_custom_call" | custom-call | flops 301989888 | bytes 3646976 | tf_op jit(solution)/shard_map/pallas_call | solution.py:314
  129.1 2.1 %copy.59 = bf16[8,128,192]{1,2,0:T(8,128)(2,1)} copy(bf16[8,128,192]{2,1,0:T(8,128)(2,1)} %copy-done.8) | data formatting | bytes 786432 | tf_op jit(solution)/shard_map/pallas_call | solution.py:314
  131.2 4.3 %all-to-all-start.3 = ((bf16[8,128,192]{1,2,0:T(8,128)(2,1)}), bf16[8,128,192]{1,2,0:T(8,128)(2,1)S(1)}, u32[]{:S(2)}, u32[]{:S(2)}) async-start(bf16[8,128,192]{1,2,0:T(8,128)(2,1)} %copy.59), calls=%async_computation.3 | async-start | bytes 786432 | tf_op jit(solution)/shard_map/all_to_all | solution.py:439
  138.1 3.0 %collective-permute-start.22 = (bf16[96,512]{1,0:T(8,128)(2,1)S(1)}, bf16[96,512]{1,0:T(8,128)(2,1)S(1)}, u32[]{:S(2)}, u32[]{:S(2)}) collective-permute-start(bf16[96,512]{1,0:T(8,128)(2,1)S(1)} %dynamic-slice_bitcast_fusion), channel_id=1, source_target_pairs={{0,4},{1,5},{2,6},{3,7},{4,0},{5,1},{6,2},{7,3},{8,12},{9,13},{10,... | collective-permute-start | bytes 294920 | tf_op jit(solution)/shard_map/ppermute | solution.py:351
  146.7 6.0 %collective-permute-done.22 = bf16[96,512]{1,0:T(8,128)(2,1)S(1)} collective-permute-done((bf16[96,512]{1,0:T(8,128)(2,1)S(1)}, bf16[96,512]{1,0:T(8,128)(2,1)S(1)}, u32[]{:S(2)}, u32[]{:S(2)}) %collective-permute-start.22) | collective-permute-done | bytes 98336 | tf_op jit(solution)/shard_map/ppermute | solution.py:351
  162.1 3.5 %all-to-all-start.4 = ((bf16[8,384,96]{1,2,0:T(8,128)(2,1)}), bf16[8,384,96]{1,2,0:T(8,128)(2,1)S(1)}, u32[]{:S(2)}, u32[]{:S(2)}) async-start(bf16[8,384,96]{1,2,0:T(8,128)(2,1)} %broadcast_in_dim.7), calls=%async_computation.4 | async-start | bytes 1179648 | tf_op jit(solution)/shard_map/all_to_all | solution.py:615
  167.7 4.9 %collective-permute-done.6 = f32[78,128]{1,0:T(8,128)S(1)} collective-permute-done((f32[78,128]{1,0:T(8,128)S(1)}, f32[78,128]{1,0:T(8,128)S(1)}, u32[]{:S(2)}, u32[]{:S(2)}) %collective-permute-start.6) | collective-permute-done | bytes 39968 | tf_op jit(solution)/shard_map/ppermute | solution.py:351
  174.3 2.8 %collective-permute-done.7 = f32[78,128]{1,0:T(8,128)S(1)} collective-permute-done((f32[78,128]{1,0:T(8,128)S(1)}, f32[78,128]{1,0:T(8,128)S(1)}, u32[]{:S(2)}, u32[]{:S(2)}) %collective-permute-start.7) | collective-permute-done | bytes 39968 | tf_op jit(solution)/shard_map/ppermute | solution.py:351
  177.0 4.1 %collective-permute-start.8 = (f32[78,128]{1,0:T(8,128)S(1)}, f32[78,128]{1,0:T(8,128)S(1)}, u32[]{:S(2)}, u32[]{:S(2)}) collective-permute-start(f32[78,128]{1,0:T(8,128)S(1)} %add.148), channel_id=1, source_target_pairs={{0,4},{1,5},{2,6},{3,7},{4,0},{5,1},{6,2},{7,3},{8,12},{9,13},{10,... | collective-permute-start | bytes 119816 | tf_op jit(solution)/shard_map/ppermute | solution.py:351
  181.8 2.1 %copy.66 = f32[2,1,1,180,768]{4,2,3,1,0:T(1,128)} copy(f32[2,1,1,180,768]{4,3,0,2,1:T(8,128)S(1)} %bitcast.115) | data formatting | bytes 2211840
  190.1 2.1 %copy.67 = f32[2,8,96,96]{3,2,1,0:T(8,128)} copy(f32[2,8,96,96]{2,0,3,1:T(2,128)} %get-tuple-element.121) | data formatting | bytes 1179648
  (252 shorter events, 83.4 us)
Async XLA Ops:
  8.8 18.9 %all-to-all-start = ((bf16[8,128,192]{1,2,0:T(8,128)(2,1)}), bf16[8,128,192]{1,2,0:T(8,128)(2,1)S(1)}, u32[]{:S(2)}, u32[]{:S(2)}) async-start(bf16[8,128,192]{1,2,0:T(8,128)(2,1)} %copy.53), calls=%async_computation | async-start | bytes 786432 | tf_op jit(solution)/shard_map/all_to_all | solution.py:437
  34.6 15.3 %all-to-all-start.1 = ((bf16[8,128,192]{1,2,0:T(8,128)(2,1)}), bf16[8,128,192]{1,2,0:T(8,128)(2,1)S(1)}, u32[]{:S(2)}, u32[]{:S(2)}) async-start(bf16[8,128,192]{1,2,0:T(8,128)(2,1)} %copy.55), calls=%async_computation.1 | async-start | bytes 786432 | tf_op jit(solution)/shard_map/all_to_all | solution.py:439
  38.4 14.5 %collective-permute-start.1 = (bf16[384,768]{1,0:T(8,128)(2,1)}, bf16[384,768]{1,0:T(8,128)(2,1)}, u32[]{:S(2)}, u32[]{:S(2)}) collective-permute-start(bf16[384,768]{1,0:T(8,128)(2,1)} %bitcast.125), channel_id=1, source_target_pairs={{0,8},{8,0},{16,24},{24,16},{1,9},{9,1},{17,25},{25,17},{2,10},{10... | collective-permute-start | bytes 1769480 | tf_op jit(solution)/shard_map/ppermute | solution.py:351
  77.9 21.5 %collective-permute-start.19 = (bf16[768,512]{1,0:T(8,128)(2,1)}, bf16[768,512]{1,0:T(8,128)(2,1)}, u32[]{:S(2)}, u32[]{:S(2)}) collective-permute-start(bf16[768,512]{1,0:T(8,128)(2,1)} %bitcast.55), channel_id=1, source_target_pairs={{0,2},{1,3},{2,0},{3,1},{4,6},{5,7},{6,4},{7,5},{8,10},{9,11},{10,... | collective-permute-start | bytes 2359304 | tf_op jit(solution)/shard_map/ppermute | solution.py:351
  78.8 7.4 %collective-permute-start.2 = (bf16[384,768]{1,0:T(8,128)(2,1)}, bf16[384,768]{1,0:T(8,128)(2,1)}, u32[]{:S(2)}, u32[]{:S(2)}) collective-permute-start(bf16[384,768]{1,0:T(8,128)(2,1)} %get-tuple-element.49), channel_id=1, source_target_pairs={{0,8},{8,0},{16,24},{24,16},{1,9},{9,1},{17,25},{25,17},{2,10},{10... | collective-permute-start | bytes 1769480 | tf_op jit(solution)/shard_map/ppermute | solution.py:351
  78.8 7.4 %collective-permute-start.3 = (bf16[384,768]{1,0:T(8,128)(2,1)}, bf16[384,768]{1,0:T(8,128)(2,1)}, u32[]{:S(2)}, u32[]{:S(2)}) collective-permute-start(bf16[384,768]{1,0:T(8,128)(2,1)} %get-tuple-element.51), channel_id=1, source_target_pairs={{0,8},{8,0},{16,24},{24,16},{1,9},{9,1},{17,25},{25,17},{2,10},{10... | collective-permute-start | bytes 1769480 | tf_op jit(solution)/shard_map/ppermute | solution.py:351
  81.4 21.3 %collective-permute-start.15 = (bf16[768,512]{1,0:T(8,128)(2,1)}, bf16[768,512]{1,0:T(8,128)(2,1)}, u32[]{:S(2)}, u32[]{:S(2)}) collective-permute-start(bf16[768,512]{1,0:T(8,128)(2,1)} %bitcast.45), channel_id=1, source_target_pairs={{0,1},{1,0},{2,3},{3,2},{4,5},{5,4},{6,7},{7,6},{8,9},{9,8},{10,11... | collective-permute-start | bytes 2359304 | tf_op jit(solution)/shard_map/ppermute | solution.py:351
  84.0 21.5 %collective-permute-start.11 = (bf16[768,512]{1,0:T(8,128)(2,1)}, bf16[768,512]{1,0:T(8,128)(2,1)}, u32[]{:S(2)}, u32[]{:S(2)}) collective-permute-start(bf16[768,512]{1,0:T(8,128)(2,1)} %bitcast.35), channel_id=1, source_target_pairs={{0,16},{8,24},{16,0},{24,8},{1,17},{9,25},{17,1},{25,9},{2,18},{10... | collective-permute-start | bytes 2359304 | tf_op jit(solution)/shard_map/ppermute | solution.py:351
  93.3 27.4 %all-to-all-start.2 = ((bf16[8,128,192]{1,2,0:T(8,128)(2,1)}), bf16[8,128,192]{1,2,0:T(8,128)(2,1)}, u32[]{:S(2)}, u32[]{:S(2)}) async-start(bf16[8,128,192]{1,2,0:T(8,128)(2,1)} %copy.57), calls=%async_computation.2 | async-start | bytes 786432 | tf_op jit(solution)/shard_map/all_to_all | solution.py:437
  100.9 11.1 %collective-permute-start.20 = (bf16[384,512]{1,0:T(8,128)(2,1)S(1)}, bf16[384,512]{1,0:T(8,128)(2,1)S(1)}, u32[]{:S(2)}, u32[]{:S(2)}) collective-permute-start(bf16[384,512]{1,0:T(8,128)(2,1)S(1)} %bitcast.140), channel_id=1, source_target_pairs={{0,16},{8,24},{16,0},{24,8},{1,17},{9,25},{17,1},{25,9},{2,18},{10... | collective-permute-start | bytes 1179656 | tf_op jit(solution)/shard_map/ppermute | solution.py:351
  104.2 10.9 %collective-permute-start.16 = (bf16[384,512]{1,0:T(8,128)(2,1)S(1)}, bf16[384,512]{1,0:T(8,128)(2,1)S(1)}, u32[]{:S(2)}, u32[]{:S(2)}) collective-permute-start(bf16[384,512]{1,0:T(8,128)(2,1)S(1)} %bitcast.138), channel_id=1, source_target_pairs={{0,2},{1,3},{2,0},{3,1},{4,6},{5,7},{6,4},{7,5},{8,10},{9,11},{10,... | collective-permute-start | bytes 1179656 | tf_op jit(solution)/shard_map/ppermute | solution.py:351
  106.9 11.8 %collective-permute-start.12 = (bf16[384,512]{1,0:T(8,128)(2,1)S(1)}, bf16[384,512]{1,0:T(8,128)(2,1)S(1)}, u32[]{:S(2)}, u32[]{:S(2)}) collective-permute-start(bf16[384,512]{1,0:T(8,128)(2,1)S(1)} %bitcast.139), channel_id=1, source_target_pairs={{0,1},{1,0},{2,3},{3,2},{4,5},{5,4},{6,7},{7,6},{8,9},{9,8},{10,11... | collective-permute-start | bytes 1179656 | tf_op jit(solution)/shard_map/ppermute | solution.py:351
  112.8 24.3 %collective-permute-start.21 = (bf16[192,512]{1,0:T(8,128)(2,1)}, bf16[192,512]{1,0:T(8,128)(2,1)}, u32[]{:S(2)}, u32[]{:S(2)}) collective-permute-start(bf16[192,512]{1,0:T(8,128)(2,1)} %bitcast.59), channel_id=1, source_target_pairs={{0,1},{1,0},{2,3},{3,2},{4,5},{5,4},{6,7},{7,6},{8,9},{9,8},{10,11... | collective-permute-start | bytes 589832 | tf_op jit(solution)/shard_map/ppermute | solution.py:351
  116.0 25.1 %collective-permute-start.17 = (bf16[192,512]{1,0:T(8,128)(2,1)}, bf16[192,512]{1,0:T(8,128)(2,1)}, u32[]{:S(2)}, u32[]{:S(2)}) collective-permute-start(bf16[192,512]{1,0:T(8,128)(2,1)} %bitcast.49), channel_id=1, source_target_pairs={{0,4},{1,5},{2,6},{3,7},{4,0},{5,1},{6,2},{7,3},{8,12},{9,13},{10,... | collective-permute-start | bytes 589832 | tf_op jit(solution)/shard_map/ppermute | solution.py:351
  119.6 24.1 %collective-permute-start.13 = (bf16[192,512]{1,0:T(8,128)(2,1)}, bf16[192,512]{1,0:T(8,128)(2,1)}, u32[]{:S(2)}, u32[]{:S(2)}) collective-permute-start(bf16[192,512]{1,0:T(8,128)(2,1)} %bitcast.39), channel_id=1, source_target_pairs={{0,2},{1,3},{2,0},{3,1},{4,6},{5,7},{6,4},{7,5},{8,10},{9,11},{10,... | collective-permute-start | bytes 589832 | tf_op jit(solution)/shard_map/ppermute | solution.py:351
  131.2 23.0 %all-to-all-start.3 = ((bf16[8,128,192]{1,2,0:T(8,128)(2,1)}), bf16[8,128,192]{1,2,0:T(8,128)(2,1)S(1)}, u32[]{:S(2)}, u32[]{:S(2)}) async-start(bf16[8,128,192]{1,2,0:T(8,128)(2,1)} %copy.59), calls=%async_computation.3 | async-start | bytes 786432 | tf_op jit(solution)/shard_map/all_to_all | solution.py:439
  137.1 8.3 %collective-permute-start.9 = (f32[384,96]{1,0:T(8,128)S(1)}, f32[384,96]{1,0:T(8,128)S(1)}, u32[]{:S(2)}, u32[]{:S(2)}) collective-permute-start(f32[384,96]{1,0:T(8,128)S(1)} %bitcast.119), channel_id=1, source_target_pairs={{0,8},{8,0},{16,24},{24,16},{1,9},{9,1},{17,25},{25,17},{2,10},{10... | collective-permute-start | bytes 442376 | tf_op jit(solution)/shard_map/ppermute | solution.py:351
  138.1 14.6 %collective-permute-start.22 = (bf16[96,512]{1,0:T(8,128)(2,1)S(1)}, bf16[96,512]{1,0:T(8,128)(2,1)S(1)}, u32[]{:S(2)}, u32[]{:S(2)}) collective-permute-start(bf16[96,512]{1,0:T(8,128)(2,1)S(1)} %dynamic-slice_bitcast_fusion), channel_id=1, source_target_pairs={{0,4},{1,5},{2,6},{3,7},{4,0},{5,1},{6,2},{7,3},{8,12},{9,13},{10,... | collective-permute-start | bytes 294920 | tf_op jit(solution)/shard_map/ppermute | solution.py:351
  142.1 11.3 %collective-permute-start.18 = (bf16[96,512]{1,0:T(8,128)(2,1)S(1)}, bf16[96,512]{1,0:T(8,128)(2,1)S(1)}, u32[]{:S(2)}, u32[]{:S(2)}) collective-permute-start(bf16[96,512]{1,0:T(8,128)(2,1)S(1)} %dynamic-slice_bitcast_fusion.1), channel_id=1, source_target_pairs={{0,16},{8,24},{16,0},{24,8},{1,17},{9,25},{17,1},{25,9},{2,18},{10... | collective-permute-start | bytes 294920 | tf_op jit(solution)/shard_map/ppermute | solution.py:351
  145.4 12.8 %collective-permute-start.14 = (bf16[96,512]{1,0:T(8,128)(2,1)}, bf16[96,512]{1,0:T(8,128)(2,1)}, u32[]{:S(2)}, u32[]{:S(2)}) collective-permute-start(bf16[96,512]{1,0:T(8,128)(2,1)} %dynamic-slice_bitcast_fusion.2), channel_id=1, source_target_pairs={{0,4},{1,5},{2,6},{3,7},{4,0},{5,1},{6,2},{7,3},{8,12},{9,13},{10,... | collective-permute-start | bytes 294920 | tf_op jit(solution)/shard_map/ppermute | solution.py:351
  146.1 13.9 %collective-permute-start.10 = (f32[384,96]{1,0:T(8,128)}, f32[384,96]{1,0:T(8,128)}, u32[]{:S(2)}, u32[]{:S(2)}) collective-permute-start(f32[384,96]{1,0:T(8,128)} %bitcast_add_fusion), channel_id=1, source_target_pairs={{0,16},{8,24},{16,0},{24,8},{1,17},{9,25},{17,1},{25,9},{2,18},{10... | collective-permute-start | bytes 442376 | tf_op jit(solution)/shard_map/ppermute | solution.py:351
  162.1 24.5 %all-to-all-start.4 = ((bf16[8,384,96]{1,2,0:T(8,128)(2,1)}), bf16[8,384,96]{1,2,0:T(8,128)(2,1)S(1)}, u32[]{:S(2)}, u32[]{:S(2)}) async-start(bf16[8,384,96]{1,2,0:T(8,128)(2,1)} %broadcast_in_dim.7), calls=%async_computation.4 | async-start | bytes 1179648 | tf_op jit(solution)/shard_map/all_to_all | solution.py:615
  165.7 6.9 %collective-permute-start.6 = (f32[78,128]{1,0:T(8,128)S(1)}, f32[78,128]{1,0:T(8,128)S(1)}, u32[]{:S(2)}, u32[]{:S(2)}) collective-permute-start(f32[78,128]{1,0:T(8,128)S(1)} %fusion.20), channel_id=1, source_target_pairs={{0,1},{1,0},{2,3},{3,2},{4,5},{5,4},{6,7},{7,6},{8,9},{9,8},{10,11... | collective-permute-start | bytes 119816 | tf_op jit(solution)/shard_map/ppermute | solution.py:351
  177.0 6.9 %collective-permute-start.8 = (f32[78,128]{1,0:T(8,128)S(1)}, f32[78,128]{1,0:T(8,128)S(1)}, u32[]{:S(2)}, u32[]{:S(2)}) collective-permute-start(f32[78,128]{1,0:T(8,128)S(1)} %add.148), channel_id=1, source_target_pairs={{0,4},{1,5},{2,6},{3,7},{4,0},{5,1},{6,2},{7,3},{8,12},{9,13},{10,... | collective-permute-start | bytes 119816 | tf_op jit(solution)/shard_map/ppermute | solution.py:351
  (61 other events, 487.8 us)
where the time goes:
time: 195 us; the launch traced here: 193 us
  local copies, waits for them, and re-layouts  53.5 us (27%)
  starting transfers between devices  47.9 us (25%)
  waiting for transfers between devices  42.5 us (22%)
  Pallas kernels  31.9 us (16%)
  other arithmetic  16 us (8%)
    pallas_call x7, Pallas kernels, call(): pl.pallas_call(kernel, out_shape=out_shape, grid_spec=pltpu.PrefetchScala...  31.9 us
    ppermute x23, starting transfers between devices, pair_swap(): return lax.ppermute(operand, axis_name, [(i, i ^ bit) for i in range(size)])  24.7 us
    unnamed x126, local copies, waits for them, and re-layouts  22.2 us
    ppermute x23, waiting for transfers between devices, pair_swap(): return lax.ppermute(operand, axis_name, [(i, i ^ bit) for i in range(size)])  22 us
    all_to_all x2, waiting for transfers between devices, exchange(): lax.all_to_all(both.reshape(groups, lat_rows * points, wide), 'lat', 0, 0...  11.5 us
    all_to_all x2, starting transfers between devices, exchange(): both = lax.all_to_all(both, 'lat', 0, 0, tiled=True)  11.5 us
    all_to_all x2, waiting for transfers between devices, exchange(): both = lax.all_to_all(both, 'lat', 0, 0, tiled=True)  9.03 us
    dynamic_slice x9, local copies, waits for them, and re-layouts, halving_scatter(): away = lax.dynamic_slice_in_dim(part, 1 - own, 1, dim).astype(bf16)  8.58 us
  transfers between devices with their start and end apart: 28, of which 11 were waited for; matrix products, arithmetic and copies ran while one was open for 20% of the time, Pallas kernels for 6%

commit v1 on v0

v1 whole, which is shorter than its diff:
```python
import functools
import math

import jax
import jax.numpy as jnp
import ml_dtypes
import numpy as np
from jax import lax
from jax.experimental import pallas as pl
from jax.experimental.pallas import tpu as pltpu
from jax.sharding import PartitionSpec as P

MODES = 64
shrink_level = 0.01
epsilon = 1e-05
inv_root_two = 1.0 / math.sqrt(2.0)
inv_root_tau = 1.0 / math.sqrt(2.0 * math.pi)
f32 = jnp.float32
bf16 = jnp.bfloat16


def table_pair(out_count, in_count, length):
    phase = np.arange(out_count)[:, None] * np.arange(in_count)[None, :] % length
    angle = phase.astype(np.float32) * np.float32(2.0 * math.pi / length)
    return np.cos(angle).astype(np.float32), np.sin(angle).astype(np.float32)


def low(values):
    return values.astype(np.float32).astype(ml_dtypes.bfloat16)


def make_tables(lon_cells, lat_count, block_size, chunk):
    lon_factor = np.float32(1.0 / math.sqrt(lon_cells))
    cosine, sine = table_pair(MODES, lon_cells, lon_cells)
    weight = np.where(np.arange(MODES) == 0, 1.0, 2.0).astype(np.float32)[:, None]
    forward = low(np.concatenate([cosine, -sine]) * lon_factor)
    inverse = low(np.concatenate([cosine * weight, -sine * weight]) * lon_factor)
    cosine, sine = table_pair(lat_count, lat_count, lat_count)
    lat_factor = np.float32(1.0 / math.sqrt(lat_count))
    same = np.eye(chunk, dtype=np.float32)
    cosine = np.kron(low(cosine * lat_factor).astype(np.float32), same)
    sine = np.kron(low(sine * lat_factor).astype(np.float32), same)
    turn_fwd = low(np.concatenate([cosine, sine], axis=1))
    turn_inv = low(np.concatenate([cosine, -sine], axis=1))
    eye, none = np.eye(block_size), np.zeros((block_size, block_size))
    swap = low(np.block([[none, -eye], [eye, none]]))
    return dict(
        fwd=forward, fwd_t=forward.T.copy(), inv=inverse, inv_t=inverse.T.copy(),
        turn_fwd=turn_fwd, turn_inv=turn_inv, swap=swap,
    )


def dot(a, b, ca, cb):
    return lax.dot_general(a, b, (((ca,), (cb,)), ((), ())), preferred_element_type=f32)


def line(ref):
    return ref[...].reshape(1, -1)


def row_mean(values):
    return jnp.sum(values, axis=-1, keepdims=True) * (1.0 / values.shape[-1])


def norm_parts(values):
    centered = values - row_mean(values)
    inv_scale = lax.rsqrt(row_mean(centered * centered) + epsilon)
    return centered * inv_scale, inv_scale


def norm_back(grad_normed, unit_values, inv_scale, gain):
    grad_unit = grad_normed * gain
    plain, cross = row_mean(grad_unit), row_mean(grad_unit * unit_values)
    return inv_scale * (grad_unit - plain - unit_values * cross)


def gelu_pair(values):
    half = 0.5 * (1.0 + lax.erf(values * inv_root_two))
    return values * half, half + values * jnp.exp(-0.5 * values * values) * inv_root_tau


def shrink_pair(values):
    inverse = lax.rsqrt(values * values + shrink_level * shrink_level)
    slope = 1.0 - shrink_level * shrink_level * shrink_level * inverse * inverse * inverse
    return values - shrink_level * values * inverse, slope


def valid_row(item, box_ref, row_ref, hole_ref, lat_rows, cells):
    crop, row = item // lat_rows, row_ref[0] + item % lat_rows
    crop_count = box_ref.shape[1]
    micro, crop = crop // crop_count, crop % crop_count
    limit = jnp.where(row < box_ref[micro, crop, 0], box_ref[micro, crop, 1], 0)
    column = lax.broadcasted_iota(jnp.int32, (1, cells), 1)
    return jnp.where((column < limit) & (hole_ref[item] > 0), 1.0, 0.0)


def as_column(row):
    cells = row.shape[1]
    down = lax.broadcasted_iota(jnp.int32, (cells, cells), 0)
    along = lax.broadcasted_iota(jnp.int32, (cells, cells), 1)
    return jnp.sum(jnp.where(down == along, row, 0.0), axis=1, keepdims=True)


def pack(both):
    half = both.shape[0] // 2
    rest = both[:, 128:]
    return both[:, :128], jnp.concatenate([rest[:half], rest[half:]], axis=1)


def unpack(packed):
    points = packed.shape[0] * 2 // 3
    rest = packed[points:]
    rest = jnp.concatenate([rest[:, :64], rest[:, 64:]], axis=0)
    return jnp.concatenate([packed[:points], rest], axis=1)


def put_modes(send_ref, item, spectrum, block_size, sub):
    spectrum = spectrum.astype(bf16)
    own = MODES // sub
    for block in range(spectrum.shape[1] // block_size):
        cut = spectrum[:, block * block_size : (block + 1) * block_size]
        both = jnp.concatenate([cut[:MODES], cut[MODES:]], axis=1)
        for j in range(sub):
            top, rest = pack(both[j * own : (j + 1) * own])
            send_ref[block * sub + j, item, :own] = top
            send_ref[block * sub + j, item, own:] = rest


def get_modes(recv_ref, item, block_size, sub):
    groups = recv_ref.shape[0]
    real, imag = [], []
    for block in range(groups // sub):
        parts = [unpack(recv_ref[block * sub + j, item]) for j in range(sub)]
        both = parts[0] if sub == 1 else jnp.concatenate(parts, axis=0)
        real.append(both[:, :block_size])
        imag.append(both[:, block_size:])
    real, imag = jnp.concatenate(real, axis=1), jnp.concatenate(imag, axis=1)
    return jnp.concatenate([real, imag], axis=0)


def unpack_all(recv_ref, points_ref):
    lat_count, crops, packed, _ = recv_ref.shape
    own = packed * 2 // 3
    for p in range(lat_count):
        for crop in range(crops):
            points_ref[p, crop * own : (crop + 1) * own] = unpack(recv_ref[p, crop])


def pack_all(points_ref, send_ref):
    lat_count, crops, packed, _ = send_ref.shape
    own = packed * 2 // 3
    for p in range(lat_count):
        for crop in range(crops):
            top, rest = pack(points_ref[p, crop * own : (crop + 1) * own])
            send_ref[p, crop, :own] = top
            send_ref[p, crop, own:] = rest


def turn_rows(src_ref, dst_ref, table, swap, chunk):
    lat_count, points, wide = src_ref.shape
    for at in range(0, points, chunk):
        piece = src_ref[:, at : at + chunk, :].reshape(lat_count * chunk, wide)
        other = dot(piece, swap, 1, 0).astype(bf16)
        out = dot(table, jnp.concatenate([piece, other], axis=0), 1, 0)
        dst_ref[:, at : at + chunk, :] = out.astype(bf16).reshape(lat_count, chunk, wide)


def pre_kernel(
    lat_rows, block_size, sub,
    box_ref, row_ref, token_ref, hole_ref, gain_ref, shift_ref, table_ref,
    send_ref,
):
    items, cells, _ = token_ref.shape
    units = [norm_parts(token_ref[item].astype(f32))[0] for item in range(items)]
    for item in range(items):
        valid = valid_row(item, box_ref, row_ref, hole_ref, lat_rows, cells)
        normed = (units[item] * line(gain_ref) + line(shift_ref)).astype(bf16)
        table = (table_ref[...].astype(f32) * valid).astype(bf16)
        put_modes(send_ref, item, dot(table, normed, 1, 0), block_size, sub)


def filter_kernel(
    chunk,
    recv_ref, inner_ref, inner_bias_ref, outer_ref, outer_bias_ref, turn_fwd_ref, turn_inv_ref, swap_ref,
    send_ref, spec, hid_out, slope_out, shrunk_out,
    hid_ref, slope_ref, shrunk_ref, filt_ref, points_ref, sems,
):
    unpack_all(recv_ref, points_ref)
    spec_ref = spec.here
    turn_rows(points_ref, spec_ref, turn_fwd_ref[...], swap_ref[...], chunk)
    spec.start()
    copies = []
    for p in range(spec_ref.shape[0]):
        pre = dot(spec_ref[p], inner_ref[...], 1, 0) + inner_bias_ref[...]
        hid, slope = gelu_pair(pre)
        hid = hid.astype(bf16)
        hid_ref[p] = hid
        slope_ref[p] = slope
        mid = dot(hid, outer_ref[...], 1, 0) + outer_bias_ref[...]
        filt, shrunk = shrink_pair(mid)
        filt_ref[p] = filt.astype(bf16)
        shrunk_ref[p] = shrunk
        for at, (kept, out) in enumerate(((hid_ref, hid_out), (slope_ref, slope_out), (shrunk_ref, shrunk_out))):
            copies.append(pltpu.make_async_copy(kept.at[p], out.at[p], sems.at[p, at]))
            copies[-1].start()
    turn_rows(filt_ref, points_ref, turn_inv_ref[...], swap_ref[...], chunk)
    pack_all(points_ref, send_ref)
    for copy in copies:
        copy.wait()


def mix_kernel(
    lat_rows, block_size, sub,
    box_ref, row_ref, recv_ref, token_ref, hole_ref, gain_ref, shift_ref,
    post_gain_ref, post_shift_ref, table_ref,
    mixed, post_ref,
):
    items, cells, width = token_ref.shape
    pad = post_ref.shape[1] - cells
    backs = [get_modes(recv_ref, item, block_size, sub) for item in range(items)]
    units = [norm_parts(token_ref[item].astype(f32))[0] for item in range(items)]
    for item in range(items):
        valid = as_column(valid_row(item, box_ref, row_ref, hole_ref, lat_rows, cells))
        normed = units[item] * line(gain_ref) + line(shift_ref)
        filtered = dot(table_ref[...], backs[item], 1, 0)
        value = token_ref[item].astype(f32) + normed + valid * filtered
        mixed[item] = value
        unit, _ = norm_parts(value)
        post_ref[item, :cells] = (unit * line(post_gain_ref) + line(post_shift_ref)).astype(bf16)
        if pad:
            post_ref[item, cells:] = jnp.zeros((pad, width), bf16)


def feed_kernel(
    cuts, runs, run,
    bit_ref, core_ref, post_own, post_other, cot_own, cot_other, expand_far, reduce_far, bias_ref,
    *refs,
):
    far_refs, refs = refs[:6], refs[6:]
    bias_grad, out_own, grad_own_ref, out_other_ref, grad_0_ref, grad_1_ref, *refs = refs
    post_ref, cot_ref, expand_ref, reduce_ref, hidden_ref, grad_ref, *refs = refs
    expand_grad_ref, reduce_grad_ref, row_sems, weight_sems, far_sems = refs
    rows = post_own.shape[0]
    arrivals = []
    for at, (source, to) in enumerate(((post_own, post_ref), (post_other, post_ref), (cot_own, cot_ref), (cot_other, cot_ref))):
        here = slice(at % 2 * rows, (at % 2 + 1) * rows)
        arrivals.append(pltpu.make_async_copy(source, to.at[here], row_sems.at[at]))
    fetches = []
    for r in range(runs):
        start = pl.multiple_of((2 * r + core_ref[0]) * run, 128)
        here, there = slice(r * run, (r + 1) * run), pl.ds(start, run)
        fetches.append(pltpu.make_async_copy(expand_far.at[:, there], expand_ref.at[:, here], weight_sems.at[0, r]))
        fetches.append(pltpu.make_async_copy(reduce_far.at[there], reduce_ref.at[here], weight_sems.at[1, r]))
    waves = [arrivals[:2] + fetches[:1], arrivals[2:] + fetches[1:2]] + [fetches[2 * r : 2 * r + 2] for r in range(1, runs)]

    def turn_over(at):
        for copy in waves[at]:
            copy.wait()
        for copy in waves[at + 1] if at + 1 < len(waves) else ():
            copy.start()

    for copy in waves[0]:
        copy.start()
    turn_over(0)
    post = post_ref[...]
    for r in range(runs):
        here = slice(r * run, (r + 1) * run)
        if r:
            turn_over(r + 1)
        start = pl.multiple_of((2 * r + core_ref[0]) * run, 128)
        pre = dot(post, expand_ref[:, here], 1, 0) + bias_ref[:, pl.ds(start, run)]
        hidden, slope = gelu_pair(pre)
        hidden_ref[:, here] = hidden.astype(bf16)
        if not r:
            turn_over(1)
        cot = cot_ref[...]
        grad = (dot(cot, reduce_ref[here], 1, 1) * slope).astype(bf16)
        grad_ref[:, here] = grad
        bias_grad.here[:, here] = jnp.sum(grad.astype(f32), axis=0, keepdims=True)
    bias_grad.start()

    for r in range(runs):
        here = slice(r * run, (r + 1) * run)
        expand_grad_ref[here] = dot(grad_ref[:, here], post, 0, 0).astype(bf16)
        reduce_grad_ref[here] = dot(hidden_ref[:, here], cot, 0, 0).astype(bf16)
    lanes = post.shape[1] // 3
    copies = []
    for group, (at, outer) in enumerate(cuts):
        inner = runs * run // (2 * outer)
        own = bit_ref[at]
        for side, source in enumerate((expand_grad_ref, reduce_grad_ref)):
            for o in range(outer):
                for target, half in enumerate((1 - own, own)):
                    start = pl.multiple_of((2 * o + half) * inner, 16)
                    part = source.at[pl.ds(start, inner), group * lanes : (group + 1) * lanes]
                    to = far_refs[2 * group + target].at[
                        o * inner : (o + 1) * inner, side * lanes : (side + 1) * lanes
                    ]
                    copies.append(pltpu.make_async_copy(part, to, far_sems.at[len(copies)]))
                    copies[-1].start()

    out = dot(hidden_ref[...], reduce_ref[...], 1, 0)
    out_own.here[...] = out[:rows]
    out_own.start()
    out_other_ref[...] = out[rows:].astype(bf16)
    back = dot(grad_ref[...], expand_ref[...], 1, 1)
    half = back.shape[1] // 2
    grad_own_ref[...] = back[:rows]
    grad_0_ref[...] = back[rows:, :half].astype(bf16)
    grad_1_ref[...] = back[rows:, half:].astype(bf16)
    for copy in copies:
        copy.wait()


def combine_kernel(places, bit_ref, *refs):
    groups = len(places)
    ins, outs = refs[: 2 * groups], refs[2 * groups :]
    for at, place in enumerate(places):
        keep, recv = ins[2 * at], ins[2 * at + 1]
        low_own = bit_ref[place] == 0
        first, second = keep[:, 0] + recv[:, 0], keep[:, 1] + recv[:, 1]
        outs[2 * at].here[...] = jnp.where(low_own, second, first)
        outs[2 * at].start()
        outs[2 * at + 1].here[...] = jnp.where(low_own, first, second)
        outs[2 * at + 1].start()


def shard_kernel(*refs):
    *ins, expand_ref, reduce_ref = refs
    lanes = ins[0].here.shape[1] // 2
    for at in range(len(ins) // 2):
        total = ins[2 * at][...].astype(f32) + ins[2 * at + 1][...].astype(f32)
        expand_ref[:, at * lanes : (at + 1) * lanes] = total[:, :lanes]
        reduce_ref[:, at * lanes : (at + 1) * lanes] = total[:, lanes:]


def both_halves(first_ref, second_ref, item, cells):
    return jnp.concatenate([first_ref[item, :cells], second_ref[item, :cells]], axis=1).astype(f32)


def result_kernel(mixed_ref, out_own_ref, out_other_ref, bias_ref, result_ref):
    items, cells, _ = result_ref.shape
    for item in range(items):
        out = out_own_ref[item, :cells] + out_other_ref[item, :cells].astype(f32)
        result_ref[item] = (mixed_ref[item] + (out + line(bias_ref))).astype(bf16)


def post_kernel(
    lat_rows, block_size, sub,
    box_ref, row_ref, mixed_ref, grad_own_ref, grad_0_ref, grad_1_ref, cot_ref, hole_ref, gain_ref, table_ref,
    grad_mixed, send_ref, sum_ref,
):
    items, cells, _ = grad_mixed.shape
    sums = 0.0
    for item in range(items):
        valid = valid_row(item, box_ref, row_ref, hole_ref, lat_rows, cells)
        grad = grad_own_ref[item, :cells] + both_halves(grad_0_ref, grad_1_ref, item, cells)
        unit, inv_scale = norm_parts(mixed_ref[item])
        cot = cot_ref[item, :cells].astype(f32)
        sums += jnp.concatenate([jnp.sum(v, axis=0, keepdims=True) for v in (grad * unit, grad, cot)], axis=0)
        value = cot + norm_back(grad, unit, inv_scale, line(gain_ref))
        grad_mixed[item] = value
        table = (table_ref[...].astype(f32) * valid).astype(bf16)
        put_modes(send_ref, item, dot(table, value.astype(bf16), 1, 0), block_size, sub)
    sum_ref[...] = sums


def small_kernel(layout, core_ref, post_sum_ref, expand_bias_ref, small_ref):
    per_run, runs, _ = layout
    small_ref[...] = jnp.zeros_like(small_ref)
    per_line = post_sum_ref.shape[1] // 128
    for line_at in range(3):
        for at in range(per_line):
            row = line_at * per_line + at
            small_ref[row : row + 1] = post_sum_ref[line_at : line_at + 1, at * 128 : (at + 1) * 128]
    for at in range(runs * per_run):
        row = (at // per_run * 2 + core_ref[0]) * per_run + at % per_run
        small_ref[pl.ds(3 * per_line + row, 1)] = expand_bias_ref[:, at * 128 : (at + 1) * 128]


def filter_back_kernel(
    chunk, bias_row, blocks, place_ref,
    recv_ref, spec_ref, hid_ref, slope_ref, shrunk_ref, inner_ref, outer_ref,
    turn_fwd_ref, turn_inv_ref, swap_ref, small_ref,
    send_ref, weight_send_ref, weight_keep_ref,
    turned_ref, grad_mid_ref, grad_pre_ref, points_ref,
):
    lat_count, points, wide = turned_ref.shape
    unpack_all(recv_ref, grad_mid_ref)
    turn_rows(grad_mid_ref, turned_ref, turn_fwd_ref[...], swap_ref[...], chunk)
    inner_bias = jnp.zeros((1, wide), f32)
    outer_bias = jnp.zeros((1, wide), f32)
    for p in range(lat_count):
        grad_mid = (turned_ref[p].astype(f32) * shrunk_ref[p]).astype(bf16)
        grad_mid_ref[p] = grad_mid
        outer_bias += jnp.sum(grad_mid.astype(f32), axis=0, keepdims=True)
        grad_pre = (dot(grad_mid, outer_ref[...], 1, 1) * slope_ref[p]).astype(bf16)
        grad_pre_ref[p] = grad_pre
        inner_bias += jnp.sum(grad_pre.astype(f32), axis=0, keepdims=True)
        turned_ref[p] = dot(grad_pre, inner_ref[...], 1, 1).astype(bf16)
    turn_rows(turned_ref, points_ref, turn_inv_ref[...], swap_ref[...], chunk)
    pack_all(points_ref, send_ref)
    flat = (lat_count * points, wide)
    half = wide // 2
    base = weight_keep_ref.shape[0] - small_ref.shape[0]
    own = place_ref[0]
    for at, (left, right) in enumerate(((spec_ref, grad_pre_ref), (hid_ref, grad_mid_ref))):
        grad = dot(left[...].reshape(flat), right[...].reshape(flat), 0, 0)
        first = grad[:half, :half] + grad[half:, half:]
        second = grad[:half, half:] - grad[half:, :half]
        top, rest = pack(jnp.concatenate([first, second], axis=1))

        @pl.when(own == at)
        def _():
            weight_keep_ref[:half] = top
            weight_keep_ref[half:base] = rest

        @pl.when(own != at)
        def _():
            weight_send_ref[:half] = top
            weight_send_ref[half:base] = rest

    weight_keep_ref[base:] = small_ref[...]
    for at, bias in enumerate((inner_bias, outer_bias)):
        for side in range(2):
            row = bias_row + (2 * at + side) * blocks + place_ref[1]
            weight_keep_ref[pl.ds(base + row, 1), :half] = bias[:, side * half : (side + 1) * half]
    weight_send_ref[base:] = weight_keep_ref[base:]


def last_kernel(
    lat_rows, block_size, sub,
    box_ref, row_ref, recv_ref, token_ref, grad_mixed_ref, hole_ref, gain_ref, table_ref,
    result_ref, tail,
):
    items, cells, width = token_ref.shape
    backs = [get_modes(recv_ref, item, block_size, sub) for item in range(items)]
    parts = [norm_parts(token_ref[item].astype(f32)) for item in range(items)]
    sums = 0.0
    grads = []
    for item in range(items):
        valid = as_column(valid_row(item, box_ref, row_ref, hole_ref, lat_rows, cells))
        grad = grad_mixed_ref[item] + valid * dot(table_ref[...], backs[item], 1, 0)
        grads.append(grad)
        sums += jnp.concatenate([jnp.sum(v, axis=0, keepdims=True) for v in (grad * parts[item][0], grad)], axis=0)

    per_line = width // 128
    pieces = [sums[i : i + 1, j * 128 : (j + 1) * 128] for i in range(2) for j in range(per_line)]
    pad = tail.shape[1] - 2 * per_line
    if pad:
        pieces.append(jnp.zeros((pad, 128), f32))
    value = jnp.concatenate(pieces, axis=0).astype(bf16)
    for device in range(tail.shape[0]):
        tail.here[device] = value
    tail.start()
    for item in range(items):
        unit, inv_scale = parts[item]
        result_ref[item] = grad_mixed_ref[item] + norm_back(grads[item], unit, inv_scale, line(gain_ref))


def put_split(ref, at, value):
    high = value.astype(bf16)
    rows = value.shape[0]
    ref[at : at + rows] = high
    ref[at + rows : at + 2 * rows] = (value - high.astype(f32)).astype(bf16)


def get_split(ref, rows):
    at = ref.shape[0] - 2 * rows
    return ref[at : at + rows].astype(f32) + ref[at + rows :].astype(f32)


def first_kernel(own_ref, recv_ref, send_ref, small_ref):
    rows = small_ref.shape[0]
    base = own_ref.shape[0] - rows
    send_ref[:base] = (own_ref[:base] + recv_ref[:base]).astype(bf16)
    total = own_ref[base:] + recv_ref[base:]
    small_ref[...] = total
    put_split(send_ref, base, total)


def second_kernel(own_ref, recv_ref, small_in_ref, send_ref, small_ref):
    rows = small_ref.shape[0]
    base = own_ref.shape[0] - 2 * rows
    send_ref[:base] = own_ref[:base]
    send_ref[base : 2 * base] = recv_ref[:base]
    total = small_in_ref[...] + get_split(recv_ref, rows)
    small_ref[...] = total
    put_split(send_ref, 2 * base, total)


def third_kernel(*refs):
    *parts, small_in_ref, weight_ref, small_ref = refs
    rows = small_ref.shape[0]
    both = parts[0].shape[0] - 2 * rows
    total = small_in_ref[...]
    for at, ref in enumerate(parts):
        weight_ref[at * both : (at + 1) * both] = ref[:both]
        if at:
            total += get_split(ref, rows)
    small_ref[...] = total


def tail_kernel(
    place_ref, tail_ref, small_ref, weight_ref, weight_other_ref,
    pre_gain_ref, pre_shift_ref, inner_ref, inner_bias_ref, outer_ref, outer_bias_ref,
    post_gain_ref, post_shift_ref, expand_bias_ref, reduce_bias_ref,
):
    per_line = pre_gain_ref.shape[0] // 128
    sums = jnp.sum(tail_ref[:, : 2 * per_line].astype(f32), axis=0)

    def put(ref, at, value):
        ref[pl.ds(at * 128, 128)] = value.reshape(128)

    for i, ref in enumerate((pre_gain_ref, pre_shift_ref)):
        for j in range(per_line):
            put(ref, j, sums[i * per_line + j : i * per_line + j + 1])

    def row(at):
        return small_ref[at : at + 1]

    at = 0
    for ref in (post_gain_ref, post_shift_ref, reduce_bias_ref, expand_bias_ref):
        for j in range(ref.shape[0] // 128):
            put(ref, j, row(at))
            at += 1
    _, blocks, size = inner_bias_ref.shape
    for ref in (inner_bias_ref, outer_bias_ref):
        for side in range(2):
            for block in range(blocks):
                ref[side, block : block + 1] = row(at)[:, :size]
                at += 1
    own = place_ref[0]
    for at in range(blocks):
        mine = unpack(weight_ref[at].astype(f32))
        theirs = unpack(weight_other_ref[at].astype(f32))
        inner, outer = jnp.where(own == 0, mine, theirs), jnp.where(own == 0, theirs, mine)
        block = at ^ place_ref[1]
        for side in range(2):
            inner_ref[side, block] = inner[:, side * size : (side + 1) * size]
            outer_ref[side, block] = outer[:, side * size : (side + 1) * size]


class Far:
    def __init__(self, far_ref, here_ref, sem, incoming):
        pair = (far_ref, here_ref) if incoming else (here_ref, far_ref)
        self.here, self.copy, self.pending = here_ref, pltpu.make_async_copy(*pair, sem), False
        if incoming:
            self.start()

    def start(self):
        self.copy.start()
        self.pending = True

    def wait(self):
        if self.pending:
            self.copy.wait()
            self.pending = False

    @property
    def shape(self):
        return self.here.shape

    def __getitem__(self, index):
        self.wait()
        return self.here[index]


def call(kernel, out_shape, args, prefetch=0, scratch=(), flops=0, vmem=16, after=(), far_in=(), far_out=(), raw=()):
    args, after = tuple(args), tuple(after)
    far_out = [len(args) + i for i in far_out]
    raw = set(i if i >= 0 else len(args) - 1 - i for i in raw)
    far = list(far_in) + far_out
    count = len(args) + len(out_shape)
    every = list(args) + list(out_shape)
    anywhere = pl.BlockSpec(memory_space=pl.ANY)

    def spec(i):
        if i in far or i in raw:
            return anywhere
        dims = every[i].shape
        rest = (0,) * len(dims)
        return pl.BlockSpec(tuple(dims), lambda *_: rest)

    def whole_kernel(*refs):
        refs = list(refs[: len(args)]) + list(refs[len(args) + len(after) :])
        sems = refs.pop() if far else None
        buffers = [refs.pop() for _ in far][::-1]
        fars = {}
        for at, i in enumerate(far):
            fars[i] = refs[i] = Far(refs[i], buffers[at], sems.at[at], i < len(args))
        kernel(*refs)
        for value in fars.values():
            value.wait()

    moved = sum(math.prod(a.shape) * np.dtype(a.dtype).itemsize for a in every)
    fixed = [pltpu.with_memory_space_constraint(a, pltpu.HBM) if i in far else a for i, a in enumerate(args)]
    shapes = [
        pltpu.HBM(a.shape, a.dtype) if i in far_out or i in raw else a for i, a in enumerate(out_shape, len(args))
    ]
    scratch = list(scratch) + [pltpu.VMEM(every[i].shape, every[i].dtype) for i in far]
    if far:
        scratch.append(pltpu.SemaphoreType.DMA((len(far),)))
    return pl.pallas_call(
        whole_kernel,
        out_shape=shapes,
        grid_spec=pltpu.PrefetchScalarGridSpec(
            num_scalar_prefetch=prefetch,
            grid=(1,),
            in_specs=[spec(i) for i in range(prefetch, len(args))] + [anywhere] * len(after),
            out_specs=[spec(i) for i in range(len(args), count)],
            scratch_shapes=scratch,
        ),
        compiler_params=pltpu.CompilerParams(
            dimension_semantics=("arbitrary",), vmem_limit_bytes=vmem << 20
        ),
        cost_estimate=pl.CostEstimate(flops=int(flops), bytes_accessed=int(moved), transcendentals=0),
    )(*fixed, *after)


def shape(dims, dtype):
    return jax.ShapeDtypeStruct(tuple(dims), dtype)


def stay(operand):
    return pltpu.with_memory_space_constraint(operand, pltpu.HBM)


def pair_swap(operand, axis_name, bit):
    size = lax.axis_size(axis_name)
    return lax.ppermute(operand, axis_name, [(i, i ^ bit) for i in range(size)])


def axis_bits(axis_name):
    size = lax.axis_size(axis_name)
    return [1 << i for i in range(size.bit_length() - 1)]


def body(
    tokens,
    boxes,
    patch_mask,
    pre_gain,
    pre_shift,
    filter_inner,
    filter_inner_bias,
    filter_outer,
    filter_outer_bias,
    post_gain,
    post_shift,
    expand_weight,
    expand_bias,
    reduce_weight,
    reduce_bias,
    cotangent,
):
    micro_count, crop_count, lat_rows, cells, width = tokens.shape
    groups = lax.axis_size("lat")
    lat_count = lat_rows * groups
    block_count, block_size = filter_inner.shape[1:3]
    sub = groups // block_count
    modes_own = MODES // sub
    crops = micro_count * crop_count
    items = crops * lat_rows
    points = crops * modes_own
    wide = 2 * block_size
    padded = -(-cells // 16) * 16
    rows = items * padded
    chunk = 16
    hidden_width = expand_weight.shape[1]
    dp_size = lax.axis_size("dp")
    lat_index, dp_index = lax.axis_index("lat"), lax.axis_index("dp")
    own_block = lat_index // sub
    tables = {k: jnp.asarray(v) for k, v in make_tables(cells, lat_count, block_size, chunk).items()}

    box = boxes
    own_row = (lat_index * lat_rows).astype(jnp.int32).reshape(1)
    core = dp_index % 2
    token_items = tokens.reshape(items, cells, width)
    cot_pad = jnp.pad(cotangent.reshape(items, cells, width), ((0, 0), (0, padded - cells), (0, 0)))
    holes = patch_mask.reshape(items, 1, cells)
    row_item = (items, cells, width)
    pad_item = (items, padded, width)
    packed = modes_own * 3 // 2
    mode_dims = (groups, items, packed, 128)
    names = (lat_rows, block_size, sub)
    lon_flops = 2 * items * 2 * MODES * cells * width

    def exchange(both, by_rows):
        if by_rows:
            both = both.reshape(groups, crops, lat_rows, packed, 128).swapaxes(1, 2)
            both = both.reshape(groups, items * packed, 128)
            both = lax.all_to_all(both, "lat", 0, 0, tiled=True)
            return both.reshape(lat_count, crops, packed, 128)
        both = both.reshape(groups, items * packed, 128)
        both = lax.all_to_all(both, "lat", 0, 0, tiled=True)
        both = both.reshape(groups, lat_rows, crops, packed, 128).swapaxes(1, 2)
        return both.reshape(mode_dims)

    def own_matrix(matrix):
        pair = lax.dynamic_index_in_dim(matrix, own_block, 1, keepdims=False)
        top = jnp.concatenate([pair[0], pair[1]], axis=1)
        under = jnp.concatenate([-pair[1], pair[0]], axis=1)
        return jnp.concatenate([top, under], axis=0)

    def own_bias(bias):
        return lax.dynamic_index_in_dim(bias, own_block, 1, keepdims=False).reshape(1, wide)

    args = (box, own_row, token_items, holes, pre_gain, pre_shift, tables["fwd"])
    (send,) = call(
        functools.partial(pre_kernel, *names),
        [shape(mode_dims, bf16)],
        args,
        prefetch=2,
        far_in=range(3, 7),
        flops=lon_flops,
    )
    recv = exchange(send, True)
    cot_other = pair_swap(cot_pad.reshape(rows, width), "dp", 1)

    spectrum = (lat_count, points, wide)
    grid_dims = (lat_count, crops, packed, 128)
    filter_flops = 4 * lat_count * points * wide * wide
    inner, outer = own_matrix(filter_inner), own_matrix(filter_outer)
    turns = (tables["turn_fwd"], tables["turn_inv"], tables["swap"])
    args = (recv, inner, own_bias(filter_inner_bias), outer, own_bias(filter_outer_bias), *turns)
    send, spec, hid, slope, shrunk = call(
        functools.partial(filter_kernel, chunk),
        [shape(grid_dims, bf16)] + [shape(spectrum, t) for t in (bf16, bf16, f32, f32)],
        args,
        far_in=(5, 6, 7),
        far_out=(1,),
        raw=(-3, -4, -5),
        scratch=[pltpu.VMEM(spectrum, t) for t in (bf16, f32, f32, bf16, bf16)]
        + [pltpu.SemaphoreType.DMA((lat_count, 3))],
        flops=filter_flops,
    )
    recv = exchange(send, False)

    args = (
        box, own_row, recv, token_items, holes, pre_gain, pre_shift, post_gain, post_shift, tables["inv_t"],
    )
    mixed, post = call(
        functools.partial(mix_kernel, *names),
        [shape(row_item, f32), shape(pad_item, bf16)],
        args,
        prefetch=2,
        far_in=range(4, 10),
        flops=lon_flops,
    )
    post = post.reshape(rows, width)
    post_other = pair_swap(post, "dp", 1)

    dp_bits = [("dp", b) for b in axis_bits("dp")[1:]]
    lat_bits = [("lat", b) for b in axis_bits("lat")]
    bit_names = dp_bits[::-1] + lat_bits[::-1]
    own_bits = jnp.stack([(lax.axis_index(n) // b) % 2 for n, b in bit_names]).astype(jnp.int32)
    own_rows = hidden_width // (dp_size * groups)
    half = hidden_width // 2
    run = hidden_width // dp_size
    runs = dp_size // 2
    core_bit = core.astype(jnp.int32).reshape(1)

    whole_rows = [n for n in lat_bits if own_rows * n[1] % 16 == 0]
    orders = [
        dp_bits + lat_bits,
        whole_rows[:1] + [n for n in lat_bits[:-1] if n != whole_rows[0]] + dp_bits + lat_bits[-1:],
        whole_rows[1:2] + dp_bits + [n for n in lat_bits if n != whole_rows[1]],
    ]
    lefts = [list(bit_names) for _ in orders]

    def place_of(step, left):
        return bit_names.index(step), 2 ** left.index(step)

    lanes = 2 * width // 3
    flat, double = (rows, width), (2 * rows, width)
    cuts = [place_of(order[0], left) for order, left in zip(orders, lefts)]
    copy_count = sum(4 * outer for _, outer in cuts)
    args = (
        own_bits, core_bit, post, post_other, cot_pad.reshape(rows, width), cot_other,
        stay(expand_weight), stay(reduce_weight), expand_bias.reshape(1, hidden_width),
    )
    *parts, grad_b, out_own, grad_own, out_other, grad_0, grad_1 = call(
        functools.partial(feed_kernel, cuts, runs, run),
        [shape((half // 2, lanes), bf16)] * 6
        + [shape((1, half), f32), shape(flat, f32), shape(flat, f32), shape(flat, bf16)]
        + [shape((rows, width // 2), bf16)] * 2,
        args,
        prefetch=2,
        far_in=(8,),
        far_out=(6, 7),
        raw=tuple(range(2, 8)) + tuple(range(-1, -7, -1)),
        scratch=[pltpu.VMEM(double, bf16)] * 2
        + [pltpu.VMEM((width, half), bf16), pltpu.VMEM((half, width), bf16)]
        + [pltpu.VMEM((2 * rows, half), bf16)] * 2
        + [pltpu.VMEM((half, width), bf16)] * 2
        + [pltpu.SemaphoreType.DMA((4,)), pltpu.SemaphoreType.DMA((2, runs))]
        + [pltpu.SemaphoreType.DMA((copy_count,))],
        flops=6 * 2 * 2 * rows * width * half,
        vmem=52,
    )
    others = [pair_swap(v, "dp", 1).reshape(items, padded, width // 2) for v in (grad_0, grad_1)]
    out_other = pair_swap(out_other, "dp", 1).reshape(pad_item)

    class Scatter:
        def __init__(self):
            self.at, self.sends, self.keeps = 0, list(parts[0::2]), list(parts[1::2])

        def swap(self):
            self.recvs = []
            for send, order, left in zip(self.sends, orders, lefts):
                left.remove(order[self.at])
                self.recvs.append(pair_swap(send, *order[self.at]))
            self.at += 1
            return list(self.recvs)

        def add(self, after=()):
            cuts = [place_of(order[self.at], left) for order, left in zip(orders, lefts)]
            left_rows = self.keeps[0].shape[0]
            dims = [(outer, 2, left_rows // (2 * outer), lanes) for _, outer in cuts]
            ins = [v.reshape(d) for keep, recv, d in zip(self.keeps, self.recvs, dims) for v in (keep, recv)]
            outs = call(
                functools.partial(combine_kernel, [place for place, _ in cuts]),
                [shape((d[0], d[2], lanes), bf16) for d in dims for _ in range(2)],
                (own_bits, *ins),
                prefetch=1,
                far_in=range(1, 7),
                far_out=range(6),
                after=after,
            )
            outs = [v.reshape(left_rows // 2, lanes) for v in outs]
            self.sends, self.keeps = outs[0::2], outs[1::2]
            return outs

    scatter = Scatter()
    scatter.swap()

    args = (
        box, own_row, mixed, grad_own.reshape(pad_item), *others, cot_pad, holes, post_gain, tables["inv"],
    )
    grad_mixed, send, post_sums = call(
        functools.partial(post_kernel, *names),
        [shape(row_item, f32), shape(mode_dims, bf16), shape((3, width), f32)],
        args,
        prefetch=2,
        far_in=(6, 7, 8, 9),
        flops=lon_flops,
    )
    (result,) = call(
        result_kernel,
        [shape(row_item, bf16)],
        (mixed, out_own.reshape(pad_item), out_other, reduce_bias),
        far_in=(1, 3),
        after=(send,),
    )
    recv = exchange(send, True)

    bias_row = 3 * width // 128 + hidden_width // 128
    small_rows = -(-(bias_row + 4 * block_count) // 16) * 16
    small_dims = (small_rows, 128)
    (small,) = call(
        functools.partial(small_kernel, (run // 128, runs, block_count)),
        [shape(small_dims, f32)],
        (core_bit, post_sums, grad_b),
        prefetch=1,
    )
    base = block_size * 3 // 2
    places = jnp.stack([core, own_block]).astype(jnp.int32)
    packed_weight = (base + small_rows, 128)
    args = (places, recv, spec, hid, slope, shrunk, inner, outer, *turns, small)
    send, weight_send, weight_keep = call(
        functools.partial(filter_back_kernel, chunk, bias_row, block_count),
        [shape(grid_dims, bf16)] + [shape(packed_weight, f32)] * 2,
        args,
        prefetch=1,
        far_in=(8, 9, 10, 5, 4, 2, 3),
        scratch=[pltpu.VMEM(spectrum, bf16)] * 4,
        flops=2 * filter_flops,
    )
    recv = exchange(send, False)

    weight = [weight_keep, pair_swap(weight_send, "dp", 1)]
    for step in dp_bits + [n for n in lat_bits if n[1] < sub]:
        weight = [weight[0] + weight[1]]
        weight.append(pair_swap(weight[0], *step))

    args = (box, own_row, recv, token_items, grad_mixed, holes, pre_gain, tables["fwd_t"])
    tail_dims = (dp_size * groups, -(-2 * width // 2048) * 16, 128)
    grad_tokens, tail = call(
        functools.partial(last_kernel, *names),
        [shape(row_item, f32), shape(tail_dims, bf16)],
        args,
        prefetch=2,
        far_in=(7, 5, 6),
        far_out=(1,),
        flops=lon_flops,
    )

    tail = lax.all_to_all(tail, ("dp", "lat"), 0, 0, tiled=True)
    gather_bits = [b for _, b in lat_bits if b >= sub]
    first_dims, second_dims = (base + 2 * small_rows, 128), (2 * base + 2 * small_rows, 128)
    while scatter.at < len(bit_names):
        stage = scatter.at
        if stage == 2:
            first, small = call(
                first_kernel, [shape(first_dims, bf16), shape(small_dims, f32)], weight, after=sums[:1]
            )
            first_recv = pair_swap(first, "lat", gather_bits[0])
        if stage == 3:
            second, small = call(
                second_kernel, [shape(second_dims, bf16), shape(small_dims, f32)], (first, first_recv, small),
                after=(grad_tokens,),
            )
            far_masks = [m * gather_bits[1] for m in range(1, block_count // 2)]
            second_recvs = [pair_swap(second, "lat", m) for m in far_masks]
            weight, small = call(
                third_kernel,
                [shape((block_count * base, 128), bf16), shape(small_dims, f32)],
                (second, *second_recvs, small),
            )
        ahead = {1: (send, weight[-1], result), 2: (grad_tokens,), 3: (tail, weight)}
        sums = scatter.add(ahead.get(stage, ()))
        scatter.swap()
    weight_other = pair_swap(weight, "dp", 1)
    merged = [v for pair in zip(scatter.keeps, scatter.recvs) for v in pair]
    expand_part, reduce_part = call(
        shard_kernel,
        [shape((own_rows, width), f32)] * 2,
        merged,
        far_in=range(6),
    )
    expand_part = expand_part.T

    rows_of = (block_size * 3 // 2, 128)
    args = (places, tail, small, weight.reshape(-1, *rows_of), weight_other.reshape(-1, *rows_of))
    line_dims = (width,)
    filter_dims, bias_dims = filter_inner.shape, filter_inner_bias.shape
    out_dims = [line_dims, line_dims, filter_dims, bias_dims, filter_dims, bias_dims]
    out_dims += [line_dims, line_dims, (hidden_width,), line_dims]
    sums = call(tail_kernel, [shape(d, f32) for d in out_dims], args, prefetch=1)
    return (
        result.reshape(tokens.shape),
        grad_tokens.reshape(tokens.shape),
        *sums[:8],
        expand_part,
        sums[8],
        reduce_part,
        sums[9],
    )


def solution(mesh):
    rows = P(None, "dp", "lat", None, None)
    in_specs = (rows, P(None, "dp", None), P(None, "dp", "lat", None)) + (P(),) * 12 + (rows,)
    out_specs = (
        (rows, rows)
        + (P(),) * 8
        + (P(None, ("dp", "lat")), P(), P(("dp", "lat"), None), P())
    )
    return jax.shard_map(body, mesh=mesh, in_specs=in_specs, out_specs=out_specs, check_vma=False)
```

time: 195 us -> 172 us (0.88)
  local copies, waits for them, and re-layouts: 53.5 us -> 13.5 us
  Pallas kernels: 31.9 us -> 56.2 us
  other arithmetic: 16 us -> 1.13 us
  waiting for transfers between devices: 42.5 us -> 47.4 us
  starting transfers between devices: 47.9 us -> 51.7 us
    pallas_call x7 -> x17, Pallas kernels: 31.9 us -> 56.2 us  [call(): pl.pallas_call(whole_kernel, out_shape=shapes, grid_spec=pltpu.PrefetchSc...]
    all_to_all x2 -> x4, waiting for transfers between devices: 9.03 us -> 27.2 us  [exchange(): both = lax.all_to_all(both, 'lat', 0, 0, tiled=True)]
    all_to_all x3 -> x1, waiting for transfers between devices: 11.5 us -> 0.01 us  [body(): tail = lax.all_to_all(tail, ('dp', 'lat'), 0, 0, tiled=True)]
    unnamed x126 -> x40, local copies, waits for them, and re-layouts: 22.2 us -> 11.7 us
    convert_element_type x10 -> x0, other arithmetic: 8.59 us -> none  [the longest x9 7.55 us: halving_scatter(): part = part.astype(bf16)]
    dynamic_slice x9 -> x0, local copies, waits for them, and re-layouts: 8.58 us -> none  [halving_scatter(): away = lax.dynamic_slice_in_dim(part, 1 - own, 1, dim).astype(bf16)]
    reshape x15 -> x0, local copies, waits for them, and re-layouts: 6.84 us -> none  [the longest x2 1.35 us: place(): return lax.dynamic_update_slice_in_dim(spread, bias.reshape(2, 1, block_s...]
    all_to_all x2 -> x4, starting transfers between devices: 11.5 us -> 18.3 us  [exchange(): both = lax.all_to_all(both, 'lat', 0, 0, tiled=True)]
  transfers between devices with their start and end apart: 28 -> 29, of which waited for: 11 -> 16; matrix products, arithmetic and copies ran while one was open for 20% -> 4% of each run, Pallas kernels for 6% -> 14%
where the time goes in v1:
time: 172 us; the launch traced here: 171 us
  Pallas kernels  56.2 us (33%)
  starting transfers between devices  51.7 us (30%)
  waiting for transfers between devices  47.4 us (28%)
  local copies, waits for them, and re-layouts  13.5 us (8%)
    pallas_call x17, Pallas kernels, call(): pl.pallas_call(whole_kernel, out_shape=shapes, grid_spec=pltpu.PrefetchSc...  56.2 us
    ppermute x24, starting transfers between devices, pair_swap(): return lax.ppermute(operand, axis_name, [(i, i ^ bit) for i in range(size)])  27.7 us
    all_to_all x4, waiting for transfers between devices, exchange(): both = lax.all_to_all(both, 'lat', 0, 0, tiled=True)  27.2 us
    ppermute x24, waiting for transfers between devices, pair_swap(): return lax.ppermute(operand, axis_name, [(i, i ^ bit) for i in range(size)])  20.2 us
    all_to_all x4, starting transfers between devices, exchange(): both = lax.all_to_all(both, 'lat', 0, 0, tiled=True)  18.3 us
    unnamed x40, local copies, waits for them, and re-layouts  11.7 us
    all_to_all x1, starting transfers between devices, body(): tail = lax.all_to_all(tail, ('dp', 'lat'), 0, 0, tiled=True)  5.76 us
  transfers between devices with their start and end apart: 29, of which 16 were waited for; matrix products, arithmetic and copies ran while one was open for 4% of the time, Pallas kernels for 14%

profile of v1, /device:TPU:0, one launch (start us, length us, event | category | flops | bytes accessed | tf_op | source)
XLA Modules:
  0.0 171.1 jit_solution(5281539033295975751)
XLA Ops:
  2.4 2.8 %shard_map.326 = bf16[8,2,96,128]{3,2,1,0:T(8,128)(2,1)} custom-call(s32[2,1,2]{2,1,0:T(1,128)S(1)} %copy-done.4, s32[1]{0:T(128)} %bitcast.refs_1_, bf16[2,180,768]{2,1,0:T(8,128)(2,1)S(1)} %bitcast.75, s32[2,1,180]{2,1,0:T(1,128)} %bitcast.113, f32[768]{0:T(1024)} %refs_6_.7, f32[768]{0:T(1024)} %refs_6_.5, bf16[128,180]{1,0:T(8,128)(2,1)} %constant.106.clone.refs_6_), custom_call_target="tpu_custom_call" | custom-call | flops 70778880 | bytes 999860 | tf_op jit(solution)/shard_map/pallas_call | solution.py:604
  5.2 7.3 %all-to-all-start = ((bf16[8,192,128]{2,1,0:T(8,128)(2,1)}), bf16[8,192,128]{2,1,0:T(8,128)(2,1)S(1)}, u32[]{:S(2)}, u32[]{:S(2)}) async-start(bf16[8,192,128]{2,1,0:T(8,128)(2,1)} %bitcast.3), calls=%async_computation | async-start | bytes 786432 | tf_op jit(solution)/shard_map/all_to_all | solution.py:693
  15.2 9.0 %all-to-all-done = bf16[8,192,128]{2,1,0:T(8,128)(2,1)S(1)} async-done(((bf16[8,192,128]{2,1,0:T(8,128)(2,1)}), bf16[8,192,128]{2,1,0:T(8,128)(2,1)S(1)}, u32[]{:S(2)}, u32[]{:S(2)}) %all-to-all-start) | async-done | bytes 393248 | tf_op jit(solution)/shard_map/all_to_all | solution.py:693
  24.2 4.5 %shard_map.327 = (bf16[8,2,96,128]{3,2,1,0:T(8,128)(2,1)}, bf16[8,128,192]{2,1,0:T(8,128)(2,1)}, bf16[8,128,192]{2,1,0:T(8,128)(2,1)}, f32[8,128,192]{2,1,0:T(8,128)}, f32[8,128,192]{2,1,0:T(8,128)}) custom-call(bf16[8,2,96,128]{3,2,1,0:T(8,128)(2,1)S(1)} %bitcast.80, bf16[192,192]{1,0:T(8,128)(2,1)S(1)} %maximum_maximum_fusion.refs_1_.refs_6_, ...), custom_call_target="tpu_custom_call" | custom-call | flops 150994944 | bytes 3499520 | tf_op jit(solution)/shard_map/pallas_call | solution.py:604
  28.7 3.6 %all-to-all-start.1 = ((bf16[8,192,128]{2,1,0:T(8,128)(2,1)}), bf16[8,192,128]{2,1,0:T(8,128)(2,1)S(1)}, u32[]{:S(2)}, u32[]{:S(2)}) async-start(bf16[8,192,128]{2,1,0:T(8,128)(2,1)} %bitcast.9), calls=%async_computation.1 | async-start | bytes 786432 | tf_op jit(solution)/shard_map/all_to_all | solution.py:696
  32.5 11.4 %all-to-all-done.1 = bf16[8,192,128]{2,1,0:T(8,128)(2,1)S(1)} async-done(((bf16[8,192,128]{2,1,0:T(8,128)(2,1)}), bf16[8,192,128]{2,1,0:T(8,128)(2,1)S(1)}, u32[]{:S(2)}, u32[]{:S(2)}) %all-to-all-start.1) | async-done | bytes 393248 | tf_op jit(solution)/shard_map/all_to_all | solution.py:696
  43.9 2.7 %shard_map.328 = (f32[2,180,768]{2,1,0:T(8,128)S(1)}, bf16[2,192,768]{2,1,0:T(8,128)(2,1)S(1)}) custom-call(s32[2,1,2]{2,1,0:T(1,128)S(1)} %copy-done.5, s32[1]{0:T(128)} %bitcast.refs_1_, bf16[8,2,96,128]{3,2,1,0:T(8,128)(2,1)S(1)} %bitcast.82, bf16[2,180,768]{2,1,0:T(8,128)(2,1)S(1)} %bitcast.76, s32[2,1,180]{2,1,0:T(1,128)} %bitcast.114, f32[768]{0:T(1024)} %refs_6_.7, ...), custom_call_target="tpu_custom_call" | custom-call | flops 70778880 | bytes 2701748 | tf_op jit(solution)/shard_map/pallas_call | solution.py:604
  48.8 18.4 %shard_map.329 = (bf16[768,512]{1,0:T(8,128)(2,1)}, bf16[768,512]{1,0:T(8,128)(2,1)}, bf16[768,512]{1,0:T(8,128)(2,1)}, bf16[768,512]{1,0:T(8,128)(2,1)}, bf16[7...) custom-call(s32[4]{0:T(128)S(1)} %pad_add_fusion.refs_0_, ...), custom_call_target="tpu_custom_call" | custom-call | flops 10871635968 | bytes 20072468 | tf_op jit(solution)/shard_map/pallas_call | solution.py:604
  70.6 3.8 %shard_map.330 = (f32[2,180,768]{2,1,0:T(8,128)S(1)}, bf16[8,2,96,128]{3,2,1,0:T(8,128)(2,1)}, f32[3,768]{1,0:T(4,128)S(1)}) custom-call(s32[2,1,2]{2,1,0:T(1,128)S(1)} %copy-done.5, s32[1]{0:T(128)} %bitcast.refs_1_, f32[2,180,768]{2,1,0:T(8,128)S(1)} %get-tuple-element.78.refs_2_.refs_0_, f32[2,192,768]{2,1,0:T(8,128)S(1)} %bitcast.83, ...), custom_call_target="tpu_custom_call" | custom-call | flops 70778880 | bytes 5024180 | tf_op jit(solution)/shard_map/pallas_call | solution.py:604
  75.5 3.7 %all-to-all-start.2 = ((bf16[8,192,128]{2,1,0:T(8,128)(2,1)}), bf16[8,192,128]{2,1,0:T(8,128)(2,1)S(1)}, u32[]{:S(2)}, u32[]{:S(2)}) async-start(bf16[8,192,128]{2,1,0:T(8,128)(2,1)} %bitcast.26), calls=%async_computation.2 | async-start | bytes 786432 | tf_op jit(solution)/shard_map/all_to_all | solution.py:693
  84.2 6.9 %all-to-all-done.2 = bf16[8,192,128]{2,1,0:T(8,128)(2,1)S(1)} async-done(((bf16[8,192,128]{2,1,0:T(8,128)(2,1)}), bf16[8,192,128]{2,1,0:T(8,128)(2,1)S(1)}, u32[]{:S(2)}, u32[]{:S(2)}) %all-to-all-start.2) | async-done | bytes 393248 | tf_op jit(solution)/shard_map/all_to_all | solution.py:693
  91.1 5.6 %shard_map.333 = (bf16[8,2,96,128]{3,2,1,0:T(8,128)(2,1)}, f32[224,128]{1,0:T(8,128)S(1)}, f32[224,128]{1,0:T(8,128)S(1)}) custom-call(s32[2]{0:T(128)S(1)} %pad_add_fusion.1.refs_0_, bf16[8,2,96,128]{3,2,1,0:T(8,128)(2,1)S(1)} %bitcast.81, bf16[8,128,192]{2,1,0:T(8,128)(2,1)} %get-tuple-element.86.refs_2_, bf16[8,128,192]{2,1,0:T(8,128)(2,1)} %get-tuple-element.87.refs_3_, ...), custom_call_target="tpu_custom_call" | custom-call | flops 301989888 | bytes 3768328 | tf_op jit(solution)/shard_map/pallas_call | solution.py:604
  97.4 3.7 %all-to-all-start.3 = ((bf16[8,192,128]{2,1,0:T(8,128)(2,1)}), bf16[8,192,128]{2,1,0:T(8,128)(2,1)S(1)}, u32[]{:S(2)}, u32[]{:S(2)}) async-start(bf16[8,192,128]{2,1,0:T(8,128)(2,1)} %bitcast.28), calls=%async_computation.3 | async-start | bytes 786432 | tf_op jit(solution)/shard_map/all_to_all | solution.py:696
  107.9 3.9 %shard_map.335 = (bf16[4,96,512]{2,1,0:T(8,128)(2,1)}, bf16[4,96,512]{2,1,0:T(8,128)(2,1)}, bf16[4,96,512]{2,1,0:T(8,128)(2,1)}, bf16[4,96,512]{2,1,0:T(8,128)(2...) custom-call(s32[4]{0:T(128)S(1)} %pad_add_fusion.refs_0_, bf16[4,2,96,512]{3,2,1,0:T(8,128)(2,1)} %bitcast.97, ...), custom_call_target="tpu_custom_call" | custom-call | bytes 7077904 | tf_op jit(solution)/shard_map/pallas_call | solution.py:604
  119.8 2.8 %shard_map.334 = (f32[2,180,768]{2,1,0:T(8,128)S(1)}, bf16[32,16,128]{2,1,0:T(8,128)(2,1)}) custom-call(s32[2,1,2]{2,1,0:T(1,128)S(1)} %copy-done.5, s32[1]{0:T(128)} %bitcast.refs_1_, bf16[8,2,96,128]{3,2,1,0:T(8,128)(2,1)S(1)} %bitcast.79, bf16[2,180,768]{2,1,0:T(8,128)(2,1)S(1)} %bitcast.77, f32[2,180,768]{2,1,0:T(8,128)S(1)} %copy-done.2, ...), custom_call_target="tpu_custom_call" | custom-call | flops 70778880 | bytes 3339700 | tf_op jit(solution)/shard_map/pallas_call | solution.py:604
  126.3 2.5 %collective-permute-start.12 = (bf16[448,128]{1,0:T(8,128)(2,1)S(1)}, bf16[448,128]{1,0:T(8,128)(2,1)S(1)}, u32[]{:S(2)}, u32[]{:S(2)}) collective-permute-start(bf16[448,128]{1,0:T(8,128)(2,1)S(1)} %get-tuple-element.107.refs_0_), channel_id=1, source_target_pairs={{0,4},{1,5},{2,6},{3,7},{4,0},{5,1},{6,2},{7,3},{8,12},{9,13},{10,... | collective-permute-start | bytes 344072 | tf_op jit(solution)/shard_map/ppermute | solution.py:631
  128.9 5.8 %all-to-all-start.4 = ((bf16[32,16,128]{2,1,0:T(8,128)(2,1)}), bf16[32,16,128]{2,1,0:T(8,128)(2,1)S(1)}, u32[]{:S(2)}, u32[]{:S(2)}) async-start(bf16[32,16,128]{2,1,0:T(8,128)(2,1)} %get-tuple-element.95), calls=%async_computation.4 | async-start | bytes 262144 | tf_op jit(solution)/shard_map/all_to_all | solution.py:899
  134.7 3.0 %shard_map.340 = (bf16[2,96,512]{2,1,0:T(8,128)(2,1)}, bf16[2,96,512]{2,1,0:T(8,128)(2,1)}, bf16[1,192,512]{2,1,0:T(8,128)(2,1)}, bf16[1,192,512]{2,1,0:T(8,128)...) custom-call(s32[4]{0:T(128)S(1)} %pad_add_fusion.refs_0_, bf16[2,2,96,512]{3,2,1,0:T(8,128)(2,1)} %bitcast.100, ...), custom_call_target="tpu_custom_call" | custom-call | bytes 3538960 | tf_op jit(solution)/shard_map/pallas_call | solution.py:604
  142.6 2.7 %collective-permute-done.18 = bf16[192,512]{1,0:T(8,128)(2,1)S(1)} collective-permute-done((bf16[192,512]{1,0:T(8,128)(2,1)}, bf16[192,512]{1,0:T(8,128)(2,1)S(1)}, u32[]{:S(2)}, u32[]{:S(2)}) %collective-permute-start.18) | collective-permute-done | bytes 196640 | tf_op jit(solution)/shard_map/ppermute | solution.py:631
  148.3 2.7 %shard_map.341 = (bf16[1,96,512]{2,1,0:T(8,128)(2,1)}, bf16[1,96,512]{2,1,0:T(8,128)(2,1)}, bf16[1,96,512]{2,1,0:T(8,128)(2,1)}, bf16[1,96,512]{2,1,0:T(8,128)(2...) custom-call(s32[4]{0:T(128)S(1)} %pad_add_fusion.refs_0_, bf16[1,2,96,512]{3,2,1,0:T(8,128)(2,1)} %bitcast.104, ...), custom_call_target="tpu_custom_call" | custom-call | bytes 1769488 | tf_op jit(solution)/shard_map/pallas_call | solution.py:604
  151.0 2.5 %collective-permute-start.21 = (bf16[96,512]{1,0:T(8,128)(2,1)}, bf16[96,512]{1,0:T(8,128)(2,1)S(1)}, u32[]{:S(2)}, u32[]{:S(2)}) collective-permute-start(bf16[96,512]{1,0:T(8,128)(2,1)} %bitcast.125), channel_id=1, source_target_pairs={{0,4},{1,5},{2,6},{3,7},{4,0},{5,1},{6,2},{7,3},{8,12},{9,13},{10,... | collective-permute-start | bytes 294920 | tf_op jit(solution)/shard_map/ppermute | solution.py:631
  154.0 2.4 %collective-permute-start.23 = (bf16[96,512]{1,0:T(8,128)(2,1)}, bf16[96,512]{1,0:T(8,128)(2,1)S(1)}, u32[]{:S(2)}, u32[]{:S(2)}) collective-permute-start(bf16[96,512]{1,0:T(8,128)(2,1)} %bitcast.123), channel_id=1, source_target_pairs={{0,4},{1,5},{2,6},{3,7},{4,0},{5,1},{6,2},{7,3},{8,12},{9,13},{10,... | collective-permute-start | bytes 294920 | tf_op jit(solution)/shard_map/ppermute | solution.py:631
  159.8 3.1 %collective-permute-done.21.refs_1_ = bf16[96,512]{1,0:T(8,128)(2,1)S(1)} collective-permute-done((bf16[96,512]{1,0:T(8,128)(2,1)}, bf16[96,512]{1,0:T(8,128)(2,1)S(1)}, u32[]{:S(2)}, u32[]{:S(2)}) %collective-permute-start.21) | collective-permute-done | bytes 98336 | tf_op jit(solution)/shard_map/ppermute | solution.py:631
  168.8 2.3 %shard_map.339 = (f32[768]{0:T(1024)}, f32[768]{0:T(1024)}, f32[2,8,96,96]{3,2,1,0:T(8,128)}, f32[2,8,96]{2,1,0:T(8,128)}, f32[2,8,96,96]{3,2,1,0:T(8,128)}, /*i...) custom-call(s32[2]{0:T(128)S(1)} %pad_add_fusion.1.refs_0_, ...), custom_call_target="tpu_custom_call" | custom-call | bytes 1981448 | tf_op jit(solution)/shard_map/pallas_call | solution.py:604
  (102 shorter events, 52.9 us)
Async XLA Ops:
  5.2 19.0 %all-to-all-start = ((bf16[8,192,128]{2,1,0:T(8,128)(2,1)}), bf16[8,192,128]{2,1,0:T(8,128)(2,1)S(1)}, u32[]{:S(2)}, u32[]{:S(2)}) async-start(bf16[8,192,128]{2,1,0:T(8,128)(2,1)} %bitcast.3), calls=%async_computation | async-start | bytes 786432 | tf_op jit(solution)/shard_map/all_to_all | solution.py:693
  28.7 15.2 %all-to-all-start.1 = ((bf16[8,192,128]{2,1,0:T(8,128)(2,1)}), bf16[8,192,128]{2,1,0:T(8,128)(2,1)S(1)}, u32[]{:S(2)}, u32[]{:S(2)}) async-start(bf16[8,192,128]{2,1,0:T(8,128)(2,1)} %bitcast.9), calls=%async_computation.1 | async-start | bytes 786432 | tf_op jit(solution)/shard_map/all_to_all | solution.py:696
  32.5 14.4 %collective-permute-start.1 = (bf16[384,768]{1,0:T(8,128)(2,1)S(1)}, bf16[384,768]{1,0:T(8,128)(2,1)}, u32[]{:S(2)}, u32[]{:S(2)}) collective-permute-start(bf16[384,768]{1,0:T(8,128)(2,1)S(1)} %bitcast.93), channel_id=1, source_target_pairs={{0,8},{8,0},{16,24},{24,16},{1,9},{9,1},{17,25},{25,17},{2,10},{10... | collective-permute-start | bytes 1769480 | tf_op jit(solution)/shard_map/ppermute | solution.py:631
  75.5 15.6 %all-to-all-start.2 = ((bf16[8,192,128]{2,1,0:T(8,128)(2,1)}), bf16[8,192,128]{2,1,0:T(8,128)(2,1)S(1)}, u32[]{:S(2)}, u32[]{:S(2)}) async-start(bf16[8,192,128]{2,1,0:T(8,128)(2,1)} %bitcast.26), calls=%async_computation.2 | async-start | bytes 786432 | tf_op jit(solution)/shard_map/all_to_all | solution.py:693
  79.2 26.7 %collective-permute-start.7 = (bf16[768,512]{1,0:T(8,128)(2,1)}, bf16[768,512]{1,0:T(8,128)(2,1)}, u32[]{:S(2)}, u32[]{:S(2)}) collective-permute-start(bf16[768,512]{1,0:T(8,128)(2,1)} %get-tuple-element.99), channel_id=1, source_target_pairs={{0,16},{8,24},{16,0},{24,8},{1,17},{9,25},{17,1},{25,9},{2,18},{10... | collective-permute-start | bytes 2359304 | tf_op jit(solution)/shard_map/ppermute | solution.py:631
  80.7 25.1 %collective-permute-start.8 = (bf16[768,512]{1,0:T(8,128)(2,1)}, bf16[768,512]{1,0:T(8,128)(2,1)}, u32[]{:S(2)}, u32[]{:S(2)}) collective-permute-start(bf16[768,512]{1,0:T(8,128)(2,1)} %get-tuple-element.101), channel_id=1, source_target_pairs={{0,1},{1,0},{2,3},{3,2},{4,5},{5,4},{6,7},{7,6},{8,9},{9,8},{10,11... | collective-permute-start | bytes 2359304 | tf_op jit(solution)/shard_map/ppermute | solution.py:631
  82.7 23.6 %collective-permute-start.9 = (bf16[768,512]{1,0:T(8,128)(2,1)}, bf16[768,512]{1,0:T(8,128)(2,1)}, u32[]{:S(2)}, u32[]{:S(2)}) collective-permute-start(bf16[768,512]{1,0:T(8,128)(2,1)} %get-tuple-element.103), channel_id=1, source_target_pairs={{0,2},{1,3},{2,0},{3,1},{4,6},{5,7},{6,4},{7,5},{8,10},{9,11},{10,... | collective-permute-start | bytes 2359304 | tf_op jit(solution)/shard_map/ppermute | solution.py:631
  84.1 20.1 %collective-permute-start.2 = (bf16[384,768]{1,0:T(8,128)(2,1)}, bf16[384,768]{1,0:T(8,128)(2,1)S(1)}, u32[]{:S(2)}, u32[]{:S(2)}) collective-permute-start(bf16[384,768]{1,0:T(8,128)(2,1)} %copy-done.7), channel_id=1, source_target_pairs={{0,8},{8,0},{16,24},{24,16},{1,9},{9,1},{17,25},{25,17},{2,10},{10... | collective-permute-start | bytes 1769480 | tf_op jit(solution)/shard_map/ppermute | solution.py:631
  97.4 21.2 %all-to-all-start.3 = ((bf16[8,192,128]{2,1,0:T(8,128)(2,1)}), bf16[8,192,128]{2,1,0:T(8,128)(2,1)S(1)}, u32[]{:S(2)}, u32[]{:S(2)}) async-start(bf16[8,192,128]{2,1,0:T(8,128)(2,1)} %bitcast.28), calls=%async_computation.3 | async-start | bytes 786432 | tf_op jit(solution)/shard_map/all_to_all | solution.py:696
  111.9 16.9 %collective-permute-start.15 = (bf16[384,512]{1,0:T(8,128)(2,1)}, bf16[384,512]{1,0:T(8,128)(2,1)S(1)}, u32[]{:S(2)}, u32[]{:S(2)}) collective-permute-start(bf16[384,512]{1,0:T(8,128)(2,1)} %bitcast.86), channel_id=1, source_target_pairs={{0,1},{1,0},{2,3},{3,2},{4,5},{5,4},{6,7},{7,6},{8,9},{9,8},{10,11... | collective-permute-start | bytes 1179656 | tf_op jit(solution)/shard_map/ppermute | solution.py:631
  114.0 20.7 %collective-permute-start.16 = (bf16[384,512]{1,0:T(8,128)(2,1)}, bf16[384,512]{1,0:T(8,128)(2,1)}, u32[]{:S(2)}, u32[]{:S(2)}) collective-permute-start(bf16[384,512]{1,0:T(8,128)(2,1)} %bitcast.118), channel_id=1, source_target_pairs={{0,2},{1,3},{2,0},{3,1},{4,6},{5,7},{6,4},{7,5},{8,10},{9,11},{10,... | collective-permute-start | bytes 1179656 | tf_op jit(solution)/shard_map/ppermute | solution.py:631
  115.4 19.3 %collective-permute-start.17 = (bf16[384,512]{1,0:T(8,128)(2,1)}, bf16[384,512]{1,0:T(8,128)(2,1)}, u32[]{:S(2)}, u32[]{:S(2)}) collective-permute-start(bf16[384,512]{1,0:T(8,128)(2,1)} %bitcast.117), channel_id=1, source_target_pairs={{0,16},{8,24},{16,0},{24,8},{1,17},{9,25},{17,1},{25,9},{2,18},{10... | collective-permute-start | bytes 1179656 | tf_op jit(solution)/shard_map/ppermute | solution.py:631
  118.0 6.5 %collective-permute-start.10 = (bf16[304,128]{1,0:T(8,128)(2,1)S(1)}, bf16[304,128]{1,0:T(8,128)(2,1)S(1)}, u32[]{:S(2)}, u32[]{:S(2)}) collective-permute-start(bf16[304,128]{1,0:T(8,128)(2,1)S(1)} %get-tuple-element.105.refs_0_), channel_id=1, source_target_pairs={{0,1},{1,0},{2,3},{3,2},{4,5},{5,4},{6,7},{7,6},{8,9},{9,8},{10,11... | collective-permute-start | bytes 233480 | tf_op jit(solution)/shard_map/ppermute | solution.py:631
  124.5 16.6 %collective-permute-start.11 = (bf16[448,128]{1,0:T(8,128)(2,1)S(1)}, bf16[448,128]{1,0:T(8,128)(2,1)S(1)}, u32[]{:S(2)}, u32[]{:S(2)}) collective-permute-start(bf16[448,128]{1,0:T(8,128)(2,1)S(1)} %get-tuple-element.107.refs_0_), channel_id=1, source_target_pairs={{0,2},{1,3},{2,0},{3,1},{4,6},{5,7},{6,4},{7,5},{8,10},{9,11},{10,... | collective-permute-start | bytes 344072 | tf_op jit(solution)/shard_map/ppermute | solution.py:631
  126.3 16.2 %collective-permute-start.12 = (bf16[448,128]{1,0:T(8,128)(2,1)S(1)}, bf16[448,128]{1,0:T(8,128)(2,1)S(1)}, u32[]{:S(2)}, u32[]{:S(2)}) collective-permute-start(bf16[448,128]{1,0:T(8,128)(2,1)S(1)} %get-tuple-element.107.refs_0_), channel_id=1, source_target_pairs={{0,4},{1,5},{2,6},{3,7},{4,0},{5,1},{6,2},{7,3},{8,12},{9,13},{10,... | collective-permute-start | bytes 344072 | tf_op jit(solution)/shard_map/ppermute | solution.py:631
  128.7 13.8 %collective-permute-start.13 = (bf16[448,128]{1,0:T(8,128)(2,1)S(1)}, bf16[448,128]{1,0:T(8,128)(2,1)S(1)}, u32[]{:S(2)}, u32[]{:S(2)}) collective-permute-start(bf16[448,128]{1,0:T(8,128)(2,1)S(1)} %get-tuple-element.107.refs_0_), channel_id=1, source_target_pairs={{0,6},{1,7},{2,4},{3,5},{4,2},{5,3},{6,0},{7,1},{8,14},{9,15},{10,... | collective-permute-start | bytes 344072 | tf_op jit(solution)/shard_map/ppermute | solution.py:631
  128.9 18.7 %all-to-all-start.4 = ((bf16[32,16,128]{2,1,0:T(8,128)(2,1)}), bf16[32,16,128]{2,1,0:T(8,128)(2,1)S(1)}, u32[]{:S(2)}, u32[]{:S(2)}) async-start(bf16[32,16,128]{2,1,0:T(8,128)(2,1)} %get-tuple-element.95), calls=%async_computation.4 | async-start | bytes 262144 | tf_op jit(solution)/shard_map/all_to_all | solution.py:899
  137.7 7.6 %collective-permute-start.18 = (bf16[192,512]{1,0:T(8,128)(2,1)}, bf16[192,512]{1,0:T(8,128)(2,1)S(1)}, u32[]{:S(2)}, u32[]{:S(2)}) collective-permute-start(bf16[192,512]{1,0:T(8,128)(2,1)} %bitcast.122), channel_id=1, source_target_pairs={{0,2},{1,3},{2,0},{3,1},{4,6},{5,7},{6,4},{7,5},{8,10},{9,11},{10,... | collective-permute-start | bytes 589832 | tf_op jit(solution)/shard_map/ppermute | solution.py:631
  139.6 7.0 %collective-permute-start.19 = (bf16[192,512]{1,0:T(8,128)(2,1)}, bf16[192,512]{1,0:T(8,128)(2,1)S(1)}, u32[]{:S(2)}, u32[]{:S(2)}) collective-permute-start(bf16[192,512]{1,0:T(8,128)(2,1)} %bitcast.121), channel_id=1, source_target_pairs={{0,16},{8,24},{16,0},{24,8},{1,17},{9,25},{17,1},{25,9},{2,18},{10... | collective-permute-start | bytes 589832 | tf_op jit(solution)/shard_map/ppermute | solution.py:631
  141.0 6.6 %collective-permute-start.20 = (bf16[192,512]{1,0:T(8,128)(2,1)}, bf16[192,512]{1,0:T(8,128)(2,1)S(1)}, u32[]{:S(2)}, u32[]{:S(2)}) collective-permute-start(bf16[192,512]{1,0:T(8,128)(2,1)} %bitcast.120), channel_id=1, source_target_pairs={{0,1},{1,0},{2,3},{3,2},{4,5},{5,4},{6,7},{7,6},{8,9},{9,8},{10,11... | collective-permute-start | bytes 589832 | tf_op jit(solution)/shard_map/ppermute | solution.py:631
  142.6 26.2 %collective-permute-start.14 = (bf16[1152,128]{1,0:T(8,128)(2,1)S(1)}, bf16[1152,128]{1,0:T(8,128)(2,1)S(1)}, u32[]{:S(2)}, u32[]{:S(2)}) collective-permute-start(bf16[1152,128]{1,0:T(8,128)(2,1)S(1)} %get-tuple-element.110.refs_8_), channel_id=1, source_target_pairs={{0,8},{8,0},{16,24},{24,16},{1,9},{9,1},{17,25},{25,17},{2,10},{10... | collective-permute-start | bytes 884744 | tf_op jit(solution)/shard_map/ppermute | solution.py:631
  151.0 11.9 %collective-permute-start.21 = (bf16[96,512]{1,0:T(8,128)(2,1)}, bf16[96,512]{1,0:T(8,128)(2,1)S(1)}, u32[]{:S(2)}, u32[]{:S(2)}) collective-permute-start(bf16[96,512]{1,0:T(8,128)(2,1)} %bitcast.125), channel_id=1, source_target_pairs={{0,4},{1,5},{2,6},{3,7},{4,0},{5,1},{6,2},{7,3},{8,12},{9,13},{10,... | collective-permute-start | bytes 294920 | tf_op jit(solution)/shard_map/ppermute | solution.py:631
  153.5 11.5 %collective-permute-start.22 = (bf16[96,512]{1,0:T(8,128)(2,1)}, bf16[96,512]{1,0:T(8,128)(2,1)S(1)}, u32[]{:S(2)}, u32[]{:S(2)}) collective-permute-start(bf16[96,512]{1,0:T(8,128)(2,1)} %bitcast.124), channel_id=1, source_target_pairs={{0,4},{1,5},{2,6},{3,7},{4,0},{5,1},{6,2},{7,3},{8,12},{9,13},{10,... | collective-permute-start | bytes 294920 | tf_op jit(solution)/shard_map/ppermute | solution.py:631
  154.0 12.1 %collective-permute-start.23 = (bf16[96,512]{1,0:T(8,128)(2,1)}, bf16[96,512]{1,0:T(8,128)(2,1)S(1)}, u32[]{:S(2)}, u32[]{:S(2)}) collective-permute-start(bf16[96,512]{1,0:T(8,128)(2,1)} %bitcast.123), channel_id=1, source_target_pairs={{0,4},{1,5},{2,6},{3,7},{4,0},{5,1},{6,2},{7,3},{8,12},{9,13},{10,... | collective-permute-start | bytes 294920 | tf_op jit(solution)/shard_map/ppermute | solution.py:631
  (23 other events, 101.9 us)

commit v2 on v1

--- a/solution.py
+++ b/solution.py
@@ -11,6 +11,8 @@
 from jax.sharding import PartitionSpec as P
 
 MODES = 64
+GROUP = 2
+COMBINE_FLOPS = 2 * 10**10
 shrink_level = 0.01
 epsilon = 1e-05
 inv_root_two = 1.0 / math.sqrt(2.0)
@@ -190,18 +192,20 @@
     turn_rows(points_ref, spec_ref, turn_fwd_ref[...], swap_ref[...], chunk)
     spec.start()
     copies = []
-    for p in range(spec_ref.shape[0]):
-        pre = dot(spec_ref[p], inner_ref[...], 1, 0) + inner_bias_ref[...]
+    lat_count, points, wide = spec_ref.shape
+    for p in range(0, lat_count, GROUP):
+        rows, dims = slice(p, p + GROUP), (GROUP, points, wide)
+        pre = dot(spec_ref[rows].reshape(GROUP * points, wide), inner_ref[...], 1, 0) + inner_bias_ref[...]
         hid, slope = gelu_pair(pre)
         hid = hid.astype(bf16)
-        hid_ref[p] = hid
-        slope_ref[p] = slope
+        hid_ref[rows] = hid.reshape(dims)
+        slope_ref[rows] = slope.reshape(dims)
         mid = dot(hid, outer_ref[...], 1, 0) + outer_bias_ref[...]
         filt, shrunk = shrink_pair(mid)
-        filt_ref[p] = filt.astype(bf16)
-        shrunk_ref[p] = shrunk
+        filt_ref[rows] = filt.astype(bf16).reshape(dims)
+        shrunk_ref[rows] = shrunk.reshape(dims)
         for at, (kept, out) in enumerate(((hid_ref, hid_out), (slope_ref, slope_out), (shrunk_ref, shrunk_out))):
-            copies.append(pltpu.make_async_copy(kept.at[p], out.at[p], sems.at[p, at]))
+            copies.append(pltpu.make_async_copy(kept.at[rows], out.at[rows], sems.at[p, at]))
             copies[-1].start()
     turn_rows(filt_ref, points_ref, turn_inv_ref[...], swap_ref[...], chunk)
     pack_all(points_ref, send_ref)
@@ -232,12 +236,12 @@
 
 
 def feed_kernel(
-    cuts, runs, run,
+    cuts, shares, runs, run,
     bit_ref, core_ref, post_own, post_other, cot_own, cot_other, expand_far, reduce_far, bias_ref,
     *refs,
 ):
     far_refs, refs = refs[:6], refs[6:]
-    bias_grad, out_own, grad_own_ref, out_other_ref, grad_0_ref, grad_1_ref, *refs = refs
+    bias_grad, out_own, grad_own, out_other_ref, grad_0_ref, grad_1_ref, *refs = refs
     post_ref, cot_ref, expand_ref, reduce_ref, hidden_ref, grad_ref, *refs = refs
     expand_grad_ref, reduce_grad_ref, row_sems, weight_sems, far_sems = refs
     rows = post_own.shape[0]
@@ -283,21 +287,22 @@
         here = slice(r * run, (r + 1) * run)
         expand_grad_ref[here] = dot(grad_ref[:, here], post, 0, 0).astype(bf16)
         reduce_grad_ref[here] = dot(hidden_ref[:, here], cot, 0, 0).astype(bf16)
-    lanes = post.shape[1] // 3
     copies = []
     for group, (at, outer) in enumerate(cuts):
         inner = runs * run // (2 * outer)
         own = bit_ref[at]
+        to_lanes = 0
         for side, source in enumerate((expand_grad_ref, reduce_grad_ref)):
+            lanes = shares[side][group]
+            from_lanes = sum(shares[side][:group])
             for o in range(outer):
                 for target, half in enumerate((1 - own, own)):
                     start = pl.multiple_of((2 * o + half) * inner, 16)
-                    part = source.at[pl.ds(start, inner), group * lanes : (group + 1) * lanes]
-                    to = far_refs[2 * group + target].at[
-                        o * inner : (o + 1) * inner, side * lanes : (side + 1) * lanes
-                    ]
+                    part = source.at[pl.ds(start, inner), from_lanes : from_lanes + lanes]
+                    to = far_refs[2 * group + target].at[o * inner : (o + 1) * inner, to_lanes : to_lanes + lanes]
                     copies.append(pltpu.make_async_copy(part, to, far_sems.at[len(copies)]))
                     copies[-1].start()
+            to_lanes += lanes
 
     out = dot(hidden_ref[...], reduce_ref[...], 1, 0)
     out_own.here[...] = out[:rows]
@@ -305,7 +310,8 @@
     out_other_ref[...] = out[rows:].astype(bf16)
     back = dot(grad_ref[...], expand_ref[...], 1, 1)
     half = back.shape[1] // 2
-    grad_own_ref[...] = back[:rows]
+    grad_own.here[...] = back[:rows]
+    grad_own.start()
     grad_0_ref[...] = back[rows:, :half].astype(bf16)
     grad_1_ref[...] = back[rows:, half:].astype(bf16)
     for copy in copies:
@@ -325,13 +331,17 @@
         outs[2 * at + 1].start()
 
 
-def shard_kernel(*refs):
+def shard_kernel(shares, *refs):
     *ins, expand_ref, reduce_ref = refs
-    lanes = ins[0].here.shape[1] // 2
+    starts = [0, 0]
     for at in range(len(ins) // 2):
         total = ins[2 * at][...].astype(f32) + ins[2 * at + 1][...].astype(f32)
-        expand_ref[:, at * lanes : (at + 1) * lanes] = total[:, :lanes]
-        reduce_ref[:, at * lanes : (at + 1) * lanes] = total[:, lanes:]
+        begin = 0
+        for side, ref in enumerate((expand_ref, reduce_ref)):
+            lanes = shares[side][at]
+            ref[:, starts[side] : starts[side] + lanes] = total[:, begin : begin + lanes]
+            starts[side] += lanes
+            begin += lanes
 
 
 def both_halves(first_ref, second_ref, item, cells):
@@ -339,30 +349,37 @@
 
 
 def result_kernel(mixed_ref, out_own_ref, out_other_ref, bias_ref, result_ref):
-    items, cells, _ = result_ref.shape
+    cells, items, _ = result_ref.shape
     for item in range(items):
         out = out_own_ref[item, :cells] + out_other_ref[item, :cells].astype(f32)
-        result_ref[item] = (mixed_ref[item] + (out + line(bias_ref))).astype(bf16)
+        value = (mixed_ref[item] + (out + line(bias_ref))).astype(bf16)
+        result_ref[:, item, :] = value
 
 
 def post_kernel(
     lat_rows, block_size, sub,
     box_ref, row_ref, mixed_ref, grad_own_ref, grad_0_ref, grad_1_ref, cot_ref, hole_ref, gain_ref, table_ref,
-    grad_mixed, send_ref, sum_ref,
+    grad_mixed, send_ref, sum_ref, mixed_grad_ref, sems,
 ):
-    items, cells, _ = grad_mixed.shape
+    items, cells, _ = mixed_grad_ref.shape
     sums = 0.0
+    copies = []
+    parts = [norm_parts(mixed_ref[item]) for item in range(items)]
     for item in range(items):
-        valid = valid_row(item, box_ref, row_ref, hole_ref, lat_rows, cells)
+        unit, inv_scale = parts[item]
         grad = grad_own_ref[item, :cells] + both_halves(grad_0_ref, grad_1_ref, item, cells)
-        unit, inv_scale = norm_parts(mixed_ref[item])
         cot = cot_ref[item, :cells].astype(f32)
         sums += jnp.concatenate([jnp.sum(v, axis=0, keepdims=True) for v in (grad * unit, grad, cot)], axis=0)
         value = cot + norm_back(grad, unit, inv_scale, line(gain_ref))
-        grad_mixed[item] = value
+        mixed_grad_ref[item] = value
+        copies.append(pltpu.make_async_copy(mixed_grad_ref.at[item], grad_mixed.at[item], sems.at[item]))
+        copies[-1].start()
+        valid = valid_row(item, box_ref, row_ref, hole_ref, lat_rows, cells)
         table = (table_ref[...].astype(f32) * valid).astype(bf16)
         put_modes(send_ref, item, dot(table, value.astype(bf16), 1, 0), block_size, sub)
     sum_ref[...] = sums
+    for copy in copies:
+        copy.wait()
 
 
 def small_kernel(layout, core_ref, post_sum_ref, expand_bias_ref, small_ref):
@@ -379,83 +396,129 @@
 
 
 def filter_back_kernel(
-    chunk, bias_row, blocks, place_ref,
-    recv_ref, spec_ref, hid_ref, slope_ref, shrunk_ref, inner_ref, outer_ref,
-    turn_fwd_ref, turn_inv_ref, swap_ref, small_ref,
-    send_ref, weight_send_ref, weight_keep_ref,
-    turned_ref, grad_mid_ref, grad_pre_ref, points_ref,
+    chunk,
+    recv_ref, slope_ref, shrunk_ref, inner_ref, outer_ref, turn_fwd_ref, turn_inv_ref, swap_ref,
+    send_ref, grad_mid, grad_pre, bias_ref,
+    turned_ref, points_ref,
 ):
     lat_count, points, wide = turned_ref.shape
-    unpack_all(recv_ref, grad_mid_ref)
-    turn_rows(grad_mid_ref, turned_ref, turn_fwd_ref[...], swap_ref[...], chunk)
+    grad_mid_ref, grad_pre_ref = grad_mid.here, grad_pre.here
+    unpack_all(recv_ref, points_ref)
+    turn_rows(points_ref, turned_ref, turn_fwd_ref[...], swap_ref[...], chunk)
     inner_bias = jnp.zeros((1, wide), f32)
     outer_bias = jnp.zeros((1, wide), f32)
-    for p in range(lat_count):
-        grad_mid = (turned_ref[p].astype(f32) * shrunk_ref[p]).astype(bf16)
-        grad_mid_ref[p] = grad_mid
-        outer_bias += jnp.sum(grad_mid.astype(f32), axis=0, keepdims=True)
-        grad_pre = (dot(grad_mid, outer_ref[...], 1, 1) * slope_ref[p]).astype(bf16)
-        grad_pre_ref[p] = grad_pre
-        inner_bias += jnp.sum(grad_pre.astype(f32), axis=0, keepdims=True)
-        turned_ref[p] = dot(grad_pre, inner_ref[...], 1, 1).astype(bf16)
+    for p in range(0, lat_count, GROUP):
+        rows, dims, flat = slice(p, p + GROUP), (GROUP, points, wide), (GROUP * points, wide)
+        mid = (turned_ref[rows].astype(f32) * shrunk_ref[rows]).astype(bf16).reshape(flat)
+        grad_mid_ref[rows] = mid.reshape(dims)
+        outer_bias += jnp.sum(mid.astype(f32), axis=0, keepdims=True)
+        pre = (dot(mid, outer_ref[...], 1, 1) * slope_ref[rows].reshape(flat)).astype(bf16)
+        grad_pre_ref[rows] = pre.reshape(dims)
+        inner_bias += jnp.sum(pre.astype(f32), axis=0, keepdims=True)
+        turned_ref[rows] = dot(pre, inner_ref[...], 1, 1).astype(bf16).reshape(dims)
+    grad_mid.start()
+    grad_pre.start()
     turn_rows(turned_ref, points_ref, turn_inv_ref[...], swap_ref[...], chunk)
     pack_all(points_ref, send_ref)
-    flat = (lat_count * points, wide)
-    half = wide // 2
-    base = weight_keep_ref.shape[0] - small_ref.shape[0]
+    bias_ref[0:1] = inner_bias
+    bias_ref[1:2] = outer_bias
+
+
+def filter_weight_kernel(
+    bias_row, blocks, place_ref, spec_ref, hid_ref, grad_mid_ref, grad_pre_ref, bias_ref, small_in_ref,
+    send_ref, keep_ref, small_ref,
+):
+    lat_count, points, wide = spec_ref.shape
+    flat, half = (lat_count * points, wide), wide // 2
     own = place_ref[0]
+    count = small_ref.shape[0] // 2
+    base = keep_ref.shape[0] - count
+    small_ref[...] = small_in_ref[...]
+    for at in range(2):
+        for side in range(2):
+            row = bias_row + (2 * at + side) * blocks + place_ref[1]
+            small_ref[pl.ds(row, 1), :half] = bias_ref[at : at + 1, side * half : (side + 1) * half]
     for at, (left, right) in enumerate(((spec_ref, grad_pre_ref), (hid_ref, grad_mid_ref))):
         grad = dot(left[...].reshape(flat), right[...].reshape(flat), 0, 0)
         first = grad[:half, :half] + grad[half:, half:]
         second = grad[:half, half:] - grad[half:, :half]
         top, rest = pack(jnp.concatenate([first, second], axis=1))
+        share = small_ref[at * count : (at + 1) * count]
 
         @pl.when(own == at)
         def _():
-            weight_keep_ref[:half] = top
-            weight_keep_ref[half:base] = rest
+            keep_ref[:half] = top
+            keep_ref[half:base] = rest
+            keep_ref[base:] = share
 
         @pl.when(own != at)
         def _():
-            weight_send_ref[:half] = top
-            weight_send_ref[half:base] = rest
-
-    weight_keep_ref[base:] = small_ref[...]
-    for at, bias in enumerate((inner_bias, outer_bias)):
-        for side in range(2):
-            row = bias_row + (2 * at + side) * blocks + place_ref[1]
-            weight_keep_ref[pl.ds(base + row, 1), :half] = bias[:, side * half : (side + 1) * half]
-    weight_send_ref[base:] = weight_keep_ref[base:]
+            send_ref[:half] = top
+            send_ref[half:base] = rest
+            send_ref[base:] = share
+
+
+def halve_kernel(base, place_ref, own_ref, recv_ref, send_ref, keep_ref):
+    low_own = place_ref[2] == 0
+    total = own_ref[...] + recv_ref[...]
+    at = 0
+    for begin, end in ((0, base), (base, total.shape[0])):
+        count = (end - begin) // 2
+        first, second = total[begin : begin + count], total[begin + count : end]
+        send_ref[at : at + count] = jnp.where(low_own, second, first)
+        keep_ref[at : at + count] = jnp.where(low_own, first, second)
+        at += count
+
+
+def last_sums_kernel(
+    lat_rows, block_size, sub, base,
+    box_ref, row_ref, recv_ref, token_ref, grad_mixed_ref, hole_ref, table_ref, own_ref, other_ref,
+    tail,
+):
+    items, cells, width = token_ref.shape
+    backs = [get_modes(recv_ref, item, block_size, sub) for item in range(items)]
+    units = [norm_parts(token_ref[item].astype(f32))[0] for item in range(items)]
+    sums = 0.0
+    for item in range(items):
+        valid = as_column(valid_row(item, box_ref, row_ref, hole_ref, lat_rows, cells))
+        grad = grad_mixed_ref[item] + valid * dot(table_ref[...], backs[item], 1, 0)
+        sums += jnp.concatenate([jnp.sum(v, axis=0, keepdims=True) for v in (grad * units[item], grad)], axis=0)
+
+    rows = own_ref.shape[0] - base
+    total = own_ref[...] + other_ref[...]
+    value_ref = tail.here.at[0]
+    value_ref[:base] = total[:base].astype(bf16)
+    put_split(value_ref, base, total[base:])
+    per_line, at = width // 128, base + 2 * rows
+    value_ref[at:] = jnp.zeros((value_ref.shape[0] - at, 128), bf16)
+    for i in range(2):
+        for j in range(per_line):
+            row = at + i * per_line + j
+            value_ref[row : row + 1] = sums[i : i + 1, j * 128 : (j + 1) * 128].astype(bf16)
+    value = value_ref[...]
+    for group in range(1, tail.shape[0]):
+        tail.here[group] = value
+    tail.start()
 
 
 def last_kernel(
     lat_rows, block_size, sub,
     box_ref, row_ref, recv_ref, token_ref, grad_mixed_ref, hole_ref, gain_ref, table_ref,
-    result_ref, tail,
+    result, result_ref, sems,
 ):
     items, cells, width = token_ref.shape
-    backs = [get_modes(recv_ref, item, block_size, sub) for item in range(items)]
-    parts = [norm_parts(token_ref[item].astype(f32)) for item in range(items)]
-    sums = 0.0
-    grads = []
+    copies = []
     for item in range(items):
+        back = get_modes(recv_ref, item, block_size, sub)
+        unit, inv_scale = norm_parts(token_ref[item].astype(f32))
         valid = as_column(valid_row(item, box_ref, row_ref, hole_ref, lat_rows, cells))
-        grad = grad_mixed_ref[item] + valid * dot(table_ref[...], backs[item], 1, 0)
-        grads.append(grad)
-        sums += jnp.concatenate([jnp.sum(v, axis=0, keepdims=True) for v in (grad * parts[item][0], grad)], axis=0)
-
-    per_line = width // 128
-    pieces = [sums[i : i + 1, j * 128 : (j + 1) * 128] for i in range(2) for j in range(per_line)]
-    pad = tail.shape[1] - 2 * per_line
-    if pad:
-        pieces.append(jnp.zeros((pad, 128), f32))
-    value = jnp.concatenate(pieces, axis=0).astype(bf16)
-    for device in range(tail.shape[0]):
-        tail.here[device] = value
-    tail.start()
-    for item in range(items):
-        unit, inv_scale = parts[item]
-        result_ref[item] = grad_mixed_ref[item] + norm_back(grads[item], unit, inv_scale, line(gain_ref))
+        grad = grad_mixed_ref[item] + valid * dot(table_ref[...], back, 1, 0)
+        value = grad_mixed_ref[item] + norm_back(grad, unit, inv_scale, line(gain_ref))
+        result_ref[item] = value[:, None, :]
+        copies.append(pltpu.make_async_copy(result_ref.at[item], result.at[item], sems.at[item]))
+        copies[-1].start()
+    for copy in copies:
+        copy.wait()
 
 
 def put_split(ref, at, value):
@@ -465,49 +528,65 @@
     ref[at + rows : at + 2 * rows] = (value - high.astype(f32)).astype(bf16)
 
 
-def get_split(ref, rows):
-    at = ref.shape[0] - 2 * rows
-    return ref[at : at + rows].astype(f32) + ref[at + rows :].astype(f32)
-
-
-def first_kernel(own_ref, recv_ref, send_ref, small_ref):
-    rows = small_ref.shape[0]
-    base = own_ref.shape[0] - rows
-    send_ref[:base] = (own_ref[:base] + recv_ref[:base]).astype(bf16)
-    total = own_ref[base:] + recv_ref[base:]
-    small_ref[...] = total
-    put_split(send_ref, base, total)
-
-
-def second_kernel(own_ref, recv_ref, small_in_ref, send_ref, small_ref):
-    rows = small_ref.shape[0]
-    base = own_ref.shape[0] - 2 * rows
-    send_ref[:base] = own_ref[:base]
-    send_ref[base : 2 * base] = recv_ref[:base]
-    total = small_in_ref[...] + get_split(recv_ref, rows)
-    small_ref[...] = total
-    put_split(send_ref, 2 * base, total)
-
-
-def third_kernel(*refs):
-    *parts, small_in_ref, weight_ref, small_ref = refs
-    rows = small_ref.shape[0]
-    both = parts[0].shape[0] - 2 * rows
-    total = small_in_ref[...]
+def get_split(ref, at, rows):
+    return ref[at : at + rows].astype(f32) + ref[at + rows : at + 2 * rows].astype(f32)
+
+
+def third_kernel(sub, rows, pre_rows, recv_ref, *refs):
+    *other_refs, out_ref = refs
+    groups, total_rows, _ = recv_ref.shape
+    base = total_rows - 2 * rows - pre_rows
+    blocks = groups // sub
+    total = 0.0
+    for block in range(blocks):
+        part = recv_ref[block * sub]
+        out_ref[block * base : (block + 1) * base] = part[:base]
+        total += part[base : base + rows].astype(f32) + part[base + rows : base + 2 * rows].astype(f32)
+    put_split(out_ref, blocks * base, total)
+    total = jnp.sum(recv_ref[:, base + 2 * rows :].astype(f32), axis=0)
+    for ref in other_refs:
+        total += jnp.sum(ref[...].astype(f32), axis=0)
+    put_split(out_ref, blocks * base + 2 * rows, total)
+
+
+def join_kernel(*refs):
+    *parts, out_ref = refs
+    rows = parts[0].shape[0]
     for at, ref in enumerate(parts):
-        weight_ref[at * both : (at + 1) * both] = ref[:both]
-        if at:
-            total += get_split(ref, rows)
-    small_ref[...] = total
+        out_ref[at * rows : (at + 1) * rows] = ref[...]
 
 
 def tail_kernel(
-    place_ref, tail_ref, small_ref, weight_ref, weight_other_ref,
-    pre_gain_ref, pre_shift_ref, inner_ref, inner_bias_ref, outer_ref, outer_bias_ref,
-    post_gain_ref, post_shift_ref, expand_bias_ref, reduce_bias_ref,
+    count, rows, pre_rows, place_ref, *refs,
 ):
+    parts, refs = list(refs[:count]), refs[count:]
+    joined = parts.pop()
+    size = parts[0].shape[0]
+    parts += [joined.at[at * size : (at + 1) * size] for at in range(len(parts))]
+    count = len(parts)
+    (
+        pre_gain_ref, pre_shift_ref, inner_ref, inner_bias_ref, outer_ref, outer_bias_ref,
+        post_gain_ref, post_shift_ref, expand_bias_ref, reduce_bias_ref, small_ref,
+    ) = refs
+    own, y_own = place_ref[0], place_ref[2]
+
+    def in_order(values):
+        if count == 4:
+            pairs = [values[0:2], values[2:4]]
+            sides = [
+                [jnp.where(y_own == 0, a, b), jnp.where(y_own == 0, b, a)] for a, b in pairs
+            ]
+        else:
+            sides = [values[0:1], values[1:2]]
+        joined = [jnp.concatenate(side, axis=0) if len(side) > 1 else side[0] for side in sides]
+        return jnp.where(own == 0, joined[0], joined[1]), jnp.where(own == 0, joined[1], joined[0])
+
+    pre_at = parts[0].shape[0] - 2 * pre_rows
+    small_at = pre_at - 2 * rows
+    for at, value in enumerate(in_order([get_split(ref, small_at, rows) for ref in parts])):
+        small_ref[at * value.shape[0] : (at + 1) * value.shape[0]] = value
     per_line = pre_gain_ref.shape[0] // 128
-    sums = jnp.sum(tail_ref[:, : 2 * per_line].astype(f32), axis=0)
+    sums = sum(get_split(ref, pre_at, pre_rows) for ref in parts)
 
     def put(ref, at, value):
         ref[pl.ds(at * 128, 128)] = value.reshape(128)
@@ -530,15 +609,13 @@
             for block in range(blocks):
                 ref[side, block : block + 1] = row(at)[:, :size]
                 at += 1
-    own = place_ref[0]
+    base = small_at // blocks
     for at in range(blocks):
-        mine = unpack(weight_ref[at].astype(f32))
-        theirs = unpack(weight_other_ref[at].astype(f32))
-        inner, outer = jnp.where(own == 0, mine, theirs), jnp.where(own == 0, theirs, mine)
-        block = at ^ place_ref[1]
-        for side in range(2):
-            inner_ref[side, block] = inner[:, side * size : (side + 1) * size]
-            outer_ref[side, block] = outer[:, side * size : (side + 1) * size]
+        cuts = [ref[at * base : (at + 1) * base].astype(f32) for ref in parts]
+        for ref, value in zip((inner_ref, outer_ref), in_order(cuts)):
+            value = unpack(value)
+            for side in range(2):
+                ref[side, at] = value[:, side * size : (side + 1) * size]
 
 
 class Far:
@@ -772,7 +849,9 @@
     def place_of(step, left):
         return bit_names.index(step), 2 ** left.index(step)
 
-    lanes = 2 * width // 3
+    third = width // 3
+    shares = ((third * 3 // 2, third, third // 2), (third,) * 3)
+    lanes = [a + b for a, b in zip(*shares)]
     flat, double = (rows, width), (2 * rows, width)
     cuts = [place_of(order[0], left) for order, left in zip(orders, lefts)]
     copy_count = sum(4 * outer for _, outer in cuts)
@@ -781,14 +860,14 @@
         stay(expand_weight), stay(reduce_weight), expand_bias.reshape(1, hidden_width),
     )
     *parts, grad_b, out_own, grad_own, out_other, grad_0, grad_1 = call(
-        functools.partial(feed_kernel, cuts, runs, run),
-        [shape((half // 2, lanes), bf16)] * 6
+        functools.partial(feed_kernel, cuts, shares, runs, run),
+        [shape((half // 2, n), bf16) for n in lanes for _ in range(2)]
         + [shape((1, half), f32), shape(flat, f32), shape(flat, f32), shape(flat, bf16)]
         + [shape((rows, width // 2), bf16)] * 2,
         args,
         prefetch=2,
         far_in=(8,),
-        far_out=(6, 7),
+        far_out=(6, 7, 8),
         raw=tuple(range(2, 8)) + tuple(range(-1, -7, -1)),
         scratch=[pltpu.VMEM(double, bf16)] * 2
         + [pltpu.VMEM((width, half), bf16), pltpu.VMEM((half, width), bf16)]
@@ -814,21 +893,22 @@
             self.at += 1
             return list(self.recvs)
 
-        def add(self, after=()):
+        def add(self, after=(), flops=0):
             cuts = [place_of(order[self.at], left) for order, left in zip(orders, lefts)]
             left_rows = self.keeps[0].shape[0]
-            dims = [(outer, 2, left_rows // (2 * outer), lanes) for _, outer in cuts]
+            dims = [(outer, 2, left_rows // (2 * outer), n) for (_, outer), n in zip(cuts, lanes)]
             ins = [v.reshape(d) for keep, recv, d in zip(self.keeps, self.recvs, dims) for v in (keep, recv)]
             outs = call(
                 functools.partial(combine_kernel, [place for place, _ in cuts]),
-                [shape((d[0], d[2], lanes), bf16) for d in dims for _ in range(2)],
+                [shape((d[0], d[2], d[3]), bf16) for d in dims for _ in range(2)],
                 (own_bits, *ins),
                 prefetch=1,
                 far_in=range(1, 7),
                 far_out=range(6),
                 after=after,
+                flops=flops,
             )
-            outs = [v.reshape(left_rows // 2, lanes) for v in outs]
+            outs = [v.reshape(left_rows // 2, v.shape[-1]) for v in outs]
             self.sends, self.keeps = outs[0::2], outs[1::2]
             return outs
 
@@ -843,20 +923,25 @@
         [shape(row_item, f32), shape(mode_dims, bf16), shape((3, width), f32)],
         args,
         prefetch=2,
-        far_in=(6, 7, 8, 9),
+        far_in=(3, 6, 8, 9, 7),
+        raw=(-1,),
+        scratch=[pltpu.VMEM(row_item, f32), pltpu.SemaphoreType.DMA((items,))],
         flops=lon_flops,
     )
     (result,) = call(
         result_kernel,
-        [shape(row_item, bf16)],
+        [shape((cells, items, width), bf16)],
         (mixed, out_own.reshape(pad_item), out_other, reduce_bias),
         far_in=(1, 3),
         after=(send,),
     )
     recv = exchange(send, True)
 
+    sums = scatter.add((send,), flops=COMBINE_FLOPS)
+    scatter.swap()
+
     bias_row = 3 * width // 128 + hidden_width // 128
-    small_rows = -(-(bias_row + 4 * block_count) // 16) * 16
+    small_rows = -(-(bias_row + 4 * block_count) // 32) * 32
     small_dims = (small_rows, 128)
     (small,) = call(
         functools.partial(small_kernel, (run // 128, runs, block_count)),
@@ -865,81 +950,124 @@
         prefetch=1,
     )
     base = block_size * 3 // 2
-    places = jnp.stack([core, own_block]).astype(jnp.int32)
-    packed_weight = (base + small_rows, 128)
-    args = (places, recv, spec, hid, slope, shrunk, inner, outer, *turns, small)
-    send, weight_send, weight_keep = call(
-        functools.partial(filter_back_kernel, chunk, bias_row, block_count),
-        [shape(grid_dims, bf16)] + [shape(packed_weight, f32)] * 2,
+    y_index = (dp_index // 2) % 2
+    places = jnp.stack([core, own_block, y_index]).astype(jnp.int32)
+    args = (recv, slope, shrunk, inner, outer, *turns)
+    send, grad_mid, grad_pre, filter_bias = call(
+        functools.partial(filter_back_kernel, chunk),
+        [shape(grid_dims, bf16), shape(spectrum, bf16), shape(spectrum, bf16), shape((2, wide), f32)],
         args,
+        far_in=(5, 7, 2, 1, 6),
+        far_out=(1, 2),
+        scratch=[pltpu.VMEM(spectrum, bf16)] * 2,
+        flops=2 * filter_flops,
+        after=[stay(v) for v in sums[:1]],
+    )
+    recv = exchange(send, False)
+
+    halves = len(dp_bits) > 0
+    packed_weight = (base + small_rows // 2, 128)
+    send_core, keep_core = call(
+        functools.partial(filter_weight_kernel, bias_row, block_count),
+        [shape(packed_weight, f32)] * 2,
+        (places, spec, hid, grad_mid, grad_pre, filter_bias, small),
         prefetch=1,
-        far_in=(8, 9, 10, 5, 4, 2, 3),
-        scratch=[pltpu.VMEM(spectrum, bf16)] * 4,
-        flops=2 * filter_flops,
-    )
-    recv = exchange(send, False)
-
-    weight = [weight_keep, pair_swap(weight_send, "dp", 1)]
-    for step in dp_bits + [n for n in lat_bits if n[1] < sub]:
+        far_in=(1, 4, 2, 3),
+        scratch=[pltpu.VMEM(small_dims, f32)],
+        after=[stay(scatter.recvs[2])],
+    )
+    weight = [keep_core, pair_swap(send_core, "dp", 1)]
+    sums = scatter.add((send, keep_core), flops=COMBINE_FLOPS)
+    ahead = scatter.swap()
+    own_base, own_small = base, small_rows // 2
+    if halves:
+        own_base, own_small = base // 2, small_rows // 4
+        send_y, keep_y = call(
+            functools.partial(halve_kernel, base),
+            [shape((own_base + own_small, 128), f32)] * 2,
+            (places, *weight),
+            prefetch=1,
+            after=[stay(sums[0])],
+        )
+        weight = [keep_y, pair_swap(send_y, *dp_bits[0])]
+    for step in dp_bits[1:] + [n for n in lat_bits if n[1] < sub]:
         weight = [weight[0] + weight[1]]
         weight.append(pair_swap(weight[0], *step))
-
-    args = (box, own_row, recv, token_items, grad_mixed, holes, pre_gain, tables["fwd_t"])
-    tail_dims = (dp_size * groups, -(-2 * width // 2048) * 16, 128)
-    grad_tokens, tail = call(
+    pre_rows = -(-2 * width // 2048) * 16
+    tail_dims = (groups, own_base + 2 * own_small + pre_rows, 128)
+    (tail_send,) = call(
+        functools.partial(last_sums_kernel, *names, own_base),
+        [shape(tail_dims, bf16)],
+        (box, own_row, recv, token_items, grad_mixed, holes, tables["fwd_t"], *weight),
+        prefetch=2,
+        far_in=(6, 5, 4),
+        far_out=(0,),
+        flops=lon_flops,
+        after=[stay(v) for v in ahead],
+    )
+    result_dims = (items, cells, 1, width)
+    (grad_tokens,) = call(
         functools.partial(last_kernel, *names),
-        [shape(row_item, f32), shape(tail_dims, bf16)],
-        args,
+        [shape(result_dims, f32)],
+        (box, own_row, recv, token_items, grad_mixed, holes, pre_gain, tables["fwd_t"]),
         prefetch=2,
-        far_in=(7, 5, 6),
-        far_out=(1,),
+        far_in=(7, 5, 4, 6),
+        raw=(-1,),
+        scratch=[pltpu.VMEM(result_dims, f32), pltpu.SemaphoreType.DMA((items,))],
         flops=lon_flops,
-    )
-
-    tail = lax.all_to_all(tail, ("dp", "lat"), 0, 0, tiled=True)
-    gather_bits = [b for _, b in lat_bits if b >= sub]
-    first_dims, second_dims = (base + 2 * small_rows, 128), (2 * base + 2 * small_rows, 128)
+        after=(stay(tail_send),),
+    )
+    tail = tail_send
+    tail = lax.all_to_all(tail, "lat", 0, 0, tiled=True)
+
     while scatter.at < len(bit_names):
-        stage = scatter.at
-        if stage == 2:
-            first, small = call(
-                first_kernel, [shape(first_dims, bf16), shape(small_dims, f32)], weight, after=sums[:1]
-            )
-            first_recv = pair_swap(first, "lat", gather_bits[0])
-        if stage == 3:
-            second, small = call(
-                second_kernel, [shape(second_dims, bf16), shape(small_dims, f32)], (first, first_recv, small),
-                after=(grad_tokens,),
-            )
-            far_masks = [m * gather_bits[1] for m in range(1, block_count // 2)]
-            second_recvs = [pair_swap(second, "lat", m) for m in far_masks]
-            weight, small = call(
-                third_kernel,
-                [shape((block_count * base, 128), bf16), shape(small_dims, f32)],
-                (second, *second_recvs, small),
-            )
-        ahead = {1: (send, weight[-1], result), 2: (grad_tokens,), 3: (tail, weight)}
-        sums = scatter.add(ahead.get(stage, ()))
+        sums = scatter.add((stay(tail_send),), flops=COMBINE_FLOPS)
         scatter.swap()
-    weight_other = pair_swap(weight, "dp", 1)
     merged = [v for pair in zip(scatter.keeps, scatter.recvs) for v in pair]
     expand_part, reduce_part = call(
-        shard_kernel,
+        functools.partial(shard_kernel, shares),
         [shape((own_rows, width), f32)] * 2,
         merged,
         far_in=range(6),
+                flops=COMBINE_FLOPS,
+        after=(result, stay(grad_tokens), tail),
     )
     expand_part = expand_part.T
-
-    rows_of = (block_size * 3 // 2, 128)
-    args = (places, tail, small, weight.reshape(-1, *rows_of), weight_other.reshape(-1, *rows_of))
+    extra = [n[1] for n in dp_bits[1:]]
+    masks = [sum(b for i, b in enumerate(extra) if m >> i & 1) for m in range(1, 2 ** len(extra))]
+    others = [pair_swap(tail[:, own_base + 2 * own_small :], "dp", m) for m in masks]
+    third_dims = (block_count * own_base + 2 * own_small + 2 * pre_rows, 128)
+    (third,) = call(
+        functools.partial(third_kernel, sub, own_small, pre_rows),
+        [shape(third_dims, bf16)],
+        (tail, *others),
+        after=(stay(sums[0]),),
+    )
+    thirds = [third]
+    if halves:
+        thirds.append(pair_swap(third, *dp_bits[0]))
+    (joined,) = call(
+        join_kernel,
+        [shape((len(thirds) * third_dims[0], 128), bf16)],
+        thirds,
+        after=(stay(reduce_part),),
+    )
+    thirds += [pair_swap(joined, "dp", 1)]
+
+    args = (places, *thirds)
     line_dims = (width,)
     filter_dims, bias_dims = filter_inner.shape, filter_inner_bias.shape
     out_dims = [line_dims, line_dims, filter_dims, bias_dims, filter_dims, bias_dims]
     out_dims += [line_dims, line_dims, (hidden_width,), line_dims]
-    sums = call(tail_kernel, [shape(d, f32) for d in out_dims], args, prefetch=1)
+    sums = call(
+        functools.partial(tail_kernel, len(thirds), own_small, pre_rows),
+        [shape(d, f32) for d in out_dims],
+        args,
+        prefetch=1,
+        scratch=[pltpu.VMEM(small_dims, f32)],
+    )
     return (
-        result.reshape(tokens.shape),
+        result.swapaxes(0, 1).reshape(tokens.shape),
         grad_tokens.reshape(tokens.shape),
         *sums[:8],
         expand_part,

time: 172 us -> 163 us (0.948)
  starting transfers between devices: 51.7 us -> 41.2 us
  Pallas kernels: 56.2 us -> 64.8 us
  local copies, waits for them, and re-layouts: 13.5 us -> 7.61 us
    ppermute x24 -> x21, starting transfers between devices: 27.7 us -> 18.3 us  [pair_swap(): return lax.ppermute(operand, axis_name, [(i, i ^ bit) for i in range(size)])]
    pallas_call x17 -> x19, Pallas kernels: 56.2 us -> 64.8 us  [call(): pl.pallas_call(whole_kernel, out_shape=shapes, grid_spec=pltpu.PrefetchSc...]
    all_to_all x4, waiting for transfers between devices: 27.2 us -> 20.4 us  [exchange(): both = lax.all_to_all(both, 'lat', 0, 0, tiled=True)]
    unnamed x40 -> x32, local copies, waits for them, and re-layouts: 11.7 us -> 5.85 us
    ppermute x24 -> x21, waiting for transfers between devices: 20.2 us -> 24.5 us  [pair_swap(): return lax.ppermute(operand, axis_name, [(i, i ^ bit) for i in range(size)])]
  transfers between devices with their start and end apart: 29 -> 26, of which waited for: 16 -> 12; matrix products, arithmetic and copies ran while one was open for 4% -> 2% of each run, Pallas kernels for 14% -> 22%
where the time goes in v2:
time: 163 us; the launch traced here: 162 us
  Pallas kernels  64.8 us (40%)
  waiting for transfers between devices  46.1 us (28%)
  starting transfers between devices  41.2 us (25%)
  local copies, waits for them, and re-layouts  7.61 us (5%)
    pallas_call x19, Pallas kernels, call(): pl.pallas_call(whole_kernel, out_shape=shapes, grid_spec=pltpu.PrefetchSc...  64.8 us
    ppermute x21, waiting for transfers between devices, pair_swap(): return lax.ppermute(operand, axis_name, [(i, i ^ bit) for i in range(size)])  24.5 us
    all_to_all x4, waiting for transfers between devices, exchange(): both = lax.all_to_all(both, 'lat', 0, 0, tiled=True)  20.4 us
    all_to_all x4, starting transfers between devices, exchange(): both = lax.all_to_all(both, 'lat', 0, 0, tiled=True)  18.4 us
    ppermute x21, starting transfers between devices, pair_swap(): return lax.ppermute(operand, axis_name, [(i, i ^ bit) for i in range(size)])  18.3 us
    unnamed x32, local copies, waits for them, and re-layouts  5.85 us
    all_to_all x1, starting transfers between devices, body(): tail = lax.all_to_all(tail, 'lat', 0, 0, tiled=True)  4.55 us
  transfers between devices with their start and end apart: 26, of which 12 were waited for; matrix products, arithmetic and copies ran while one was open for 2% of the time, Pallas kernels for 22%

profile of v2, /device:TPU:0, one launch (start us, length us, event | category | flops | bytes accessed | tf_op | source)
XLA Modules:
  0.0 161.9 jit_solution(1714329617192535546)
XLA Ops:
  2.4 2.8 %shard_map.326 = bf16[8,2,96,128]{3,2,1,0:T(8,128)(2,1)} custom-call(s32[2,1,2]{2,1,0:T(1,128)S(1)} %copy-done.1, s32[1]{0:T(128)} %bitcast.refs_1_, bf16[2,180,768]{2,1,0:T(8,128)(2,1)S(1)} %bitcast.76, s32[2,1,180]{2,1,0:T(1,128)} %bitcast.106, f32[768]{0:T(1024)} %refs_6_.9, f32[768]{0:T(1024)} %refs_6_.7, bf16[128,180]{1,0:T(8,128)(2,1)} %constant.110.clone.refs_6_), custom_call_target="tpu_custom_call" | custom-call | flops 70778880 | bytes 999860 | tf_op jit(solution)/shard_map/pallas_call | solution.py:681
  5.2 7.3 %all-to-all-start = ((bf16[8,192,128]{2,1,0:T(8,128)(2,1)}), bf16[8,192,128]{2,1,0:T(8,128)(2,1)S(1)}, u32[]{:S(2)}, u32[]{:S(2)}) async-start(bf16[8,192,128]{2,1,0:T(8,128)(2,1)} %bitcast.3), calls=%async_computation | async-start | bytes 786432 | tf_op jit(solution)/shard_map/all_to_all | solution.py:770
  15.2 9.0 %all-to-all-done = bf16[8,192,128]{2,1,0:T(8,128)(2,1)S(1)} async-done(((bf16[8,192,128]{2,1,0:T(8,128)(2,1)}), bf16[8,192,128]{2,1,0:T(8,128)(2,1)S(1)}, u32[]{:S(2)}, u32[]{:S(2)}) %all-to-all-start) | async-done | bytes 393248 | tf_op jit(solution)/shard_map/all_to_all | solution.py:770
  24.2 4.5 %shard_map.327 = (bf16[8,2,96,128]{3,2,1,0:T(8,128)(2,1)}, bf16[8,128,192]{2,1,0:T(8,128)(2,1)}, bf16[8,128,192]{2,1,0:T(8,128)(2,1)}, f32[8,128,192]{2,1,0:T(8,128)}, f32[8,128,192]{2,1,0:T(8,128)}) custom-call(bf16[8,2,96,128]{3,2,1,0:T(8,128)(2,1)S(1)} %bitcast.82, bf16[192,192]{1,0:T(8,128)(2,1)S(1)} %maximum_maximum_fusion.refs_1_.refs_3_, ...), custom_call_target="tpu_custom_call" | custom-call | flops 150994944 | bytes 3499520 | tf_op jit(solution)/shard_map/pallas_call | solution.py:681
  28.7 3.6 %all-to-all-start.1 = ((bf16[8,192,128]{2,1,0:T(8,128)(2,1)}), bf16[8,192,128]{2,1,0:T(8,128)(2,1)S(1)}, u32[]{:S(2)}, u32[]{:S(2)}) async-start(bf16[8,192,128]{2,1,0:T(8,128)(2,1)} %bitcast.9), calls=%async_computation.1 | async-start | bytes 786432 | tf_op jit(solution)/shard_map/all_to_all | solution.py:773
  32.6 11.4 %all-to-all-done.1 = bf16[8,192,128]{2,1,0:T(8,128)(2,1)S(1)} async-done(((bf16[8,192,128]{2,1,0:T(8,128)(2,1)}), bf16[8,192,128]{2,1,0:T(8,128)(2,1)S(1)}, u32[]{:S(2)}, u32[]{:S(2)}) %all-to-all-start.1) | async-done | bytes 393248 | tf_op jit(solution)/shard_map/all_to_all | solution.py:773
  48.9 18.5 %shard_map.329 = (bf16[768,640]{1,0:T(8,128)(2,1)}, bf16[768,640]{1,0:T(8,128)(2,1)}, bf16[768,512]{1,0:T(8,128)(2,1)}, bf16[768,512]{1,0:T(8,128)(2,1)}, bf16[7...) custom-call(s32[4]{0:T(128)S(1)} %pad_add_fusion.refs_0_, ...), custom_call_target="tpu_custom_call" | custom-call | flops 10871635968 | bytes 20072468 | tf_op jit(solution)/shard_map/pallas_call | solution.py:681
  72.4 4.6 %shard_map.330 = (f32[2,180,768]{2,1,0:T(8,128)}, bf16[8,2,96,128]{3,2,1,0:T(8,128)(2,1)}, f32[3,768]{1,0:T(4,128)S(1)}) custom-call(s32[2,1,2]{2,1,0:T(1,128)S(1)} %copy-done.2, s32[1]{0:T(128)} %bitcast.refs_1_, f32[2,180,768]{2,1,0:T(8,128)S(1)} %get-tuple-element.75.refs_2_.refs_0_, f32[2,192,768]{2,1,0:T(8,128)} %bitcast.94, ...), custom_call_target="tpu_custom_call" | custom-call | flops 70778880 | bytes 5024180 | tf_op jit(solution)/shard_map/pallas_call | solution.py:681
  77.0 3.7 %all-to-all-start.2 = ((bf16[8,192,128]{2,1,0:T(8,128)(2,1)}), bf16[8,192,128]{2,1,0:T(8,128)(2,1)S(1)}, u32[]{:S(2)}, u32[]{:S(2)}) async-start(bf16[8,192,128]{2,1,0:T(8,128)(2,1)} %bitcast.27), calls=%async_computation.2 | async-start | bytes 786432 | tf_op jit(solution)/shard_map/all_to_all | solution.py:770
  80.7 8.3 %collective-permute-done.7 = bf16[768,384]{1,0:T(8,128)(2,1)} collective-permute-done((bf16[768,384]{1,0:T(8,128)(2,1)}, bf16[768,384]{1,0:T(8,128)(2,1)}, u32[]{:S(2)}, u32[]{:S(2)}) %collective-permute-start.7) | collective-permute-done | bytes 589856 | tf_op jit(solution)/shard_map/ppermute | solution.py:708
  89.0 3.2 %collective-permute-done.6 = bf16[768,512]{1,0:T(8,128)(2,1)} collective-permute-done((bf16[768,512]{1,0:T(8,128)(2,1)}, bf16[768,512]{1,0:T(8,128)(2,1)}, u32[]{:S(2)}, u32[]{:S(2)}) %collective-permute-start.6) | collective-permute-done | bytes 786464 | tf_op jit(solution)/shard_map/ppermute | solution.py:708
  93.3 3.8 %shard_map.332 = (bf16[4,96,640]{2,1,0:T(8,128)(2,1)}, bf16[4,96,640]{2,1,0:T(8,128)(2,1)}, bf16[4,96,512]{2,1,0:T(8,128)(2,1)}, bf16[4,96,512]{2,1,0:T(8,128)(2...) custom-call(s32[4]{0:T(128)S(1)} %pad_add_fusion.refs_0_, bf16[4,2,96,640]{3,2,1,0:T(8,128)(2,1)} %bitcast.121, ...), custom_call_target="tpu_custom_call" | custom-call | flops 20000000000 | bytes 7077904 | tf_op jit(solution)/shard_map/pallas_call | solution.py:681
  99.4 3.9 %shard_map.333 = (bf16[8,2,96,128]{3,2,1,0:T(8,128)(2,1)}, bf16[8,128,192]{2,1,0:T(8,128)(2,1)}, bf16[8,128,192]{2,1,0:T(8,128)(2,1)}, f32[2,192]{1,0:T(2,128)S(1)}) custom-call(bf16[8,2,96,128]{3,2,1,0:T(8,128)(2,1)S(1)} %bitcast.84, f32[8,128,192]{2,1,0:T(8,128)} %get-tuple-element.83.refs_1_, f32[8,128,192]{2,1,0:T(8,128)} %get-tuple-element.84.refs_2_, ...), custom_call_target="tpu_custom_call" | custom-call | flops 301989888 | bytes 3499520 | tf_op jit(solution)/shard_map/pallas_call | solution.py:681
  103.3 3.7 %all-to-all-start.3 = ((bf16[8,192,128]{2,1,0:T(8,128)(2,1)}), bf16[8,192,128]{2,1,0:T(8,128)(2,1)S(1)}, u32[]{:S(2)}, u32[]{:S(2)}) async-start(bf16[8,192,128]{2,1,0:T(8,128)(2,1)} %bitcast.36), calls=%async_computation.3 | async-start | bytes 786432 | tf_op jit(solution)/shard_map/all_to_all | solution.py:773
  107.8 2.8 %shard_map.335 = (f32[192,128]{1,0:T(8,128)S(1)}, f32[192,128]{1,0:T(8,128)S(1)}) custom-call(s32[3]{0:T(128)S(1)} %pad_add_fusion.1.refs_0_, bf16[8,128,192]{2,1,0:T(8,128)(2,1)} %get-tuple-element.94.refs_1_, bf16[8,128,192]{2,1,0:T(8,128)(2,1)} %get-tuple-element.95.refs_2_, bf16[8,128,192]{2,1,0:T(8,128)(2,1)} %get-tuple-element.96.refs_3_, ...), custom_call_target="tpu_custom_call" | custom-call | bytes 1820172 | tf_op jit(solution)/shard_map/pallas_call | solution.py:681
  111.5 3.0 %shard_map.336 = (bf16[2,96,640]{2,1,0:T(8,128)(2,1)}, bf16[2,96,640]{2,1,0:T(8,128)(2,1)}, bf16[1,192,512]{2,1,0:T(8,128)(2,1)}, bf16[1,192,512]{2,1,0:T(8,128)...) custom-call(s32[4]{0:T(128)S(1)} %pad_add_fusion.refs_0_, bf16[2,2,96,640]{3,2,1,0:T(8,128)(2,1)} %bitcast.124, ...), custom_call_target="tpu_custom_call" | custom-call | flops 20000000000 | bytes 3538960 | tf_op jit(solution)/shard_map/pallas_call | solution.py:681
  120.7 3.3 %collective-permute-done.12.refs_8_ = f32[96,128]{1,0:T(8,128)S(1)} collective-permute-done((f32[96,128]{1,0:T(8,128)S(1)}, f32[96,128]{1,0:T(8,128)S(1)}, u32[]{:S(2)}, u32[]{:S(2)}) %collective-permute-start.12) | collective-permute-done | bytes 49184 | tf_op jit(solution)/shard_map/ppermute | solution.py:708
  125.1 3.3 %shard_map.338.refs_8_.refs_7_ = bf16[8,136,128]{2,1,0:T(8,128)(2,1)} custom-call(s32[2,1,2]{2,1,0:T(1,128)S(1)} %copy-done.2, s32[1]{0:T(128)} %bitcast.refs_1_, bf16[8,2,96,128]{3,2,1,0:T(8,128)(2,1)S(1)} %bitcast.80, bf16[2,180,768]{2,1,0:T(8,128)(2,1)S(1)} %bitcast.78, f32[2,180,768]{2,1,0:T(8,128)} %get-tuple-element.93.refs_4_, ...), custom_call_target="tpu_custom_call" | custom-call | flops 70778880 | bytes 2476468 | tf_op jit(solution)/shard_map/pallas_call | solution.py:681
  128.5 4.6 %all-to-all-start.4 = ((bf16[8,136,128]{2,1,0:T(8,128)(2,1)}), bf16[8,136,128]{2,1,0:T(8,128)(2,1)S(1)}, u32[]{:S(2)}, u32[]{:S(2)}) async-start(bf16[8,136,128]{2,1,0:T(8,128)(2,1)} %shard_map.338.refs_8_.refs_7_), calls=%async_computation.4 | async-start | bytes 557056 | tf_op jit(solution)/shard_map/all_to_all | solution.py:1021
  135.7 3.0 %collective-permute-start.17 = (bf16[96,640]{1,0:T(8,128)(2,1)}, bf16[96,640]{1,0:T(8,128)(2,1)S(1)}, u32[]{:S(2)}, u32[]{:S(2)}) collective-permute-start(bf16[96,640]{1,0:T(8,128)(2,1)} %bitcast.104), channel_id=1, source_target_pairs={{0,4},{1,5},{2,6},{3,7},{4,0},{5,1},{6,2},{7,3},{8,12},{9,13},{10,... | collective-permute-start | bytes 368648 | tf_op jit(solution)/shard_map/ppermute | solution.py:708
  138.7 2.8 %collective-permute-start.19 = (bf16[96,384]{1,0:T(8,128)(2,1)}, bf16[96,384]{1,0:T(8,128)(2,1)S(1)}, u32[]{:S(2)}, u32[]{:S(2)}) collective-permute-start(bf16[96,384]{1,0:T(8,128)(2,1)} %bitcast.119), channel_id=1, source_target_pairs={{0,4},{1,5},{2,6},{3,7},{4,0},{5,1},{6,2},{7,3},{8,12},{9,13},{10,... | collective-permute-start | bytes 221192 | tf_op jit(solution)/shard_map/ppermute | solution.py:708
  141.6 2.9 %shard_map.331.refs_6_ = bf16[180,2,768]{2,1,0:T(2,128)(2,1)} custom-call(f32[2,180,768]{2,1,0:T(8,128)S(1)} %get-tuple-element.75.refs_2_.refs_0_, f32[2,192,768]{2,1,0:T(8,128)} %bitcast.95, bf16[2,192,768]{2,1,0:T(8,128)(2,1)S(1)} %bitcast.85, f32[768]{0:T(1024)} %refs_3_.1, bf16[8,2,96,128]{3,2,1,0:T(8,128)(2,1)} %get-tuple-element.82.refs_4_.refs_7_), custom_call_target="tpu_custom_call" | custom-call | bytes 3431424 | tf_op jit(solution)/shard_map/pallas_call | solution.py:681
  144.5 4.0 %shard_map.339.refs_7_ = f32[2,180,1,768]{3,2,1,0:T(1,128)} custom-call(s32[2,1,2]{2,1,0:T(1,128)S(1)} %copy-done.2, s32[1]{0:T(128)} %bitcast.refs_1_, bf16[8,2,96,128]{3,2,1,0:T(8,128)(2,1)S(1)} %bitcast.81, bf16[2,180,768]{2,1,0:T(8,128)(2,1)S(1)} %bitcast.79, f32[2,180,768]{2,1,0:T(8,128)} %get-tuple-element.93.refs_4_, s32[2,1,180]{2,1,0:T(1,128)} %bitcast.110, ...), custom_call_target="tpu_custom_call" | custom-call | flops 70778880 | bytes 3208628 | tf_op jit(solution)/shard_map/pallas_call | solution.py:681
  150.6 4.2 %collective-permute-done.19.refs_5_ = bf16[96,384]{1,0:T(8,128)(2,1)S(1)} collective-permute-done((bf16[96,384]{1,0:T(8,128)(2,1)}, bf16[96,384]{1,0:T(8,128)(2,1)S(1)}, u32[]{:S(2)}, u32[]{:S(2)}) %collective-permute-start.19) | collective-permute-done | bytes 73760 | tf_op jit(solution)/shard_map/ppermute | solution.py:708
  (89 shorter events, 38.6 us)
Async XLA Ops:
  5.2 19.0 %all-to-all-start = ((bf16[8,192,128]{2,1,0:T(8,128)(2,1)}), bf16[8,192,128]{2,1,0:T(8,128)(2,1)S(1)}, u32[]{:S(2)}, u32[]{:S(2)}) async-start(bf16[8,192,128]{2,1,0:T(8,128)(2,1)} %bitcast.3), calls=%async_computation | async-start | bytes 786432 | tf_op jit(solution)/shard_map/all_to_all | solution.py:770
  28.7 15.2 %all-to-all-start.1 = ((bf16[8,192,128]{2,1,0:T(8,128)(2,1)}), bf16[8,192,128]{2,1,0:T(8,128)(2,1)S(1)}, u32[]{:S(2)}, u32[]{:S(2)}) async-start(bf16[8,192,128]{2,1,0:T(8,128)(2,1)} %bitcast.9), calls=%async_computation.1 | async-start | bytes 786432 | tf_op jit(solution)/shard_map/all_to_all | solution.py:773
  32.5 14.4 %collective-permute-start.1 = (bf16[384,768]{1,0:T(8,128)(2,1)S(1)}, bf16[384,768]{1,0:T(8,128)(2,1)}, u32[]{:S(2)}, u32[]{:S(2)}) collective-permute-start(bf16[384,768]{1,0:T(8,128)(2,1)S(1)} %bitcast.91), channel_id=1, source_target_pairs={{0,8},{8,0},{16,24},{24,16},{1,9},{9,1},{17,25},{25,17},{2,10},{10... | collective-permute-start | bytes 1769480 | tf_op jit(solution)/shard_map/ppermute | solution.py:708
  46.7 2.2 %collective-permute-start = (bf16[384,768]{1,0:T(8,128)(2,1)S(1)}, bf16[384,768]{1,0:T(8,128)(2,1)}, u32[]{:S(2)}, u32[]{:S(2)}) collective-permute-start(bf16[384,768]{1,0:T(8,128)(2,1)S(1)} %bitcast.89), channel_id=1, source_target_pairs={{0,8},{8,0},{16,24},{24,16},{1,9},{9,1},{17,25},{25,17},{2,10},{10... | collective-permute-start | bytes 1769480 | tf_op jit(solution)/shard_map/ppermute | solution.py:708
  67.4 24.9 %collective-permute-start.5 = (bf16[768,640]{1,0:T(8,128)(2,1)}, bf16[768,640]{1,0:T(8,128)(2,1)S(1)}, u32[]{:S(2)}, u32[]{:S(2)}) collective-permute-start(bf16[768,640]{1,0:T(8,128)(2,1)} %get-tuple-element.86), channel_id=1, source_target_pairs={{0,16},{8,24},{16,0},{24,8},{1,17},{9,25},{17,1},{25,9},{2,18},{10... | collective-permute-start | bytes 2949128 | tf_op jit(solution)/shard_map/ppermute | solution.py:708
  69.0 23.3 %collective-permute-start.6 = (bf16[768,512]{1,0:T(8,128)(2,1)}, bf16[768,512]{1,0:T(8,128)(2,1)}, u32[]{:S(2)}, u32[]{:S(2)}) collective-permute-start(bf16[768,512]{1,0:T(8,128)(2,1)} %get-tuple-element.88), channel_id=1, source_target_pairs={{0,1},{1,0},{2,3},{3,2},{4,5},{5,4},{6,7},{7,6},{8,9},{9,8},{10,11... | collective-permute-start | bytes 2359304 | tf_op jit(solution)/shard_map/ppermute | solution.py:708
  70.4 18.6 %collective-permute-start.7 = (bf16[768,384]{1,0:T(8,128)(2,1)}, bf16[768,384]{1,0:T(8,128)(2,1)}, u32[]{:S(2)}, u32[]{:S(2)}) collective-permute-start(bf16[768,384]{1,0:T(8,128)(2,1)} %get-tuple-element.90), channel_id=1, source_target_pairs={{0,2},{1,3},{2,0},{3,1},{4,6},{5,7},{6,4},{7,5},{8,10},{9,11},{10,... | collective-permute-start | bytes 1769480 | tf_op jit(solution)/shard_map/ppermute | solution.py:708
  70.4 2.0 %collective-permute-start.4 = (bf16[384,384]{1,0:T(8,128)(2,1)S(1)}, bf16[384,384]{1,0:T(8,128)(2,1)S(1)}, u32[]{:S(2)}, u32[]{:S(2)}) collective-permute-start(bf16[384,384]{1,0:T(8,128)(2,1)S(1)} %get-tuple-element.81), channel_id=1, source_target_pairs={{0,8},{8,0},{16,24},{24,16},{1,9},{9,1},{17,25},{25,17},{2,10},{10... | collective-permute-start | bytes 884744 | tf_op jit(solution)/shard_map/ppermute | solution.py:708
  77.0 22.4 %all-to-all-start.2 = ((bf16[8,192,128]{2,1,0:T(8,128)(2,1)}), bf16[8,192,128]{2,1,0:T(8,128)(2,1)S(1)}, u32[]{:S(2)}, u32[]{:S(2)}) async-start(bf16[8,192,128]{2,1,0:T(8,128)(2,1)} %bitcast.27), calls=%async_computation.2 | async-start | bytes 786432 | tf_op jit(solution)/shard_map/all_to_all | solution.py:770
  97.1 13.5 %collective-permute-start.10 = (bf16[384,640]{1,0:T(8,128)(2,1)}, bf16[384,640]{1,0:T(8,128)(2,1)S(1)}, u32[]{:S(2)}, u32[]{:S(2)}) collective-permute-start(bf16[384,640]{1,0:T(8,128)(2,1)} %bitcast.97), channel_id=1, source_target_pairs={{0,1},{1,0},{2,3},{3,2},{4,5},{5,4},{6,7},{7,6},{8,9},{9,8},{10,11... | collective-permute-start | bytes 1474568 | tf_op jit(solution)/shard_map/ppermute | solution.py:708
  98.1 12.5 %collective-permute-start.11 = (bf16[384,512]{1,0:T(8,128)(2,1)}, bf16[384,512]{1,0:T(8,128)(2,1)S(1)}, u32[]{:S(2)}, u32[]{:S(2)}) collective-permute-start(bf16[384,512]{1,0:T(8,128)(2,1)} %bitcast.114), channel_id=1, source_target_pairs={{0,2},{1,3},{2,0},{3,1},{4,6},{5,7},{6,4},{7,5},{8,10},{9,11},{10,... | collective-permute-start | bytes 1179656 | tf_op jit(solution)/shard_map/ppermute | solution.py:708
  98.3 8.7 %collective-permute-start.8 = (bf16[384,384]{1,0:T(8,128)(2,1)}, bf16[384,384]{1,0:T(8,128)(2,1)S(1)}, u32[]{:S(2)}, u32[]{:S(2)}) collective-permute-start(bf16[384,384]{1,0:T(8,128)(2,1)} %bitcast.115), channel_id=1, source_target_pairs={{0,16},{8,24},{16,0},{24,8},{1,17},{9,25},{17,1},{25,9},{2,18},{10... | collective-permute-start | bytes 884744 | tf_op jit(solution)/shard_map/ppermute | solution.py:708
  103.3 21.1 %all-to-all-start.3 = ((bf16[8,192,128]{2,1,0:T(8,128)(2,1)}), bf16[8,192,128]{2,1,0:T(8,128)(2,1)S(1)}, u32[]{:S(2)}, u32[]{:S(2)}) async-start(bf16[8,192,128]{2,1,0:T(8,128)(2,1)} %bitcast.36), calls=%async_computation.3 | async-start | bytes 786432 | tf_op jit(solution)/shard_map/all_to_all | solution.py:773
  114.5 9.9 %collective-permute-start.13 = (bf16[192,640]{1,0:T(8,128)(2,1)}, bf16[192,640]{1,0:T(8,128)(2,1)S(1)}, u32[]{:S(2)}, u32[]{:S(2)}) collective-permute-start(bf16[192,640]{1,0:T(8,128)(2,1)} %bitcast.101), channel_id=1, source_target_pairs={{0,2},{1,3},{2,0},{3,1},{4,6},{5,7},{6,4},{7,5},{8,10},{9,11},{10,... | collective-permute-start | bytes 737288 | tf_op jit(solution)/shard_map/ppermute | solution.py:708
  116.6 7.8 %collective-permute-start.14 = (bf16[192,512]{1,0:T(8,128)(2,1)}, bf16[192,512]{1,0:T(8,128)(2,1)S(1)}, u32[]{:S(2)}, u32[]{:S(2)}) collective-permute-start(bf16[192,512]{1,0:T(8,128)(2,1)} %bitcast.116), channel_id=1, source_target_pairs={{0,16},{8,24},{16,0},{24,8},{1,17},{9,25},{17,1},{25,9},{2,18},{10... | collective-permute-start | bytes 589832 | tf_op jit(solution)/shard_map/ppermute | solution.py:708
  117.8 6.6 %collective-permute-start.15 = (bf16[192,384]{1,0:T(8,128)(2,1)}, bf16[192,384]{1,0:T(8,128)(2,1)}, u32[]{:S(2)}, u32[]{:S(2)}) collective-permute-start(bf16[192,384]{1,0:T(8,128)(2,1)} %bitcast.117), channel_id=1, source_target_pairs={{0,1},{1,0},{2,3},{3,2},{4,5},{5,4},{6,7},{7,6},{8,9},{9,8},{10,11... | collective-permute-start | bytes 442376 | tf_op jit(solution)/shard_map/ppermute | solution.py:708
  119.8 4.2 %collective-permute-start.12 = (f32[96,128]{1,0:T(8,128)S(1)}, f32[96,128]{1,0:T(8,128)S(1)}, u32[]{:S(2)}, u32[]{:S(2)}) collective-permute-start(f32[96,128]{1,0:T(8,128)S(1)} %get-tuple-element.110), channel_id=1, source_target_pairs={{0,16},{8,24},{16,0},{24,8},{1,17},{9,25},{17,1},{25,9},{2,18},{10... | collective-permute-start | bytes 147464 | tf_op jit(solution)/shard_map/ppermute | solution.py:708
  120.7 20.9 %collective-permute-start.2 = (bf16[384,768]{1,0:T(8,128)(2,1)}, bf16[384,768]{1,0:T(8,128)(2,1)S(1)}, u32[]{:S(2)}, u32[]{:S(2)}) collective-permute-start(bf16[384,768]{1,0:T(8,128)(2,1)} %get-tuple-element.78), channel_id=1, source_target_pairs={{0,8},{8,0},{16,24},{24,16},{1,9},{9,1},{17,25},{25,17},{2,10},{10... | collective-permute-start | bytes 1769480 | tf_op jit(solution)/shard_map/ppermute | solution.py:708
  128.5 21.3 %all-to-all-start.4 = ((bf16[8,136,128]{2,1,0:T(8,128)(2,1)}), bf16[8,136,128]{2,1,0:T(8,128)(2,1)S(1)}, u32[]{:S(2)}, u32[]{:S(2)}) async-start(bf16[8,136,128]{2,1,0:T(8,128)(2,1)} %shard_map.338.refs_8_.refs_7_), calls=%async_computation.4 | async-start | bytes 557056 | tf_op jit(solution)/shard_map/all_to_all | solution.py:1021
  135.7 19.1 %collective-permute-start.17 = (bf16[96,640]{1,0:T(8,128)(2,1)}, bf16[96,640]{1,0:T(8,128)(2,1)S(1)}, u32[]{:S(2)}, u32[]{:S(2)}) collective-permute-start(bf16[96,640]{1,0:T(8,128)(2,1)} %bitcast.104), channel_id=1, source_target_pairs={{0,4},{1,5},{2,6},{3,7},{4,0},{5,1},{6,2},{7,3},{8,12},{9,13},{10,... | collective-permute-start | bytes 368648 | tf_op jit(solution)/shard_map/ppermute | solution.py:708
  138.7 16.1 %collective-permute-start.18 = (bf16[96,512]{1,0:T(8,128)(2,1)}, bf16[96,512]{1,0:T(8,128)(2,1)S(1)}, u32[]{:S(2)}, u32[]{:S(2)}) collective-permute-start(bf16[96,512]{1,0:T(8,128)(2,1)} %bitcast.118), channel_id=1, source_target_pairs={{0,4},{1,5},{2,6},{3,7},{4,0},{5,1},{6,2},{7,3},{8,12},{9,13},{10,... | collective-permute-start | bytes 294920 | tf_op jit(solution)/shard_map/ppermute | solution.py:708
  138.7 16.1 %collective-permute-start.19 = (bf16[96,384]{1,0:T(8,128)(2,1)}, bf16[96,384]{1,0:T(8,128)(2,1)S(1)}, u32[]{:S(2)}, u32[]{:S(2)}) collective-permute-start(bf16[96,384]{1,0:T(8,128)(2,1)} %bitcast.119), channel_id=1, source_target_pairs={{0,4},{1,5},{2,6},{3,7},{4,0},{5,1},{6,2},{7,3},{8,12},{9,13},{10,... | collective-permute-start | bytes 221192 | tf_op jit(solution)/shard_map/ppermute | solution.py:708
  149.8 7.7 %collective-permute-start.16 = (bf16[656,128]{1,0:T(8,128)(2,1)S(1)}, bf16[656,128]{1,0:T(8,128)(2,1)S(1)}, u32[]{:S(2)}, u32[]{:S(2)}) collective-permute-start(bf16[656,128]{1,0:T(8,128)(2,1)S(1)} %shard_map.341.refs_0_.refs_1_), channel_id=1, source_target_pairs={{0,16},{8,24},{16,0},{24,8},{1,17},{9,25},{17,1},{25,9},{2,18},{10... | collective-permute-start | bytes 503816 | tf_op jit(solution)/shard_map/ppermute | solution.py:708
  157.6 1.7 %collective-permute-start.20 = (bf16[1312,128]{1,0:T(8,128)(2,1)S(1)}, bf16[1312,128]{1,0:T(8,128)(2,1)S(1)}, u32[]{:S(2)}, u32[]{:S(2)}) collective-permute-start(bf16[1312,128]{1,0:T(8,128)(2,1)S(1)} %shard_map.343), channel_id=1, source_target_pairs={{0,8},{8,0},{16,24},{24,16},{1,9},{9,1},{17,25},{25,17},{2,10},{10... | collective-permute-start | bytes 1007624 | tf_op jit(solution)/shard_map/ppermute | solution.py:708
  (17 other events, 75.4 us)

commit v3 on v2

--- a/solution.py
+++ b/solution.py
@@ -241,7 +241,7 @@
     *refs,
 ):
     far_refs, refs = refs[:6], refs[6:]
-    bias_grad, out_own, grad_own, out_other_ref, grad_0_ref, grad_1_ref, *refs = refs
+    bias_grad, out_own, grad_own, out_other_ref, grad_other_ref, *refs = refs
     post_ref, cot_ref, expand_ref, reduce_ref, hidden_ref, grad_ref, *refs = refs
     expand_grad_ref, reduce_grad_ref, row_sems, weight_sems, far_sems = refs
     rows = post_own.shape[0]
@@ -304,16 +304,13 @@
                     copies[-1].start()
             to_lanes += lanes
 
-    out = dot(hidden_ref[...], reduce_ref[...], 1, 0)
-    out_own.here[...] = out[:rows]
-    out_own.start()
-    out_other_ref[...] = out[rows:].astype(bf16)
     back = dot(grad_ref[...], expand_ref[...], 1, 1)
-    half = back.shape[1] // 2
     grad_own.here[...] = back[:rows]
     grad_own.start()
-    grad_0_ref[...] = back[rows:, :half].astype(bf16)
-    grad_1_ref[...] = back[rows:, half:].astype(bf16)
+    grad_other_ref[...] = back[rows:].astype(bf16)
+    out_own.here[...] = dot(hidden_ref[:rows], reduce_ref[...], 1, 0)
+    out_own.start()
+    out_other_ref[...] = dot(hidden_ref[rows:], reduce_ref[...], 1, 0).astype(bf16)
     for copy in copies:
         copy.wait()
 
@@ -344,10 +341,6 @@
             begin += lanes
 
 
-def both_halves(first_ref, second_ref, item, cells):
-    return jnp.concatenate([first_ref[item, :cells], second_ref[item, :cells]], axis=1).astype(f32)
-
-
 def result_kernel(mixed_ref, out_own_ref, out_other_ref, bias_ref, result_ref):
     cells, items, _ = result_ref.shape
     for item in range(items):
@@ -358,25 +351,27 @@
 
 def post_kernel(
     lat_rows, block_size, sub,
-    box_ref, row_ref, mixed_ref, grad_own_ref, grad_0_ref, grad_1_ref, cot_ref, hole_ref, gain_ref, table_ref,
+    box_ref, row_ref, mixed_ref, grad_own_ref, grad_other_ref, cot_ref, hole_ref, gain_ref, table_ref,
     grad_mixed, send_ref, sum_ref, mixed_grad_ref, sems,
 ):
     items, cells, _ = mixed_grad_ref.shape
     sums = 0.0
-    copies = []
+    copies, rounded = [], []
     parts = [norm_parts(mixed_ref[item]) for item in range(items)]
     for item in range(items):
         unit, inv_scale = parts[item]
-        grad = grad_own_ref[item, :cells] + both_halves(grad_0_ref, grad_1_ref, item, cells)
+        grad = grad_own_ref[item, :cells] + grad_other_ref[item, :cells].astype(f32)
         cot = cot_ref[item, :cells].astype(f32)
         sums += jnp.concatenate([jnp.sum(v, axis=0, keepdims=True) for v in (grad * unit, grad, cot)], axis=0)
         value = cot + norm_back(grad, unit, inv_scale, line(gain_ref))
         mixed_grad_ref[item] = value
         copies.append(pltpu.make_async_copy(mixed_grad_ref.at[item], grad_mixed.at[item], sems.at[item]))
         copies[-1].start()
+        rounded.append(value.astype(bf16))
+    for item in range(items):
         valid = valid_row(item, box_ref, row_ref, hole_ref, lat_rows, cells)
         table = (table_ref[...].astype(f32) * valid).astype(bf16)
-        put_modes(send_ref, item, dot(table, value.astype(bf16), 1, 0), block_size, sub)
+        put_modes(send_ref, item, dot(table, rounded[item], 1, 0), block_size, sub)
     sum_ref[...] = sums
     for copy in copies:
         copy.wait()
@@ -488,8 +483,8 @@
     total = own_ref[...] + other_ref[...]
     value_ref = tail.here.at[0]
     value_ref[:base] = total[:base].astype(bf16)
-    put_split(value_ref, base, total[base:])
-    per_line, at = width // 128, base + 2 * rows
+    value_ref[base : base + rows] = total[base:].astype(bf16)
+    per_line, at = width // 128, base + rows
     value_ref[at:] = jnp.zeros((value_ref.shape[0] - at, 128), bf16)
     for i in range(2):
         for j in range(per_line):
@@ -532,18 +527,16 @@
     return ref[at : at + rows].astype(f32) + ref[at + rows : at + 2 * rows].astype(f32)
 
 
-def third_kernel(sub, rows, pre_rows, recv_ref, *refs):
+def third_kernel(sub, base, rows, pre_rows, recv_ref, *refs):
     *other_refs, out_ref = refs
-    groups, total_rows, _ = recv_ref.shape
-    base = total_rows - 2 * rows - pre_rows
-    blocks = groups // sub
+    blocks = recv_ref.shape[0] // sub
     total = 0.0
     for block in range(blocks):
         part = recv_ref[block * sub]
         out_ref[block * base : (block + 1) * base] = part[:base]
-        total += part[base : base + rows].astype(f32) + part[base + rows : base + 2 * rows].astype(f32)
+        total += part[base : base + rows].astype(f32)
     put_split(out_ref, blocks * base, total)
-    total = jnp.sum(recv_ref[:, base + 2 * rows :].astype(f32), axis=0)
+    total = jnp.sum(recv_ref[:, base + rows : base + rows + pre_rows].astype(f32), axis=0)
     for ref in other_refs:
         total += jnp.sum(ref[...].astype(f32), axis=0)
     put_split(out_ref, blocks * base + 2 * rows, total)
@@ -643,7 +636,7 @@
         return self.here[index]
 
 
-def call(kernel, out_shape, args, prefetch=0, scratch=(), flops=0, vmem=16, after=(), far_in=(), far_out=(), raw=()):
+def call(kernel, out_shape, args, prefetch=0, scratch=(), flops=0, vmem=16, after=(), far_in=(), far_out=(), raw=(), loose=()):
     args, after = tuple(args), tuple(after)
     far_out = [len(args) + i for i in far_out]
     raw = set(i if i >= 0 else len(args) - 1 - i for i in raw)
@@ -671,7 +664,7 @@
             value.wait()
 
     moved = sum(math.prod(a.shape) * np.dtype(a.dtype).itemsize for a in every)
-    fixed = [pltpu.with_memory_space_constraint(a, pltpu.HBM) if i in far else a for i, a in enumerate(args)]
+    fixed = [pltpu.with_memory_space_constraint(a, pltpu.HBM) if i in far and i not in loose else a for i, a in enumerate(args)]
     shapes = [
         pltpu.HBM(a.shape, a.dtype) if i in far_out or i in raw else a for i, a in enumerate(out_shape, len(args))
     ]
@@ -750,7 +743,7 @@
     own_block = lat_index // sub
     tables = {k: jnp.asarray(v) for k, v in make_tables(cells, lat_count, block_size, chunk).items()}
 
-    box = boxes
+    box = stay(boxes)
     own_row = (lat_index * lat_rows).astype(jnp.int32).reshape(1)
     core = dp_index % 2
     token_items = tokens.reshape(items, cells, width)
@@ -856,14 +849,13 @@
     cuts = [place_of(order[0], left) for order, left in zip(orders, lefts)]
     copy_count = sum(4 * outer for _, outer in cuts)
     args = (
-        own_bits, core_bit, post, post_other, cot_pad.reshape(rows, width), cot_other,
+        own_bits, core_bit, post, post_other, stay(cot_pad.reshape(rows, width)), cot_other,
         stay(expand_weight), stay(reduce_weight), expand_bias.reshape(1, hidden_width),
     )
-    *parts, grad_b, out_own, grad_own, out_other, grad_0, grad_1 = call(
+    *parts, grad_b, out_own, grad_own, out_other, grad_other = call(
         functools.partial(feed_kernel, cuts, shares, runs, run),
         [shape((half // 2, n), bf16) for n in lanes for _ in range(2)]
-        + [shape((1, half), f32), shape(flat, f32), shape(flat, f32), shape(flat, bf16)]
-        + [shape((rows, width // 2), bf16)] * 2,
+        + [shape((1, half), f32), shape(flat, f32), shape(flat, f32), shape(flat, bf16), shape(flat, bf16)],
         args,
         prefetch=2,
         far_in=(8,),
@@ -878,7 +870,7 @@
         flops=6 * 2 * 2 * rows * width * half,
         vmem=52,
     )
-    others = [pair_swap(v, "dp", 1).reshape(items, padded, width // 2) for v in (grad_0, grad_1)]
+    grad_other = pair_swap(grad_other, "dp", 1).reshape(pad_item)
     out_other = pair_swap(out_other, "dp", 1).reshape(pad_item)
 
     class Scatter:
@@ -904,6 +896,7 @@
                 (own_bits, *ins),
                 prefetch=1,
                 far_in=range(1, 7),
+                loose=(2, 4, 6),
                 far_out=range(6),
                 after=after,
                 flops=flops,
@@ -916,14 +909,14 @@
     scatter.swap()
 
     args = (
-        box, own_row, mixed, grad_own.reshape(pad_item), *others, cot_pad, holes, post_gain, tables["inv"],
+        box, own_row, mixed, grad_own.reshape(pad_item), grad_other, cot_pad, holes, post_gain, tables["inv"],
     )
     grad_mixed, send, post_sums = call(
         functools.partial(post_kernel, *names),
         [shape(row_item, f32), shape(mode_dims, bf16), shape((3, width), f32)],
         args,
         prefetch=2,
-        far_in=(3, 6, 8, 9, 7),
+        far_in=(3, 5, 7, 8, 6),
         raw=(-1,),
         scratch=[pltpu.VMEM(row_item, f32), pltpu.SemaphoreType.DMA((items,))],
         flops=lon_flops,
@@ -974,7 +967,7 @@
         prefetch=1,
         far_in=(1, 4, 2, 3),
         scratch=[pltpu.VMEM(small_dims, f32)],
-        after=[stay(scatter.recvs[2])],
+        after=(scatter.recvs[2],),
     )
     weight = [keep_core, pair_swap(send_core, "dp", 1)]
     sums = scatter.add((send, keep_core), flops=COMBINE_FLOPS)
@@ -994,7 +987,7 @@
         weight = [weight[0] + weight[1]]
         weight.append(pair_swap(weight[0], *step))
     pre_rows = -(-2 * width // 2048) * 16
-    tail_dims = (groups, own_base + 2 * own_small + pre_rows, 128)
+    tail_dims = (groups, -(-(own_base + own_small + pre_rows) // 16) * 16, 128)
     (tail_send,) = call(
         functools.partial(last_sums_kernel, *names, own_base),
         [shape(tail_dims, bf16)],
@@ -1003,7 +996,7 @@
         far_in=(6, 5, 4),
         far_out=(0,),
         flops=lon_flops,
-        after=[stay(v) for v in ahead],
+        after=ahead,
     )
     result_dims = (items, cells, 1, width)
     (grad_tokens,) = call(
@@ -1029,16 +1022,17 @@
         [shape((own_rows, width), f32)] * 2,
         merged,
         far_in=range(6),
+        loose=(1, 3, 5),
                 flops=COMBINE_FLOPS,
         after=(result, stay(grad_tokens), tail),
     )
     expand_part = expand_part.T
     extra = [n[1] for n in dp_bits[1:]]
     masks = [sum(b for i, b in enumerate(extra) if m >> i & 1) for m in range(1, 2 ** len(extra))]
-    others = [pair_swap(tail[:, own_base + 2 * own_small :], "dp", m) for m in masks]
+    others = [pair_swap(tail[:, own_base + own_small : own_base + own_small + pre_rows], "dp", m) for m in masks]
     third_dims = (block_count * own_base + 2 * own_small + 2 * pre_rows, 128)
     (third,) = call(
-        functools.partial(third_kernel, sub, own_small, pre_rows),
+        functools.partial(third_kernel, sub, own_base, own_small, pre_rows),
         [shape(third_dims, bf16)],
         (tail, *others),
         after=(stay(sums[0]),),

time: 163 us -> 157 us (0.963)
  local copies, waits for them, and re-layouts: 7.61 us -> 2.95 us
  waiting for transfers between devices: 46.1 us -> 44 us
    unnamed x32 -> x10, local copies, waits for them, and re-layouts: 5.85 us -> 1.19 us
    ppermute x21 -> x20, waiting for transfers between devices: 24.5 us -> 23.6 us  [pair_swap(): return lax.ppermute(operand, axis_name, [(i, i ^ bit) for i in range(size)])]
    ppermute x21 -> x20, starting transfers between devices: 18.3 us -> 18.7 us  [pair_swap(): return lax.ppermute(operand, axis_name, [(i, i ^ bit) for i in range(size)])]
  transfers between devices with their start and end apart: 26 -> 25, of which waited for: 12 -> 11; matrix products, arithmetic and copies ran while one was open for 2% -> 2% of each run, Pallas kernels for 22% -> 24%
where the time goes in v3:
time: 157 us; the launch traced here: 156 us
  Pallas kernels  65.5 us (42%)
  waiting for transfers between devices  44 us (28%)
  starting transfers between devices  41.6 us (26%)
  local copies, waits for them, and re-layouts  2.95 us (2%)
    pallas_call x19, Pallas kernels, call(): pl.pallas_call(whole_kernel, out_shape=shapes, grid_spec=pltpu.PrefetchSc...  65.5 us
    ppermute x20, waiting for transfers between devices, pair_swap(): return lax.ppermute(operand, axis_name, [(i, i ^ bit) for i in range(size)])  23.6 us
    all_to_all x4, waiting for transfers between devices, exchange(): both = lax.all_to_all(both, 'lat', 0, 0, tiled=True)  20.4 us
    ppermute x20, starting transfers between devices, pair_swap(): return lax.ppermute(operand, axis_name, [(i, i ^ bit) for i in range(size)])  18.7 us
    all_to_all x4, starting transfers between devices, exchange(): both = lax.all_to_all(both, 'lat', 0, 0, tiled=True)  18.3 us
    all_to_all x1, starting transfers between devices, body(): tail = lax.all_to_all(tail, 'lat', 0, 0, tiled=True)  4.55 us
  transfers between devices with their start and end apart: 25, of which 11 were waited for; matrix products, arithmetic and copies ran while one was open for 2% of the time, Pallas kernels for 24%

profile of v3, /device:TPU:0, one launch (start us, length us, event | category | flops | bytes accessed | tf_op | source)
XLA Modules:
  0.0 156.2 jit_solution(1348195187037500551)
XLA Ops:
  1.8 2.9 %shard_map.326 = bf16[8,2,96,128]{3,2,1,0:T(8,128)(2,1)} custom-call(s32[2,1,2]{2,1,0:T(1,128)} %refs_0_.9, s32[1]{0:T(128)} %bitcast.refs_1_, bf16[2,180,768]{2,1,0:T(8,128)(2,1)S(1)} %bitcast.75, s32[2,1,180]{2,1,0:T(1,128)} %bitcast.107, f32[768]{0:T(1024)} %refs_6_.9, f32[768]{0:T(1024)} %refs_6_.7, bf16[128,180]{1,0:T(8,128)(2,1)} %constant.110.clone.refs_6_), custom_call_target="tpu_custom_call" | custom-call | flops 70778880 | bytes 999860 | tf_op jit(solution)/shard_map/pallas_call | solution.py:674
  4.7 7.3 %all-to-all-start = ((bf16[8,192,128]{2,1,0:T(8,128)(2,1)}), bf16[8,192,128]{2,1,0:T(8,128)(2,1)S(1)}, u32[]{:S(2)}, u32[]{:S(2)}) async-start(bf16[8,192,128]{2,1,0:T(8,128)(2,1)} %bitcast.3), calls=%async_computation | async-start | bytes 786432 | tf_op jit(solution)/shard_map/all_to_all | solution.py:763
  14.7 9.0 %all-to-all-done = bf16[8,192,128]{2,1,0:T(8,128)(2,1)S(1)} async-done(((bf16[8,192,128]{2,1,0:T(8,128)(2,1)}), bf16[8,192,128]{2,1,0:T(8,128)(2,1)S(1)}, u32[]{:S(2)}, u32[]{:S(2)}) %all-to-all-start) | async-done | bytes 393248 | tf_op jit(solution)/shard_map/all_to_all | solution.py:763
  23.6 4.6 %shard_map.327 = (bf16[8,2,96,128]{3,2,1,0:T(8,128)(2,1)}, bf16[8,128,192]{2,1,0:T(8,128)(2,1)}, bf16[8,128,192]{2,1,0:T(8,128)(2,1)}, f32[8,128,192]{2,1,0:T(8,128)}, f32[8,128,192]{2,1,0:T(8,128)}) custom-call(bf16[8,2,96,128]{3,2,1,0:T(8,128)(2,1)S(1)} %bitcast.81, bf16[192,192]{1,0:T(8,128)(2,1)S(1)} %maximum_maximum_fusion.refs_1_.refs_3_, ...), custom_call_target="tpu_custom_call" | custom-call | flops 150994944 | bytes 3499520 | tf_op jit(solution)/shard_map/pallas_call | solution.py:674
  28.2 3.6 %all-to-all-start.1 = ((bf16[8,192,128]{2,1,0:T(8,128)(2,1)}), bf16[8,192,128]{2,1,0:T(8,128)(2,1)S(1)}, u32[]{:S(2)}, u32[]{:S(2)}) async-start(bf16[8,192,128]{2,1,0:T(8,128)(2,1)} %bitcast.9), calls=%async_computation.1 | async-start | bytes 786432 | tf_op jit(solution)/shard_map/all_to_all | solution.py:766
  32.0 11.4 %all-to-all-done.1 = bf16[8,192,128]{2,1,0:T(8,128)(2,1)S(1)} async-done(((bf16[8,192,128]{2,1,0:T(8,128)(2,1)}), bf16[8,192,128]{2,1,0:T(8,128)(2,1)S(1)}, u32[]{:S(2)}, u32[]{:S(2)}) %all-to-all-start.1) | async-done | bytes 393248 | tf_op jit(solution)/shard_map/all_to_all | solution.py:766
  43.4 2.9 %shard_map.328 = (f32[2,180,768]{2,1,0:T(8,128)S(1)}, bf16[2,192,768]{2,1,0:T(8,128)(2,1)S(1)}) custom-call(s32[2,1,2]{2,1,0:T(1,128)} %refs_0_.9, s32[1]{0:T(128)} %bitcast.refs_1_, bf16[8,2,96,128]{3,2,1,0:T(8,128)(2,1)S(1)} %bitcast.82, bf16[2,180,768]{2,1,0:T(8,128)(2,1)S(1)} %bitcast.76, s32[2,1,180]{2,1,0:T(1,128)} %bitcast.108, f32[768]{0:T(1024)} %refs_6_.9, ...), custom_call_target="tpu_custom_call" | custom-call | flops 70778880 | bytes 2701748 | tf_op jit(solution)/shard_map/pallas_call | solution.py:674
  48.5 18.4 %shard_map.329 = (bf16[768,640]{1,0:T(8,128)(2,1)}, bf16[768,640]{1,0:T(8,128)(2,1)}, bf16[768,512]{1,0:T(8,128)(2,1)}, bf16[768,512]{1,0:T(8,128)(2,1)}, bf16[7...) custom-call(s32[4]{0:T(128)S(1)} %pad_add_fusion.refs_0_, ...), custom_call_target="tpu_custom_call" | custom-call | flops 10871635968 | bytes 20072468 | tf_op jit(solution)/shard_map/pallas_call | solution.py:674
  71.9 4.7 %shard_map.330 = (f32[2,180,768]{2,1,0:T(8,128)}, bf16[8,2,96,128]{3,2,1,0:T(8,128)(2,1)}, f32[3,768]{1,0:T(4,128)S(1)}) custom-call(s32[2,1,2]{2,1,0:T(1,128)} %refs_0_.9, s32[1]{0:T(128)} %bitcast.refs_1_, f32[2,180,768]{2,1,0:T(8,128)S(1)} %get-tuple-element.74.refs_2_.refs_0_, f32[2,192,768]{2,1,0:T(8,128)} %bitcast.98, ...), custom_call_target="tpu_custom_call" | custom-call | flops 70778880 | bytes 5024180 | tf_op jit(solution)/shard_map/pallas_call | solution.py:674
  76.6 3.7 %all-to-all-start.2 = ((bf16[8,192,128]{2,1,0:T(8,128)(2,1)}), bf16[8,192,128]{2,1,0:T(8,128)(2,1)S(1)}, u32[]{:S(2)}, u32[]{:S(2)}) async-start(bf16[8,192,128]{2,1,0:T(8,128)(2,1)} %bitcast.26), calls=%async_computation.2 | async-start | bytes 786432 | tf_op jit(solution)/shard_map/all_to_all | solution.py:763
  80.3 10.0 %collective-permute-done.6 = bf16[768,384]{1,0:T(8,128)(2,1)} collective-permute-done((bf16[768,384]{1,0:T(8,128)(2,1)}, bf16[768,384]{1,0:T(8,128)(2,1)}, u32[]{:S(2)}, u32[]{:S(2)}) %collective-permute-start.6) | collective-permute-done | bytes 589856 | tf_op jit(solution)/shard_map/ppermute | solution.py:701
  91.1 3.6 %shard_map.332 = (bf16[4,96,640]{2,1,0:T(8,128)(2,1)}, bf16[4,96,640]{2,1,0:T(8,128)(2,1)}, bf16[4,96,512]{2,1,0:T(8,128)(2,1)}, bf16[4,96,512]{2,1,0:T(8,128)(2...) custom-call(s32[4]{0:T(128)S(1)} %pad_add_fusion.refs_0_, bf16[4,2,96,640]{3,2,1,0:T(8,128)(2,1)} %bitcast.119, ...), custom_call_target="tpu_custom_call" | custom-call | flops 20000000000 | bytes 7077904 | tf_op jit(solution)/shard_map/pallas_call | solution.py:674
  97.8 3.9 %shard_map.333 = (bf16[8,2,96,128]{3,2,1,0:T(8,128)(2,1)}, bf16[8,128,192]{2,1,0:T(8,128)(2,1)}, bf16[8,128,192]{2,1,0:T(8,128)(2,1)}, f32[2,192]{1,0:T(2,128)S(1)}) custom-call(bf16[8,2,96,128]{3,2,1,0:T(8,128)(2,1)S(1)} %bitcast.83, f32[8,128,192]{2,1,0:T(8,128)} %get-tuple-element.81.refs_1_, f32[8,128,192]{2,1,0:T(8,128)} %get-tuple-element.82.refs_2_, ...), custom_call_target="tpu_custom_call" | custom-call | flops 301989888 | bytes 3499520 | tf_op jit(solution)/shard_map/pallas_call | solution.py:674
  101.7 3.7 %all-to-all-start.3 = ((bf16[8,192,128]{2,1,0:T(8,128)(2,1)}), bf16[8,192,128]{2,1,0:T(8,128)(2,1)S(1)}, u32[]{:S(2)}, u32[]{:S(2)}) async-start(bf16[8,192,128]{2,1,0:T(8,128)(2,1)} %bitcast.35), calls=%async_computation.3 | async-start | bytes 786432 | tf_op jit(solution)/shard_map/all_to_all | solution.py:766
  108.3 3.0 %shard_map.336 = (bf16[2,96,640]{2,1,0:T(8,128)(2,1)}, bf16[2,96,640]{2,1,0:T(8,128)(2,1)}, bf16[1,192,512]{2,1,0:T(8,128)(2,1)}, bf16[1,192,512]{2,1,0:T(8,128)...) custom-call(s32[4]{0:T(128)S(1)} %pad_add_fusion.refs_0_, bf16[2,2,96,640]{3,2,1,0:T(8,128)(2,1)} %bitcast.122, ...), custom_call_target="tpu_custom_call" | custom-call | flops 20000000000 | bytes 3538960 | tf_op jit(solution)/shard_map/pallas_call | solution.py:674
  117.5 3.2 %collective-permute-done.11.refs_8_ = f32[96,128]{1,0:T(8,128)S(1)} collective-permute-done((f32[96,128]{1,0:T(8,128)S(1)}, f32[96,128]{1,0:T(8,128)S(1)}, u32[]{:S(2)}, u32[]{:S(2)}) %collective-permute-start.11) | collective-permute-done | bytes 49184 | tf_op jit(solution)/shard_map/ppermute | solution.py:701
  121.0 3.4 %shard_map.338.refs_8_.refs_7_ = bf16[8,112,128]{2,1,0:T(8,128)(2,1)} custom-call(s32[2,1,2]{2,1,0:T(1,128)} %refs_0_.9, s32[1]{0:T(128)} %bitcast.refs_1_, bf16[8,2,96,128]{3,2,1,0:T(8,128)(2,1)S(1)} %bitcast.79, bf16[2,180,768]{2,1,0:T(8,128)(2,1)S(1)} %bitcast.77, f32[2,180,768]{2,1,0:T(8,128)} %get-tuple-element.91.refs_4_, s32[2,1,180]{2,1,0:T(1,128)} %bitcast.110, ...), custom_call_target="tpu_custom_call" | custom-call | flops 70778880 | bytes 2427316 | tf_op jit(solution)/shard_map/pallas_call | solution.py:674
  124.4 4.5 %all-to-all-start.4 = ((bf16[8,112,128]{2,1,0:T(8,128)(2,1)}), bf16[8,112,128]{2,1,0:T(8,128)(2,1)S(1)}, u32[]{:S(2)}, u32[]{:S(2)}) async-start(bf16[8,112,128]{2,1,0:T(8,128)(2,1)} %shard_map.338.refs_8_.refs_7_), calls=%async_computation.4 | async-start | bytes 458752 | tf_op jit(solution)/shard_map/all_to_all | solution.py:1014
  129.0 2.9 %shard_map.340 = (bf16[1,96,640]{2,1,0:T(8,128)(2,1)}, bf16[1,96,640]{2,1,0:T(8,128)(2,1)}, bf16[1,96,512]{2,1,0:T(8,128)(2,1)}, bf16[1,96,512]{2,1,0:T(8,128)(2...) custom-call(s32[4]{0:T(128)S(1)} %pad_add_fusion.refs_0_, bf16[1,2,96,640]{3,2,1,0:T(8,128)(2,1)} %bitcast.126, ...), custom_call_target="tpu_custom_call" | custom-call | flops 20000000000 | bytes 1769488 | tf_op jit(solution)/shard_map/pallas_call | solution.py:674
  131.8 3.0 %collective-permute-start.16 = (bf16[96,640]{1,0:T(8,128)(2,1)}, bf16[96,640]{1,0:T(8,128)(2,1)S(1)}, u32[]{:S(2)}, u32[]{:S(2)}) collective-permute-start(bf16[96,640]{1,0:T(8,128)(2,1)} %bitcast.105), channel_id=1, source_target_pairs={{0,4},{1,5},{2,6},{3,7},{4,0},{5,1},{6,2},{7,3},{8,12},{9,13},{10,... | collective-permute-start | bytes 368648 | tf_op jit(solution)/shard_map/ppermute | solution.py:701
  134.9 2.8 %collective-permute-start.18 = (bf16[96,384]{1,0:T(8,128)(2,1)}, bf16[96,384]{1,0:T(8,128)(2,1)S(1)}, u32[]{:S(2)}, u32[]{:S(2)}) collective-permute-start(bf16[96,384]{1,0:T(8,128)(2,1)} %bitcast.117), channel_id=1, source_target_pairs={{0,4},{1,5},{2,6},{3,7},{4,0},{5,1},{6,2},{7,3},{8,12},{9,13},{10,... | collective-permute-start | bytes 221192 | tf_op jit(solution)/shard_map/ppermute | solution.py:701
  137.8 2.9 %shard_map.331.refs_6_ = bf16[180,2,768]{2,1,0:T(2,128)(2,1)} custom-call(f32[2,180,768]{2,1,0:T(8,128)S(1)} %get-tuple-element.74.refs_2_.refs_0_, f32[2,192,768]{2,1,0:T(8,128)} %bitcast.99, bf16[2,192,768]{2,1,0:T(8,128)(2,1)S(1)} %bitcast.85, f32[768]{0:T(1024)} %refs_3_.1, bf16[8,2,96,128]{3,2,1,0:T(8,128)(2,1)} %get-tuple-element.80.refs_4_.refs_7_), custom_call_target="tpu_custom_call" | custom-call | bytes 3431424 | tf_op jit(solution)/shard_map/pallas_call | solution.py:674
  140.7 4.2 %shard_map.339.refs_7_ = f32[2,180,1,768]{3,2,1,0:T(1,128)} custom-call(s32[2,1,2]{2,1,0:T(1,128)} %refs_0_.9, s32[1]{0:T(128)} %bitcast.refs_1_, bf16[8,2,96,128]{3,2,1,0:T(8,128)(2,1)S(1)} %bitcast.80, bf16[2,180,768]{2,1,0:T(8,128)(2,1)S(1)} %bitcast.78, f32[2,180,768]{2,1,0:T(8,128)} %get-tuple-element.91.refs_4_, s32[2,1,180]{2,1,0:T(1,128)} %bitcast.111, ...), custom_call_target="tpu_custom_call" | custom-call | flops 70778880 | bytes 3208628 | tf_op jit(solution)/shard_map/pallas_call | solution.py:674
  145.9 3.8 %collective-permute-done.18.refs_5_ = bf16[96,384]{1,0:T(8,128)(2,1)S(1)} collective-permute-done((bf16[96,384]{1,0:T(8,128)(2,1)}, bf16[96,384]{1,0:T(8,128)(2,1)S(1)}, u32[]{:S(2)}, u32[]{:S(2)}) %collective-permute-start.18) | collective-permute-done | bytes 73760 | tf_op jit(solution)/shard_map/ppermute | solution.py:701
  (65 shorter events, 31.8 us)
Async XLA Ops:
  4.7 19.0 %all-to-all-start = ((bf16[8,192,128]{2,1,0:T(8,128)(2,1)}), bf16[8,192,128]{2,1,0:T(8,128)(2,1)S(1)}, u32[]{:S(2)}, u32[]{:S(2)}) async-start(bf16[8,192,128]{2,1,0:T(8,128)(2,1)} %bitcast.3), calls=%async_computation | async-start | bytes 786432 | tf_op jit(solution)/shard_map/all_to_all | solution.py:763
  28.2 15.2 %all-to-all-start.1 = ((bf16[8,192,128]{2,1,0:T(8,128)(2,1)}), bf16[8,192,128]{2,1,0:T(8,128)(2,1)S(1)}, u32[]{:S(2)}, u32[]{:S(2)}) async-start(bf16[8,192,128]{2,1,0:T(8,128)(2,1)} %bitcast.9), calls=%async_computation.1 | async-start | bytes 786432 | tf_op jit(solution)/shard_map/all_to_all | solution.py:766
  32.0 14.6 %collective-permute-start.1 = (bf16[384,768]{1,0:T(8,128)(2,1)S(1)}, bf16[384,768]{1,0:T(8,128)(2,1)}, u32[]{:S(2)}, u32[]{:S(2)}) collective-permute-start(bf16[384,768]{1,0:T(8,128)(2,1)S(1)} %bitcast.95), channel_id=1, source_target_pairs={{0,8},{8,0},{16,24},{24,16},{1,9},{9,1},{17,25},{25,17},{2,10},{10... | collective-permute-start | bytes 1769480 | tf_op jit(solution)/shard_map/ppermute | solution.py:701
  46.3 2.2 %collective-permute-start = (bf16[384,768]{1,0:T(8,128)(2,1)S(1)}, bf16[384,768]{1,0:T(8,128)(2,1)}, u32[]{:S(2)}, u32[]{:S(2)}) collective-permute-start(bf16[384,768]{1,0:T(8,128)(2,1)S(1)} %bitcast.92), channel_id=1, source_target_pairs={{0,8},{8,0},{16,24},{24,16},{1,9},{9,1},{17,25},{25,17},{2,10},{10... | collective-permute-start | bytes 1769480 | tf_op jit(solution)/shard_map/ppermute | solution.py:701
  66.9 24.2 %collective-permute-start.4 = (bf16[768,640]{1,0:T(8,128)(2,1)}, bf16[768,640]{1,0:T(8,128)(2,1)}, u32[]{:S(2)}, u32[]{:S(2)}) collective-permute-start(bf16[768,640]{1,0:T(8,128)(2,1)} %get-tuple-element.84), channel_id=1, source_target_pairs={{0,16},{8,24},{16,0},{24,8},{1,17},{9,25},{17,1},{25,9},{2,18},{10... | collective-permute-start | bytes 2949128 | tf_op jit(solution)/shard_map/ppermute | solution.py:701
  68.5 22.3 %collective-permute-start.5 = (bf16[768,512]{1,0:T(8,128)(2,1)}, bf16[768,512]{1,0:T(8,128)(2,1)S(1)}, u32[]{:S(2)}, u32[]{:S(2)}) collective-permute-start(bf16[768,512]{1,0:T(8,128)(2,1)} %get-tuple-element.86), channel_id=1, source_target_pairs={{0,1},{1,0},{2,3},{3,2},{4,5},{5,4},{6,7},{7,6},{8,9},{9,8},{10,11... | collective-permute-start | bytes 2359304 | tf_op jit(solution)/shard_map/ppermute | solution.py:701
  69.9 2.0 %collective-permute-start.3 = (bf16[384,768]{1,0:T(8,128)(2,1)S(1)}, bf16[384,768]{1,0:T(8,128)(2,1)S(1)}, u32[]{:S(2)}, u32[]{:S(2)}) collective-permute-start(bf16[384,768]{1,0:T(8,128)(2,1)S(1)} %get-tuple-element.79), channel_id=1, source_target_pairs={{0,8},{8,0},{16,24},{24,16},{1,9},{9,1},{17,25},{25,17},{2,10},{10... | collective-permute-start | bytes 1769480 | tf_op jit(solution)/shard_map/ppermute | solution.py:701
  69.9 20.4 %collective-permute-start.6 = (bf16[768,384]{1,0:T(8,128)(2,1)}, bf16[768,384]{1,0:T(8,128)(2,1)}, u32[]{:S(2)}, u32[]{:S(2)}) collective-permute-start(bf16[768,384]{1,0:T(8,128)(2,1)} %get-tuple-element.88), channel_id=1, source_target_pairs={{0,2},{1,3},{2,0},{3,1},{4,6},{5,7},{6,4},{7,5},{8,10},{9,11},{10,... | collective-permute-start | bytes 1769480 | tf_op jit(solution)/shard_map/ppermute | solution.py:701
  76.6 21.2 %all-to-all-start.2 = ((bf16[8,192,128]{2,1,0:T(8,128)(2,1)}), bf16[8,192,128]{2,1,0:T(8,128)(2,1)S(1)}, u32[]{:S(2)}, u32[]{:S(2)}) async-start(bf16[8,192,128]{2,1,0:T(8,128)(2,1)} %bitcast.26), calls=%async_computation.2 | async-start | bytes 786432 | tf_op jit(solution)/shard_map/all_to_all | solution.py:763
  94.7 13.6 %collective-permute-start.9 = (bf16[384,640]{1,0:T(8,128)(2,1)}, bf16[384,640]{1,0:T(8,128)(2,1)S(1)}, u32[]{:S(2)}, u32[]{:S(2)}) collective-permute-start(bf16[384,640]{1,0:T(8,128)(2,1)} %bitcast.101), channel_id=1, source_target_pairs={{0,1},{1,0},{2,3},{3,2},{4,5},{5,4},{6,7},{7,6},{8,9},{9,8},{10,11... | collective-permute-start | bytes 1474568 | tf_op jit(solution)/shard_map/ppermute | solution.py:701
  96.8 11.5 %collective-permute-start.10 = (bf16[384,512]{1,0:T(8,128)(2,1)}, bf16[384,512]{1,0:T(8,128)(2,1)}, u32[]{:S(2)}, u32[]{:S(2)}) collective-permute-start(bf16[384,512]{1,0:T(8,128)(2,1)} %bitcast.112), channel_id=1, source_target_pairs={{0,2},{1,3},{2,0},{3,1},{4,6},{5,7},{6,4},{7,5},{8,10},{9,11},{10,... | collective-permute-start | bytes 1179656 | tf_op jit(solution)/shard_map/ppermute | solution.py:701
  96.8 8.7 %collective-permute-start.7 = (bf16[384,384]{1,0:T(8,128)(2,1)}, bf16[384,384]{1,0:T(8,128)(2,1)S(1)}, u32[]{:S(2)}, u32[]{:S(2)}) collective-permute-start(bf16[384,384]{1,0:T(8,128)(2,1)} %bitcast.113), channel_id=1, source_target_pairs={{0,16},{8,24},{16,0},{24,8},{1,17},{9,25},{17,1},{25,9},{2,18},{10... | collective-permute-start | bytes 884744 | tf_op jit(solution)/shard_map/ppermute | solution.py:701
  101.7 19.3 %all-to-all-start.3 = ((bf16[8,192,128]{2,1,0:T(8,128)(2,1)}), bf16[8,192,128]{2,1,0:T(8,128)(2,1)S(1)}, u32[]{:S(2)}, u32[]{:S(2)}) async-start(bf16[8,192,128]{2,1,0:T(8,128)(2,1)} %bitcast.35), calls=%async_computation.3 | async-start | bytes 786432 | tf_op jit(solution)/shard_map/all_to_all | solution.py:766
  111.3 9.7 %collective-permute-start.12 = (bf16[192,640]{1,0:T(8,128)(2,1)}, bf16[192,640]{1,0:T(8,128)(2,1)S(1)}, u32[]{:S(2)}, u32[]{:S(2)}) collective-permute-start(bf16[192,640]{1,0:T(8,128)(2,1)} %bitcast.103), channel_id=1, source_target_pairs={{0,2},{1,3},{2,0},{3,1},{4,6},{5,7},{6,4},{7,5},{8,10},{9,11},{10,... | collective-permute-start | bytes 737288 | tf_op jit(solution)/shard_map/ppermute | solution.py:701
  113.4 7.6 %collective-permute-start.13 = (bf16[192,512]{1,0:T(8,128)(2,1)}, bf16[192,512]{1,0:T(8,128)(2,1)S(1)}, u32[]{:S(2)}, u32[]{:S(2)}) collective-permute-start(bf16[192,512]{1,0:T(8,128)(2,1)} %bitcast.114), channel_id=1, source_target_pairs={{0,16},{8,24},{16,0},{24,8},{1,17},{9,25},{17,1},{25,9},{2,18},{10... | collective-permute-start | bytes 589832 | tf_op jit(solution)/shard_map/ppermute | solution.py:701
  114.5 6.5 %collective-permute-start.14 = (bf16[192,384]{1,0:T(8,128)(2,1)}, bf16[192,384]{1,0:T(8,128)(2,1)S(1)}, u32[]{:S(2)}, u32[]{:S(2)}) collective-permute-start(bf16[192,384]{1,0:T(8,128)(2,1)} %bitcast.115), channel_id=1, source_target_pairs={{0,1},{1,0},{2,3},{3,2},{4,5},{5,4},{6,7},{7,6},{8,9},{9,8},{10,11... | collective-permute-start | bytes 442376 | tf_op jit(solution)/shard_map/ppermute | solution.py:701
  116.6 4.2 %collective-permute-start.11 = (f32[96,128]{1,0:T(8,128)S(1)}, f32[96,128]{1,0:T(8,128)S(1)}, u32[]{:S(2)}, u32[]{:S(2)}) collective-permute-start(f32[96,128]{1,0:T(8,128)S(1)} %get-tuple-element.108), channel_id=1, source_target_pairs={{0,16},{8,24},{16,0},{24,8},{1,17},{9,25},{17,1},{25,9},{2,18},{10... | collective-permute-start | bytes 147464 | tf_op jit(solution)/shard_map/ppermute | solution.py:701
  117.5 20.2 %collective-permute-start.2 = (bf16[384,768]{1,0:T(8,128)(2,1)}, bf16[384,768]{1,0:T(8,128)(2,1)S(1)}, u32[]{:S(2)}, u32[]{:S(2)}) collective-permute-start(bf16[384,768]{1,0:T(8,128)(2,1)} %get-tuple-element.77), channel_id=1, source_target_pairs={{0,8},{8,0},{16,24},{24,16},{1,9},{9,1},{17,25},{25,17},{2,10},{10... | collective-permute-start | bytes 1769480 | tf_op jit(solution)/shard_map/ppermute | solution.py:701
  124.4 20.5 %all-to-all-start.4 = ((bf16[8,112,128]{2,1,0:T(8,128)(2,1)}), bf16[8,112,128]{2,1,0:T(8,128)(2,1)S(1)}, u32[]{:S(2)}, u32[]{:S(2)}) async-start(bf16[8,112,128]{2,1,0:T(8,128)(2,1)} %shard_map.338.refs_8_.refs_7_), calls=%async_computation.4 | async-start | bytes 458752 | tf_op jit(solution)/shard_map/all_to_all | solution.py:1014
  131.8 17.8 %collective-permute-start.16 = (bf16[96,640]{1,0:T(8,128)(2,1)}, bf16[96,640]{1,0:T(8,128)(2,1)S(1)}, u32[]{:S(2)}, u32[]{:S(2)}) collective-permute-start(bf16[96,640]{1,0:T(8,128)(2,1)} %bitcast.105), channel_id=1, source_target_pairs={{0,4},{1,5},{2,6},{3,7},{4,0},{5,1},{6,2},{7,3},{8,12},{9,13},{10,... | collective-permute-start | bytes 368648 | tf_op jit(solution)/shard_map/ppermute | solution.py:701
  134.8 14.9 %collective-permute-start.17 = (bf16[96,512]{1,0:T(8,128)(2,1)}, bf16[96,512]{1,0:T(8,128)(2,1)S(1)}, u32[]{:S(2)}, u32[]{:S(2)}) collective-permute-start(bf16[96,512]{1,0:T(8,128)(2,1)} %bitcast.116), channel_id=1, source_target_pairs={{0,4},{1,5},{2,6},{3,7},{4,0},{5,1},{6,2},{7,3},{8,12},{9,13},{10,... | collective-permute-start | bytes 294920 | tf_op jit(solution)/shard_map/ppermute | solution.py:701
  134.9 14.8 %collective-permute-start.18 = (bf16[96,384]{1,0:T(8,128)(2,1)}, bf16[96,384]{1,0:T(8,128)(2,1)S(1)}, u32[]{:S(2)}, u32[]{:S(2)}) collective-permute-start(bf16[96,384]{1,0:T(8,128)(2,1)} %bitcast.117), channel_id=1, source_target_pairs={{0,4},{1,5},{2,6},{3,7},{4,0},{5,1},{6,2},{7,3},{8,12},{9,13},{10,... | collective-permute-start | bytes 221192 | tf_op jit(solution)/shard_map/ppermute | solution.py:701
  145.0 6.8 %collective-permute-start.15 = (bf16[656,128]{1,0:T(8,128)(2,1)S(1)}, bf16[656,128]{1,0:T(8,128)(2,1)S(1)}, u32[]{:S(2)}, u32[]{:S(2)}) collective-permute-start(bf16[656,128]{1,0:T(8,128)(2,1)S(1)} %shard_map.341.refs_0_.refs_1_), channel_id=1, source_target_pairs={{0,16},{8,24},{16,0},{24,8},{1,17},{9,25},{17,1},{25,9},{2,18},{10... | collective-permute-start | bytes 503816 | tf_op jit(solution)/shard_map/ppermute | solution.py:701
  151.8 1.7 %collective-permute-start.19 = (bf16[1312,128]{1,0:T(8,128)(2,1)S(1)}, bf16[1312,128]{1,0:T(8,128)(2,1)S(1)}, u32[]{:S(2)}, u32[]{:S(2)}) collective-permute-start(bf16[1312,128]{1,0:T(8,128)(2,1)S(1)} %shard_map.343), channel_id=1, source_target_pairs={{0,8},{8,0},{16,24},{24,16},{1,9},{9,1},{17,25},{25,17},{2,10},{10... | collective-permute-start | bytes 1007624 | tf_op jit(solution)/shard_map/ppermute | solution.py:701
  (5 other events, 53.7 us)

commit v4 on v3

--- a/solution.py
+++ b/solution.py
@@ -542,21 +542,14 @@
     put_split(out_ref, blocks * base + 2 * rows, total)
 
 
-def join_kernel(*refs):
-    *parts, out_ref = refs
-    rows = parts[0].shape[0]
-    for at, ref in enumerate(parts):
-        out_ref[at * rows : (at + 1) * rows] = ref[...]
+def pass_kernel(in_ref, out_ref):
+    out_ref[...] = in_ref[...]
 
 
 def tail_kernel(
     count, rows, pre_rows, place_ref, *refs,
 ):
-    parts, refs = list(refs[:count]), refs[count:]
-    joined = parts.pop()
-    size = parts[0].shape[0]
-    parts += [joined.at[at * size : (at + 1) * size] for at in range(len(parts))]
-    count = len(parts)
+    parts, refs = refs[:count], refs[count:]
     (
         pre_gain_ref, pre_shift_ref, inner_ref, inner_bias_ref, outer_ref, outer_bias_ref,
         post_gain_ref, post_shift_ref, expand_bias_ref, reduce_bias_ref, small_ref,
@@ -996,7 +989,6 @@
         far_in=(6, 5, 4),
         far_out=(0,),
         flops=lon_flops,
-        after=ahead,
     )
     result_dims = (items, cells, 1, width)
     (grad_tokens,) = call(
@@ -1040,13 +1032,13 @@
     thirds = [third]
     if halves:
         thirds.append(pair_swap(third, *dp_bits[0]))
-    (joined,) = call(
-        join_kernel,
-        [shape((len(thirds) * third_dims[0], 128), bf16)],
-        thirds,
+    (last,) = call(
+        pass_kernel,
+        [shape(third_dims, bf16)],
+        thirds[-1:],
         after=(stay(reduce_part),),
     )
-    thirds += [pair_swap(joined, "dp", 1)]
+    thirds += [pair_swap(v, "dp", 1) for v in thirds[:-1] + [last]]
 
     args = (places, *thirds)
     line_dims = (width,)

time: 157 us -> 156 us (level)
    ppermute x20 -> x21, waiting for transfers between devices: 23.6 us -> 23.3 us  [pair_swap(): return lax.ppermute(operand, axis_name, [(i, i ^ bit) for i in range(size)])]
    ppermute x20 -> x21, starting transfers between devices: 18.7 us -> 18.8 us  [pair_swap(): return lax.ppermute(operand, axis_name, [(i, i ^ bit) for i in range(size)])]
  transfers between devices with their start and end apart: 25 -> 26, of which waited for: 11 -> 10; matrix products, arithmetic and copies ran while one was open for 2% -> 2% of each run, Pallas kernels for 24% -> 24%
where the time goes in v4:
time: 156 us; the launch traced here: 155 us
  Pallas kernels  64.6 us (41%)
  waiting for transfers between devices  43.6 us (28%)
  starting transfers between devices  41.5 us (27%)
  local copies, waits for them, and re-layouts  2.95 us (2%)
    pallas_call x19, Pallas kernels, call(): pl.pallas_call(whole_kernel, out_shape=shapes, grid_spec=pltpu.PrefetchSc...  64.6 us
    ppermute x21, waiting for transfers between devices, pair_swap(): return lax.ppermute(operand, axis_name, [(i, i ^ bit) for i in range(size)])  23.3 us
    all_to_all x4, waiting for transfers between devices, exchange(): both = lax.all_to_all(both, 'lat', 0, 0, tiled=True)  20.4 us
    ppermute x21, starting transfers between devices, pair_swap(): return lax.ppermute(operand, axis_name, [(i, i ^ bit) for i in range(size)])  18.8 us
    all_to_all x4, starting transfers between devices, exchange(): both = lax.all_to_all(both, 'lat', 0, 0, tiled=True)  18.3 us
    all_to_all x1, starting transfers between devices, body(): tail = lax.all_to_all(tail, 'lat', 0, 0, tiled=True)  4.38 us
  transfers between devices with their start and end apart: 26, of which 10 were waited for; matrix products, arithmetic and copies ran while one was open for 2% of the time, Pallas kernels for 24%

profile of v4, /device:TPU:0, one launch (start us, length us, event | category | flops | bytes accessed | tf_op | source)
XLA Modules:
  0.0 154.9 jit_solution(6125619213496845745)
XLA Ops:
  1.8 2.9 %shard_map.326 = bf16[8,2,96,128]{3,2,1,0:T(8,128)(2,1)} custom-call(s32[2,1,2]{2,1,0:T(1,128)} %refs_0_.9, s32[1]{0:T(128)} %bitcast.refs_1_, bf16[2,180,768]{2,1,0:T(8,128)(2,1)S(1)} %bitcast.75, s32[2,1,180]{2,1,0:T(1,128)} %bitcast.102, f32[768]{0:T(1024)} %refs_6_.9, f32[768]{0:T(1024)} %refs_6_.7, bf16[128,180]{1,0:T(8,128)(2,1)} %constant.110.clone.refs_6_), custom_call_target="tpu_custom_call" | custom-call | flops 70778880 | bytes 999860 | tf_op jit(solution)/shard_map/pallas_call | solution.py:667
  4.7 7.3 %all-to-all-start = ((bf16[8,192,128]{2,1,0:T(8,128)(2,1)}), bf16[8,192,128]{2,1,0:T(8,128)(2,1)S(1)}, u32[]{:S(2)}, u32[]{:S(2)}) async-start(bf16[8,192,128]{2,1,0:T(8,128)(2,1)} %bitcast.3), calls=%async_computation | async-start | bytes 786432 | tf_op jit(solution)/shard_map/all_to_all | solution.py:756
  14.7 9.0 %all-to-all-done = bf16[8,192,128]{2,1,0:T(8,128)(2,1)S(1)} async-done(((bf16[8,192,128]{2,1,0:T(8,128)(2,1)}), bf16[8,192,128]{2,1,0:T(8,128)(2,1)S(1)}, u32[]{:S(2)}, u32[]{:S(2)}) %all-to-all-start) | async-done | bytes 393248 | tf_op jit(solution)/shard_map/all_to_all | solution.py:756
  23.6 4.5 %shard_map.327 = (bf16[8,2,96,128]{3,2,1,0:T(8,128)(2,1)}, bf16[8,128,192]{2,1,0:T(8,128)(2,1)}, bf16[8,128,192]{2,1,0:T(8,128)(2,1)}, f32[8,128,192]{2,1,0:T(8,128)}, f32[8,128,192]{2,1,0:T(8,128)}) custom-call(bf16[8,2,96,128]{3,2,1,0:T(8,128)(2,1)S(1)} %bitcast.81, bf16[192,192]{1,0:T(8,128)(2,1)S(1)} %maximum_maximum_fusion.refs_1_.refs_3_, ...), custom_call_target="tpu_custom_call" | custom-call | flops 150994944 | bytes 3499520 | tf_op jit(solution)/shard_map/pallas_call | solution.py:667
  28.2 3.6 %all-to-all-start.1 = ((bf16[8,192,128]{2,1,0:T(8,128)(2,1)}), bf16[8,192,128]{2,1,0:T(8,128)(2,1)S(1)}, u32[]{:S(2)}, u32[]{:S(2)}) async-start(bf16[8,192,128]{2,1,0:T(8,128)(2,1)} %bitcast.9), calls=%async_computation.1 | async-start | bytes 786432 | tf_op jit(solution)/shard_map/all_to_all | solution.py:759
  32.0 11.4 %all-to-all-done.1 = bf16[8,192,128]{2,1,0:T(8,128)(2,1)S(1)} async-done(((bf16[8,192,128]{2,1,0:T(8,128)(2,1)}), bf16[8,192,128]{2,1,0:T(8,128)(2,1)S(1)}, u32[]{:S(2)}, u32[]{:S(2)}) %all-to-all-start.1) | async-done | bytes 393248 | tf_op jit(solution)/shard_map/all_to_all | solution.py:759
  43.4 2.9 %shard_map.328 = (f32[2,180,768]{2,1,0:T(8,128)S(1)}, bf16[2,192,768]{2,1,0:T(8,128)(2,1)S(1)}) custom-call(s32[2,1,2]{2,1,0:T(1,128)} %refs_0_.9, s32[1]{0:T(128)} %bitcast.refs_1_, bf16[8,2,96,128]{3,2,1,0:T(8,128)(2,1)S(1)} %bitcast.82, bf16[2,180,768]{2,1,0:T(8,128)(2,1)S(1)} %bitcast.76, s32[2,1,180]{2,1,0:T(1,128)} %bitcast.103, f32[768]{0:T(1024)} %refs_6_.9, ...), custom_call_target="tpu_custom_call" | custom-call | flops 70778880 | bytes 2701748 | tf_op jit(solution)/shard_map/pallas_call | solution.py:667
  48.5 17.6 %shard_map.329 = (bf16[768,640]{1,0:T(8,128)(2,1)}, bf16[768,640]{1,0:T(8,128)(2,1)}, bf16[768,512]{1,0:T(8,128)(2,1)}, bf16[768,512]{1,0:T(8,128)(2,1)}, bf16[7...) custom-call(s32[4]{0:T(128)S(1)} %pad_add_fusion.refs_0_, ...), custom_call_target="tpu_custom_call" | custom-call | flops 10871635968 | bytes 20072468 | tf_op jit(solution)/shard_map/pallas_call | solution.py:667
  71.1 4.7 %shard_map.330 = (f32[2,180,768]{2,1,0:T(8,128)}, bf16[8,2,96,128]{3,2,1,0:T(8,128)(2,1)}, f32[3,768]{1,0:T(4,128)S(1)}) custom-call(s32[2,1,2]{2,1,0:T(1,128)} %refs_0_.9, s32[1]{0:T(128)} %bitcast.refs_1_, f32[2,180,768]{2,1,0:T(8,128)S(1)} %get-tuple-element.74.refs_2_.refs_0_, f32[2,192,768]{2,1,0:T(8,128)} %bitcast.93, ...), custom_call_target="tpu_custom_call" | custom-call | flops 70778880 | bytes 5024180 | tf_op jit(solution)/shard_map/pallas_call | solution.py:667
  75.8 3.7 %all-to-all-start.2 = ((bf16[8,192,128]{2,1,0:T(8,128)(2,1)}), bf16[8,192,128]{2,1,0:T(8,128)(2,1)S(1)}, u32[]{:S(2)}, u32[]{:S(2)}) async-start(bf16[8,192,128]{2,1,0:T(8,128)(2,1)} %bitcast.26), calls=%async_computation.2 | async-start | bytes 786432 | tf_op jit(solution)/shard_map/all_to_all | solution.py:756
  79.5 10.0 %collective-permute-done.6 = bf16[768,384]{1,0:T(8,128)(2,1)} collective-permute-done((bf16[768,384]{1,0:T(8,128)(2,1)}, bf16[768,384]{1,0:T(8,128)(2,1)}, u32[]{:S(2)}, u32[]{:S(2)}) %collective-permute-start.6) | collective-permute-done | bytes 589856 | tf_op jit(solution)/shard_map/ppermute | solution.py:694
  90.3 3.8 %shard_map.332 = (bf16[4,96,640]{2,1,0:T(8,128)(2,1)}, bf16[4,96,640]{2,1,0:T(8,128)(2,1)}, bf16[4,96,512]{2,1,0:T(8,128)(2,1)}, bf16[4,96,512]{2,1,0:T(8,128)(2...) custom-call(s32[4]{0:T(128)S(1)} %pad_add_fusion.refs_0_, bf16[4,2,96,640]{3,2,1,0:T(8,128)(2,1)} %bitcast.114, ...), custom_call_target="tpu_custom_call" | custom-call | flops 20000000000 | bytes 7077904 | tf_op jit(solution)/shard_map/pallas_call | solution.py:667
  97.2 3.9 %shard_map.333 = (bf16[8,2,96,128]{3,2,1,0:T(8,128)(2,1)}, bf16[8,128,192]{2,1,0:T(8,128)(2,1)}, bf16[8,128,192]{2,1,0:T(8,128)(2,1)}, f32[2,192]{1,0:T(2,128)S(1)}) custom-call(bf16[8,2,96,128]{3,2,1,0:T(8,128)(2,1)S(1)} %bitcast.83, f32[8,128,192]{2,1,0:T(8,128)} %get-tuple-element.81.refs_1_, f32[8,128,192]{2,1,0:T(8,128)} %get-tuple-element.82.refs_2_, ...), custom_call_target="tpu_custom_call" | custom-call | flops 301989888 | bytes 3499520 | tf_op jit(solution)/shard_map/pallas_call | solution.py:667
  101.1 3.7 %all-to-all-start.3 = ((bf16[8,192,128]{2,1,0:T(8,128)(2,1)}), bf16[8,192,128]{2,1,0:T(8,128)(2,1)S(1)}, u32[]{:S(2)}, u32[]{:S(2)}) async-start(bf16[8,192,128]{2,1,0:T(8,128)(2,1)} %bitcast.35), calls=%async_computation.3 | async-start | bytes 786432 | tf_op jit(solution)/shard_map/all_to_all | solution.py:759
  104.9 2.8 %shard_map.335 = (f32[192,128]{1,0:T(8,128)S(1)}, f32[192,128]{1,0:T(8,128)S(1)}) custom-call(s32[3]{0:T(128)S(1)} %pad_add_fusion.1.refs_0_, bf16[8,128,192]{2,1,0:T(8,128)(2,1)} %get-tuple-element.92.refs_1_, bf16[8,128,192]{2,1,0:T(8,128)(2,1)} %get-tuple-element.93.refs_2_, bf16[8,128,192]{2,1,0:T(8,128)(2,1)} %get-tuple-element.94.refs_3_, ...), custom_call_target="tpu_custom_call" | custom-call | bytes 1820172 | tf_op jit(solution)/shard_map/pallas_call | solution.py:667
  107.7 2.9 %shard_map.336 = (bf16[2,96,640]{2,1,0:T(8,128)(2,1)}, bf16[2,96,640]{2,1,0:T(8,128)(2,1)}, bf16[1,192,512]{2,1,0:T(8,128)(2,1)}, bf16[1,192,512]{2,1,0:T(8,128)...) custom-call(s32[4]{0:T(128)S(1)} %pad_add_fusion.refs_0_, bf16[2,2,96,640]{3,2,1,0:T(8,128)(2,1)} %bitcast.117, ...), custom_call_target="tpu_custom_call" | custom-call | flops 20000000000 | bytes 3538960 | tf_op jit(solution)/shard_map/pallas_call | solution.py:667
  116.9 3.3 %collective-permute-done.11.refs_8_ = f32[96,128]{1,0:T(8,128)S(1)} collective-permute-done((f32[96,128]{1,0:T(8,128)S(1)}, f32[96,128]{1,0:T(8,128)S(1)}, u32[]{:S(2)}, u32[]{:S(2)}) %collective-permute-start.11) | collective-permute-done | bytes 49184 | tf_op jit(solution)/shard_map/ppermute | solution.py:694
  120.1 3.4 %shard_map.338.refs_8_.refs_7_ = bf16[8,112,128]{2,1,0:T(8,128)(2,1)} custom-call(s32[2,1,2]{2,1,0:T(1,128)} %refs_0_.9, s32[1]{0:T(128)} %bitcast.refs_1_, bf16[8,2,96,128]{3,2,1,0:T(8,128)(2,1)S(1)} %bitcast.79, bf16[2,180,768]{2,1,0:T(8,128)(2,1)S(1)} %bitcast.77, f32[2,180,768]{2,1,0:T(8,128)} %get-tuple-element.91.refs_4_, s32[2,1,180]{2,1,0:T(1,128)} %bitcast.105, ...), custom_call_target="tpu_custom_call" | custom-call | flops 70778880 | bytes 2427316 | tf_op jit(solution)/shard_map/pallas_call | solution.py:667
  123.6 4.4 %all-to-all-start.4 = ((bf16[8,112,128]{2,1,0:T(8,128)(2,1)}), bf16[8,112,128]{2,1,0:T(8,128)(2,1)S(1)}, u32[]{:S(2)}, u32[]{:S(2)}) async-start(bf16[8,112,128]{2,1,0:T(8,128)(2,1)} %shard_map.338.refs_8_.refs_7_), calls=%async_computation.4 | async-start | bytes 458752 | tf_op jit(solution)/shard_map/all_to_all | solution.py:1006
  130.7 3.0 %collective-permute-start.17 = (bf16[96,640]{1,0:T(8,128)(2,1)}, bf16[96,640]{1,0:T(8,128)(2,1)}, u32[]{:S(2)}, u32[]{:S(2)}) collective-permute-start(bf16[96,640]{1,0:T(8,128)(2,1)} %bitcast.100), channel_id=1, source_target_pairs={{0,4},{1,5},{2,6},{3,7},{4,0},{5,1},{6,2},{7,3},{8,12},{9,13},{10,... | collective-permute-start | bytes 368648 | tf_op jit(solution)/shard_map/ppermute | solution.py:694
  133.7 2.8 %collective-permute-start.19 = (bf16[96,384]{1,0:T(8,128)(2,1)}, bf16[96,384]{1,0:T(8,128)(2,1)}, u32[]{:S(2)}, u32[]{:S(2)}) collective-permute-start(bf16[96,384]{1,0:T(8,128)(2,1)} %bitcast.112), channel_id=1, source_target_pairs={{0,4},{1,5},{2,6},{3,7},{4,0},{5,1},{6,2},{7,3},{8,12},{9,13},{10,... | collective-permute-start | bytes 221192 | tf_op jit(solution)/shard_map/ppermute | solution.py:694
  136.6 2.9 %shard_map.331.refs_6_ = bf16[180,2,768]{2,1,0:T(2,128)(2,1)} custom-call(f32[2,180,768]{2,1,0:T(8,128)S(1)} %get-tuple-element.74.refs_2_.refs_0_, f32[2,192,768]{2,1,0:T(8,128)} %bitcast.94, bf16[2,192,768]{2,1,0:T(8,128)(2,1)S(1)} %bitcast.85, f32[768]{0:T(1024)} %refs_3_.1, bf16[8,2,96,128]{3,2,1,0:T(8,128)(2,1)} %get-tuple-element.80.refs_4_.refs_7_), custom_call_target="tpu_custom_call" | custom-call | bytes 3431424 | tf_op jit(solution)/shard_map/pallas_call | solution.py:667
  139.5 4.2 %shard_map.339.refs_7_ = f32[2,180,1,768]{3,2,1,0:T(1,128)} custom-call(s32[2,1,2]{2,1,0:T(1,128)} %refs_0_.9, s32[1]{0:T(128)} %bitcast.refs_1_, bf16[8,2,96,128]{3,2,1,0:T(8,128)(2,1)S(1)} %bitcast.80, bf16[2,180,768]{2,1,0:T(8,128)(2,1)S(1)} %bitcast.78, f32[2,180,768]{2,1,0:T(8,128)} %get-tuple-element.91.refs_4_, s32[2,1,180]{2,1,0:T(1,128)} %bitcast.106, ...), custom_call_target="tpu_custom_call" | custom-call | flops 70778880 | bytes 3208628 | tf_op jit(solution)/shard_map/pallas_call | solution.py:667
  144.8 3.9 %collective-permute-done.19.refs_5_ = bf16[96,384]{1,0:T(8,128)(2,1)} collective-permute-done((bf16[96,384]{1,0:T(8,128)(2,1)}, bf16[96,384]{1,0:T(8,128)(2,1)}, u32[]{:S(2)}, u32[]{:S(2)}) %collective-permute-start.19) | collective-permute-done | bytes 73760 | tf_op jit(solution)/shard_map/ppermute | solution.py:694
  (67 shorter events, 31.1 us)
Async XLA Ops:
  4.7 19.0 %all-to-all-start = ((bf16[8,192,128]{2,1,0:T(8,128)(2,1)}), bf16[8,192,128]{2,1,0:T(8,128)(2,1)S(1)}, u32[]{:S(2)}, u32[]{:S(2)}) async-start(bf16[8,192,128]{2,1,0:T(8,128)(2,1)} %bitcast.3), calls=%async_computation | async-start | bytes 786432 | tf_op jit(solution)/shard_map/all_to_all | solution.py:756
  28.2 15.2 %all-to-all-start.1 = ((bf16[8,192,128]{2,1,0:T(8,128)(2,1)}), bf16[8,192,128]{2,1,0:T(8,128)(2,1)S(1)}, u32[]{:S(2)}, u32[]{:S(2)}) async-start(bf16[8,192,128]{2,1,0:T(8,128)(2,1)} %bitcast.9), calls=%async_computation.1 | async-start | bytes 786432 | tf_op jit(solution)/shard_map/all_to_all | solution.py:759
  32.0 14.6 %collective-permute-start.1 = (bf16[384,768]{1,0:T(8,128)(2,1)S(1)}, bf16[384,768]{1,0:T(8,128)(2,1)}, u32[]{:S(2)}, u32[]{:S(2)}) collective-permute-start(bf16[384,768]{1,0:T(8,128)(2,1)S(1)} %bitcast.90), channel_id=1, source_target_pairs={{0,8},{8,0},{16,24},{24,16},{1,9},{9,1},{17,25},{25,17},{2,10},{10... | collective-permute-start | bytes 1769480 | tf_op jit(solution)/shard_map/ppermute | solution.py:694
  46.3 2.2 %collective-permute-start = (bf16[384,768]{1,0:T(8,128)(2,1)S(1)}, bf16[384,768]{1,0:T(8,128)(2,1)}, u32[]{:S(2)}, u32[]{:S(2)}) collective-permute-start(bf16[384,768]{1,0:T(8,128)(2,1)S(1)} %bitcast.88), channel_id=1, source_target_pairs={{0,8},{8,0},{16,24},{24,16},{1,9},{9,1},{17,25},{25,17},{2,10},{10... | collective-permute-start | bytes 1769480 | tf_op jit(solution)/shard_map/ppermute | solution.py:694
  66.1 24.2 %collective-permute-start.4 = (bf16[768,640]{1,0:T(8,128)(2,1)}, bf16[768,640]{1,0:T(8,128)(2,1)}, u32[]{:S(2)}, u32[]{:S(2)}) collective-permute-start(bf16[768,640]{1,0:T(8,128)(2,1)} %get-tuple-element.84), channel_id=1, source_target_pairs={{0,16},{8,24},{16,0},{24,8},{1,17},{9,25},{17,1},{25,9},{2,18},{10... | collective-permute-start | bytes 2949128 | tf_op jit(solution)/shard_map/ppermute | solution.py:694
  67.7 22.3 %collective-permute-start.5 = (bf16[768,512]{1,0:T(8,128)(2,1)}, bf16[768,512]{1,0:T(8,128)(2,1)}, u32[]{:S(2)}, u32[]{:S(2)}) collective-permute-start(bf16[768,512]{1,0:T(8,128)(2,1)} %get-tuple-element.86), channel_id=1, source_target_pairs={{0,1},{1,0},{2,3},{3,2},{4,5},{5,4},{6,7},{7,6},{8,9},{9,8},{10,11... | collective-permute-start | bytes 2359304 | tf_op jit(solution)/shard_map/ppermute | solution.py:694
  69.1 2.0 %collective-permute-start.3 = (bf16[384,768]{1,0:T(8,128)(2,1)S(1)}, bf16[384,768]{1,0:T(8,128)(2,1)S(1)}, u32[]{:S(2)}, u32[]{:S(2)}) collective-permute-start(bf16[384,768]{1,0:T(8,128)(2,1)S(1)} %get-tuple-element.79), channel_id=1, source_target_pairs={{0,8},{8,0},{16,24},{24,16},{1,9},{9,1},{17,25},{25,17},{2,10},{10... | collective-permute-start | bytes 1769480 | tf_op jit(solution)/shard_map/ppermute | solution.py:694
  69.1 20.4 %collective-permute-start.6 = (bf16[768,384]{1,0:T(8,128)(2,1)}, bf16[768,384]{1,0:T(8,128)(2,1)}, u32[]{:S(2)}, u32[]{:S(2)}) collective-permute-start(bf16[768,384]{1,0:T(8,128)(2,1)} %get-tuple-element.88), channel_id=1, source_target_pairs={{0,2},{1,3},{2,0},{3,1},{4,6},{5,7},{6,4},{7,5},{8,10},{9,11},{10,... | collective-permute-start | bytes 1769480 | tf_op jit(solution)/shard_map/ppermute | solution.py:694
  75.8 21.4 %all-to-all-start.2 = ((bf16[8,192,128]{2,1,0:T(8,128)(2,1)}), bf16[8,192,128]{2,1,0:T(8,128)(2,1)S(1)}, u32[]{:S(2)}, u32[]{:S(2)}) async-start(bf16[8,192,128]{2,1,0:T(8,128)(2,1)} %bitcast.26), calls=%async_computation.2 | async-start | bytes 786432 | tf_op jit(solution)/shard_map/all_to_all | solution.py:756
  94.1 13.6 %collective-permute-start.9 = (bf16[384,640]{1,0:T(8,128)(2,1)}, bf16[384,640]{1,0:T(8,128)(2,1)}, u32[]{:S(2)}, u32[]{:S(2)}) collective-permute-start(bf16[384,640]{1,0:T(8,128)(2,1)} %bitcast.96), channel_id=1, source_target_pairs={{0,1},{1,0},{2,3},{3,2},{4,5},{5,4},{6,7},{7,6},{8,9},{9,8},{10,11... | collective-permute-start | bytes 1474568 | tf_op jit(solution)/shard_map/ppermute | solution.py:694
  96.3 11.4 %collective-permute-start.10 = (bf16[384,512]{1,0:T(8,128)(2,1)}, bf16[384,512]{1,0:T(8,128)(2,1)}, u32[]{:S(2)}, u32[]{:S(2)}) collective-permute-start(bf16[384,512]{1,0:T(8,128)(2,1)} %bitcast.107), channel_id=1, source_target_pairs={{0,2},{1,3},{2,0},{3,1},{4,6},{5,7},{6,4},{7,5},{8,10},{9,11},{10,... | collective-permute-start | bytes 1179656 | tf_op jit(solution)/shard_map/ppermute | solution.py:694
  96.3 8.6 %collective-permute-start.7 = (bf16[384,384]{1,0:T(8,128)(2,1)}, bf16[384,384]{1,0:T(8,128)(2,1)S(1)}, u32[]{:S(2)}, u32[]{:S(2)}) collective-permute-start(bf16[384,384]{1,0:T(8,128)(2,1)} %bitcast.108), channel_id=1, source_target_pairs={{0,16},{8,24},{16,0},{24,8},{1,17},{9,25},{17,1},{25,9},{2,18},{10... | collective-permute-start | bytes 884744 | tf_op jit(solution)/shard_map/ppermute | solution.py:694
  101.1 19.0 %all-to-all-start.3 = ((bf16[8,192,128]{2,1,0:T(8,128)(2,1)}), bf16[8,192,128]{2,1,0:T(8,128)(2,1)S(1)}, u32[]{:S(2)}, u32[]{:S(2)}) async-start(bf16[8,192,128]{2,1,0:T(8,128)(2,1)} %bitcast.35), calls=%async_computation.3 | async-start | bytes 786432 | tf_op jit(solution)/shard_map/all_to_all | solution.py:759
  110.7 17.3 %collective-permute-start.12 = (bf16[192,640]{1,0:T(8,128)(2,1)}, bf16[192,640]{1,0:T(8,128)(2,1)}, u32[]{:S(2)}, u32[]{:S(2)}) collective-permute-start(bf16[192,640]{1,0:T(8,128)(2,1)} %bitcast.98), channel_id=1, source_target_pairs={{0,2},{1,3},{2,0},{3,1},{4,6},{5,7},{6,4},{7,5},{8,10},{9,11},{10,... | collective-permute-start | bytes 737288 | tf_op jit(solution)/shard_map/ppermute | solution.py:694
  112.7 15.2 %collective-permute-start.13 = (bf16[192,512]{1,0:T(8,128)(2,1)}, bf16[192,512]{1,0:T(8,128)(2,1)}, u32[]{:S(2)}, u32[]{:S(2)}) collective-permute-start(bf16[192,512]{1,0:T(8,128)(2,1)} %bitcast.109), channel_id=1, source_target_pairs={{0,16},{8,24},{16,0},{24,8},{1,17},{9,25},{17,1},{25,9},{2,18},{10... | collective-permute-start | bytes 589832 | tf_op jit(solution)/shard_map/ppermute | solution.py:694
  114.0 14.0 %collective-permute-start.14 = (bf16[192,384]{1,0:T(8,128)(2,1)}, bf16[192,384]{1,0:T(8,128)(2,1)}, u32[]{:S(2)}, u32[]{:S(2)}) collective-permute-start(bf16[192,384]{1,0:T(8,128)(2,1)} %bitcast.110), channel_id=1, source_target_pairs={{0,1},{1,0},{2,3},{3,2},{4,5},{5,4},{6,7},{7,6},{8,9},{9,8},{10,11... | collective-permute-start | bytes 442376 | tf_op jit(solution)/shard_map/ppermute | solution.py:694
  116.0 4.2 %collective-permute-start.11 = (f32[96,128]{1,0:T(8,128)S(1)}, f32[96,128]{1,0:T(8,128)S(1)}, u32[]{:S(2)}, u32[]{:S(2)}) collective-permute-start(f32[96,128]{1,0:T(8,128)S(1)} %get-tuple-element.108), channel_id=1, source_target_pairs={{0,16},{8,24},{16,0},{24,8},{1,17},{9,25},{17,1},{25,9},{2,18},{10... | collective-permute-start | bytes 147464 | tf_op jit(solution)/shard_map/ppermute | solution.py:694
  116.9 19.7 %collective-permute-start.2 = (bf16[384,768]{1,0:T(8,128)(2,1)S(1)}, bf16[384,768]{1,0:T(8,128)(2,1)S(1)}, u32[]{:S(2)}, u32[]{:S(2)}) collective-permute-start(bf16[384,768]{1,0:T(8,128)(2,1)S(1)} %get-tuple-element.77), channel_id=1, source_target_pairs={{0,8},{8,0},{16,24},{24,16},{1,9},{9,1},{17,25},{25,17},{2,10},{10... | collective-permute-start | bytes 1769480 | tf_op jit(solution)/shard_map/ppermute | solution.py:694
  123.6 20.1 %all-to-all-start.4 = ((bf16[8,112,128]{2,1,0:T(8,128)(2,1)}), bf16[8,112,128]{2,1,0:T(8,128)(2,1)S(1)}, u32[]{:S(2)}, u32[]{:S(2)}) async-start(bf16[8,112,128]{2,1,0:T(8,128)(2,1)} %shard_map.338.refs_8_.refs_7_), calls=%async_computation.4 | async-start | bytes 458752 | tf_op jit(solution)/shard_map/all_to_all | solution.py:1006
  130.7 18.1 %collective-permute-start.17 = (bf16[96,640]{1,0:T(8,128)(2,1)}, bf16[96,640]{1,0:T(8,128)(2,1)}, u32[]{:S(2)}, u32[]{:S(2)}) collective-permute-start(bf16[96,640]{1,0:T(8,128)(2,1)} %bitcast.100), channel_id=1, source_target_pairs={{0,4},{1,5},{2,6},{3,7},{4,0},{5,1},{6,2},{7,3},{8,12},{9,13},{10,... | collective-permute-start | bytes 368648 | tf_op jit(solution)/shard_map/ppermute | solution.py:694
  133.6 15.1 %collective-permute-start.18 = (bf16[96,512]{1,0:T(8,128)(2,1)}, bf16[96,512]{1,0:T(8,128)(2,1)}, u32[]{:S(2)}, u32[]{:S(2)}) collective-permute-start(bf16[96,512]{1,0:T(8,128)(2,1)} %bitcast.111), channel_id=1, source_target_pairs={{0,4},{1,5},{2,6},{3,7},{4,0},{5,1},{6,2},{7,3},{8,12},{9,13},{10,... | collective-permute-start | bytes 294920 | tf_op jit(solution)/shard_map/ppermute | solution.py:694
  133.7 15.0 %collective-permute-start.19 = (bf16[96,384]{1,0:T(8,128)(2,1)}, bf16[96,384]{1,0:T(8,128)(2,1)}, u32[]{:S(2)}, u32[]{:S(2)}) collective-permute-start(bf16[96,384]{1,0:T(8,128)(2,1)} %bitcast.112), channel_id=1, source_target_pairs={{0,4},{1,5},{2,6},{3,7},{4,0},{5,1},{6,2},{7,3},{8,12},{9,13},{10,... | collective-permute-start | bytes 221192 | tf_op jit(solution)/shard_map/ppermute | solution.py:694
  143.8 7.1 %collective-permute-start.16 = (bf16[656,128]{1,0:T(8,128)(2,1)S(1)}, bf16[656,128]{1,0:T(8,128)(2,1)S(1)}, u32[]{:S(2)}, u32[]{:S(2)}) collective-permute-start(bf16[656,128]{1,0:T(8,128)(2,1)S(1)} %shard_map.341.refs_1_), channel_id=1, source_target_pairs={{0,8},{8,0},{16,24},{24,16},{1,9},{9,1},{17,25},{25,17},{2,10},{10... | collective-permute-start | bytes 503816 | tf_op jit(solution)/shard_map/ppermute | solution.py:694
  143.8 6.9 %collective-permute-start.15 = (bf16[656,128]{1,0:T(8,128)(2,1)S(1)}, bf16[656,128]{1,0:T(8,128)(2,1)S(1)}, u32[]{:S(2)}, u32[]{:S(2)}) collective-permute-start(bf16[656,128]{1,0:T(8,128)(2,1)S(1)} %shard_map.341.refs_1_), channel_id=1, source_target_pairs={{0,16},{8,24},{16,0},{24,8},{1,17},{9,25},{17,1},{25,9},{2,18},{10... | collective-permute-start | bytes 503816 | tf_op jit(solution)/shard_map/ppermute | solution.py:694
  (6 other events, 55.5 us)

commit v5 on v4

--- a/solution.py
+++ b/solution.py
@@ -11,7 +11,7 @@
 from jax.sharding import PartitionSpec as P
 
 MODES = 64
-GROUP = 2
+GROUP = 4
 COMBINE_FLOPS = 2 * 10**10
 shrink_level = 0.01
 epsilon = 1e-05
@@ -540,6 +540,10 @@
     for ref in other_refs:
         total += jnp.sum(ref[...].astype(f32), axis=0)
     put_split(out_ref, blocks * base + 2 * rows, total)
+
+
+def gate_kernel(place_ref, out_ref):
+    out_ref[...] = jnp.zeros_like(out_ref)
 
 
 def pass_kernel(in_ref, out_ref):
@@ -1032,11 +1036,19 @@
     thirds = [third]
     if halves:
         thirds.append(pair_swap(third, *dp_bits[0]))
+    (gate,) = call(
+        gate_kernel,
+        [shape((8, 128), f32)],
+        (places,),
+        prefetch=1,
+        flops=COMBINE_FLOPS,
+        after=scatter.recvs,
+    )
     (last,) = call(
         pass_kernel,
         [shape(third_dims, bf16)],
         thirds[-1:],
-        after=(stay(reduce_part),),
+        after=(gate,),
     )
     thirds += [pair_swap(v, "dp", 1) for v in thirds[:-1] + [last]]
 

time: 156 us -> 156 us (level)
    pallas_call x19 -> x20, Pallas kernels: 64.6 us -> 65 us  [call(): pl.pallas_call(whole_kernel, out_shape=shapes, grid_spec=pltpu.PrefetchSc...]
  transfers between devices with their start and end apart: 26 -> 26, of which waited for: 10 -> 9; matrix products, arithmetic and copies ran while one was open for 2% -> 2% of each run, Pallas kernels for 24% -> 24%
where the time goes in v5:
time: 156 us; the launch traced here: 155 us
  Pallas kernels  65 us (42%)
  waiting for transfers between devices  42.5 us (27%)
  starting transfers between devices  42 us (27%)
  local copies, waits for them, and re-layouts  2.95 us (2%)
    pallas_call x20, Pallas kernels, call(): pl.pallas_call(whole_kernel, out_shape=shapes, grid_spec=pltpu.PrefetchSc...  65 us
    ppermute x21, waiting for transfers between devices, pair_swap(): return lax.ppermute(operand, axis_name, [(i, i ^ bit) for i in range(size)])  22.1 us
    all_to_all x4, waiting for transfers between devices, exchange(): both = lax.all_to_all(both, 'lat', 0, 0, tiled=True)  20.4 us
    ppermute x21, starting transfers between devices, pair_swap(): return lax.ppermute(operand, axis_name, [(i, i ^ bit) for i in range(size)])  19.3 us
    all_to_all x4, starting transfers between devices, exchange(): both = lax.all_to_all(both, 'lat', 0, 0, tiled=True)  18.3 us
    all_to_all x1, starting transfers between devices, body(): tail = lax.all_to_all(tail, 'lat', 0, 0, tiled=True)  4.38 us
  transfers between devices with their start and end apart: 26, of which 9 were waited for; matrix products, arithmetic and copies ran while one was open for 2% of the time, Pallas kernels for 24%

profile of v5, /device:TPU:0, one launch (start us, length us, event | category | flops | bytes accessed | tf_op | source)
XLA Modules:
  0.0 154.6 jit_solution(6066506130695782262)
XLA Ops:
  1.8 2.9 %shard_map.326 = bf16[8,2,96,128]{3,2,1,0:T(8,128)(2,1)} custom-call(s32[2,1,2]{2,1,0:T(1,128)} %refs_0_.9, s32[1]{0:T(128)} %bitcast.refs_1_, bf16[2,180,768]{2,1,0:T(8,128)(2,1)S(1)} %bitcast.75, s32[2,1,180]{2,1,0:T(1,128)} %bitcast.102, f32[768]{0:T(1024)} %refs_6_.9, f32[768]{0:T(1024)} %refs_6_.7, bf16[128,180]{1,0:T(8,128)(2,1)} %constant.110.clone.refs_6_), custom_call_target="tpu_custom_call" | custom-call | flops 70778880 | bytes 999860 | tf_op jit(solution)/shard_map/pallas_call | solution.py:671
  4.7 7.3 %all-to-all-start = ((bf16[8,192,128]{2,1,0:T(8,128)(2,1)}), bf16[8,192,128]{2,1,0:T(8,128)(2,1)S(1)}, u32[]{:S(2)}, u32[]{:S(2)}) async-start(bf16[8,192,128]{2,1,0:T(8,128)(2,1)} %bitcast.3), calls=%async_computation | async-start | bytes 786432 | tf_op jit(solution)/shard_map/all_to_all | solution.py:760
  14.7 9.0 %all-to-all-done = bf16[8,192,128]{2,1,0:T(8,128)(2,1)S(1)} async-done(((bf16[8,192,128]{2,1,0:T(8,128)(2,1)}), bf16[8,192,128]{2,1,0:T(8,128)(2,1)S(1)}, u32[]{:S(2)}, u32[]{:S(2)}) %all-to-all-start) | async-done | bytes 393248 | tf_op jit(solution)/shard_map/all_to_all | solution.py:760
  23.6 4.5 %shard_map.327 = (bf16[8,2,96,128]{3,2,1,0:T(8,128)(2,1)}, bf16[8,128,192]{2,1,0:T(8,128)(2,1)}, bf16[8,128,192]{2,1,0:T(8,128)(2,1)}, f32[8,128,192]{2,1,0:T(8,128)}, f32[8,128,192]{2,1,0:T(8,128)}) custom-call(bf16[8,2,96,128]{3,2,1,0:T(8,128)(2,1)S(1)} %bitcast.81, bf16[192,192]{1,0:T(8,128)(2,1)S(1)} %maximum_maximum_fusion.refs_1_.refs_3_, ...), custom_call_target="tpu_custom_call" | custom-call | flops 150994944 | bytes 3499520 | tf_op jit(solution)/shard_map/pallas_call | solution.py:671
  28.1 3.6 %all-to-all-start.1 = ((bf16[8,192,128]{2,1,0:T(8,128)(2,1)}), bf16[8,192,128]{2,1,0:T(8,128)(2,1)S(1)}, u32[]{:S(2)}, u32[]{:S(2)}) async-start(bf16[8,192,128]{2,1,0:T(8,128)(2,1)} %bitcast.9), calls=%async_computation.1 | async-start | bytes 786432 | tf_op jit(solution)/shard_map/all_to_all | solution.py:763
  32.0 11.4 %all-to-all-done.1 = bf16[8,192,128]{2,1,0:T(8,128)(2,1)S(1)} async-done(((bf16[8,192,128]{2,1,0:T(8,128)(2,1)}), bf16[8,192,128]{2,1,0:T(8,128)(2,1)S(1)}, u32[]{:S(2)}, u32[]{:S(2)}) %all-to-all-start.1) | async-done | bytes 393248 | tf_op jit(solution)/shard_map/all_to_all | solution.py:763
  43.3 2.9 %shard_map.328 = (f32[2,180,768]{2,1,0:T(8,128)S(1)}, bf16[2,192,768]{2,1,0:T(8,128)(2,1)S(1)}) custom-call(s32[2,1,2]{2,1,0:T(1,128)} %refs_0_.9, s32[1]{0:T(128)} %bitcast.refs_1_, bf16[8,2,96,128]{3,2,1,0:T(8,128)(2,1)S(1)} %bitcast.82, bf16[2,180,768]{2,1,0:T(8,128)(2,1)S(1)} %bitcast.76, s32[2,1,180]{2,1,0:T(1,128)} %bitcast.103, f32[768]{0:T(1024)} %refs_6_.9, ...), custom_call_target="tpu_custom_call" | custom-call | flops 70778880 | bytes 2701748 | tf_op jit(solution)/shard_map/pallas_call | solution.py:671
  48.4 17.6 %shard_map.329 = (bf16[768,640]{1,0:T(8,128)(2,1)}, bf16[768,640]{1,0:T(8,128)(2,1)}, bf16[768,512]{1,0:T(8,128)(2,1)}, bf16[768,512]{1,0:T(8,128)(2,1)}, bf16[7...) custom-call(s32[4]{0:T(128)S(1)} %pad_add_fusion.refs_0_, ...), custom_call_target="tpu_custom_call" | custom-call | flops 10871635968 | bytes 20072468 | tf_op jit(solution)/shard_map/pallas_call | solution.py:671
  71.0 4.7 %shard_map.330 = (f32[2,180,768]{2,1,0:T(8,128)}, bf16[8,2,96,128]{3,2,1,0:T(8,128)(2,1)}, f32[3,768]{1,0:T(4,128)S(1)}) custom-call(s32[2,1,2]{2,1,0:T(1,128)} %refs_0_.9, s32[1]{0:T(128)} %bitcast.refs_1_, f32[2,180,768]{2,1,0:T(8,128)S(1)} %get-tuple-element.74.refs_2_.refs_0_, f32[2,192,768]{2,1,0:T(8,128)} %bitcast.93, ...), custom_call_target="tpu_custom_call" | custom-call | flops 70778880 | bytes 5024180 | tf_op jit(solution)/shard_map/pallas_call | solution.py:671
  75.8 3.7 %all-to-all-start.2 = ((bf16[8,192,128]{2,1,0:T(8,128)(2,1)}), bf16[8,192,128]{2,1,0:T(8,128)(2,1)S(1)}, u32[]{:S(2)}, u32[]{:S(2)}) async-start(bf16[8,192,128]{2,1,0:T(8,128)(2,1)} %bitcast.26), calls=%async_computation.2 | async-start | bytes 786432 | tf_op jit(solution)/shard_map/all_to_all | solution.py:760
  79.5 10.0 %collective-permute-done.6 = bf16[768,384]{1,0:T(8,128)(2,1)} collective-permute-done((bf16[768,384]{1,0:T(8,128)(2,1)}, bf16[768,384]{1,0:T(8,128)(2,1)}, u32[]{:S(2)}, u32[]{:S(2)}) %collective-permute-start.6) | collective-permute-done | bytes 589856 | tf_op jit(solution)/shard_map/ppermute | solution.py:698
  90.2 3.8 %shard_map.332 = (bf16[4,96,640]{2,1,0:T(8,128)(2,1)}, bf16[4,96,640]{2,1,0:T(8,128)(2,1)}, bf16[4,96,512]{2,1,0:T(8,128)(2,1)}, bf16[4,96,512]{2,1,0:T(8,128)(2...) custom-call(s32[4]{0:T(128)S(1)} %pad_add_fusion.refs_0_, bf16[4,2,96,640]{3,2,1,0:T(8,128)(2,1)} %bitcast.114, ...), custom_call_target="tpu_custom_call" | custom-call | flops 20000000000 | bytes 7077904 | tf_op jit(solution)/shard_map/pallas_call | solution.py:671
  97.1 3.9 %shard_map.333 = (bf16[8,2,96,128]{3,2,1,0:T(8,128)(2,1)}, bf16[8,128,192]{2,1,0:T(8,128)(2,1)}, bf16[8,128,192]{2,1,0:T(8,128)(2,1)}, f32[2,192]{1,0:T(2,128)S(1)}) custom-call(bf16[8,2,96,128]{3,2,1,0:T(8,128)(2,1)S(1)} %bitcast.83, f32[8,128,192]{2,1,0:T(8,128)} %get-tuple-element.81.refs_1_, f32[8,128,192]{2,1,0:T(8,128)} %get-tuple-element.82.refs_2_, ...), custom_call_target="tpu_custom_call" | custom-call | flops 301989888 | bytes 3499520 | tf_op jit(solution)/shard_map/pallas_call | solution.py:671
  101.1 3.7 %all-to-all-start.3 = ((bf16[8,192,128]{2,1,0:T(8,128)(2,1)}), bf16[8,192,128]{2,1,0:T(8,128)(2,1)S(1)}, u32[]{:S(2)}, u32[]{:S(2)}) async-start(bf16[8,192,128]{2,1,0:T(8,128)(2,1)} %bitcast.35), calls=%async_computation.3 | async-start | bytes 786432 | tf_op jit(solution)/shard_map/all_to_all | solution.py:763
  104.8 2.8 %shard_map.335 = (f32[192,128]{1,0:T(8,128)S(1)}, f32[192,128]{1,0:T(8,128)S(1)}) custom-call(s32[3]{0:T(128)S(1)} %pad_add_fusion.1.refs_0_, bf16[8,128,192]{2,1,0:T(8,128)(2,1)} %get-tuple-element.92.refs_1_, bf16[8,128,192]{2,1,0:T(8,128)(2,1)} %get-tuple-element.93.refs_2_, bf16[8,128,192]{2,1,0:T(8,128)(2,1)} %get-tuple-element.94.refs_3_, ...), custom_call_target="tpu_custom_call" | custom-call | bytes 1820172 | tf_op jit(solution)/shard_map/pallas_call | solution.py:671
  107.7 2.9 %shard_map.336 = (bf16[2,96,640]{2,1,0:T(8,128)(2,1)}, bf16[2,96,640]{2,1,0:T(8,128)(2,1)}, bf16[1,192,512]{2,1,0:T(8,128)(2,1)}, bf16[1,192,512]{2,1,0:T(8,128)...) custom-call(s32[4]{0:T(128)S(1)} %pad_add_fusion.refs_0_, bf16[2,2,96,640]{3,2,1,0:T(8,128)(2,1)} %bitcast.117, ...), custom_call_target="tpu_custom_call" | custom-call | flops 20000000000 | bytes 3538960 | tf_op jit(solution)/shard_map/pallas_call | solution.py:671
  116.8 3.3 %collective-permute-done.11.refs_8_ = f32[96,128]{1,0:T(8,128)S(1)} collective-permute-done((f32[96,128]{1,0:T(8,128)S(1)}, f32[96,128]{1,0:T(8,128)S(1)}, u32[]{:S(2)}, u32[]{:S(2)}) %collective-permute-start.11) | collective-permute-done | bytes 49184 | tf_op jit(solution)/shard_map/ppermute | solution.py:698
  120.1 3.4 %shard_map.338.refs_8_.refs_7_ = bf16[8,112,128]{2,1,0:T(8,128)(2,1)} custom-call(s32[2,1,2]{2,1,0:T(1,128)} %refs_0_.9, s32[1]{0:T(128)} %bitcast.refs_1_, bf16[8,2,96,128]{3,2,1,0:T(8,128)(2,1)S(1)} %bitcast.79, bf16[2,180,768]{2,1,0:T(8,128)(2,1)S(1)} %bitcast.77, f32[2,180,768]{2,1,0:T(8,128)} %get-tuple-element.91.refs_4_, s32[2,1,180]{2,1,0:T(1,128)} %bitcast.105, ...), custom_call_target="tpu_custom_call" | custom-call | flops 70778880 | bytes 2427316 | tf_op jit(solution)/shard_map/pallas_call | solution.py:671
  123.5 4.4 %all-to-all-start.4 = ((bf16[8,112,128]{2,1,0:T(8,128)(2,1)}), bf16[8,112,128]{2,1,0:T(8,128)(2,1)S(1)}, u32[]{:S(2)}, u32[]{:S(2)}) async-start(bf16[8,112,128]{2,1,0:T(8,128)(2,1)} %shard_map.338.refs_8_.refs_7_), calls=%async_computation.4 | async-start | bytes 458752 | tf_op jit(solution)/shard_map/all_to_all | solution.py:1010
  130.6 3.0 %collective-permute-start.17 = (bf16[96,640]{1,0:T(8,128)(2,1)}, bf16[96,640]{1,0:T(8,128)(2,1)}, u32[]{:S(2)}, u32[]{:S(2)}) collective-permute-start(bf16[96,640]{1,0:T(8,128)(2,1)} %bitcast.100), channel_id=1, source_target_pairs={{0,4},{1,5},{2,6},{3,7},{4,0},{5,1},{6,2},{7,3},{8,12},{9,13},{10,... | collective-permute-start | bytes 368648 | tf_op jit(solution)/shard_map/ppermute | solution.py:698
  133.7 2.8 %collective-permute-start.19 = (bf16[96,384]{1,0:T(8,128)(2,1)}, bf16[96,384]{1,0:T(8,128)(2,1)}, u32[]{:S(2)}, u32[]{:S(2)}) collective-permute-start(bf16[96,384]{1,0:T(8,128)(2,1)} %bitcast.112), channel_id=1, source_target_pairs={{0,4},{1,5},{2,6},{3,7},{4,0},{5,1},{6,2},{7,3},{8,12},{9,13},{10,... | collective-permute-start | bytes 221192 | tf_op jit(solution)/shard_map/ppermute | solution.py:698
  136.5 2.9 %shard_map.331.refs_6_ = bf16[180,2,768]{2,1,0:T(2,128)(2,1)} custom-call(f32[2,180,768]{2,1,0:T(8,128)S(1)} %get-tuple-element.74.refs_2_.refs_0_, f32[2,192,768]{2,1,0:T(8,128)} %bitcast.94, bf16[2,192,768]{2,1,0:T(8,128)(2,1)S(1)} %bitcast.85, f32[768]{0:T(1024)} %refs_3_.1, bf16[8,2,96,128]{3,2,1,0:T(8,128)(2,1)} %get-tuple-element.80.refs_4_.refs_7_), custom_call_target="tpu_custom_call" | custom-call | bytes 3431424 | tf_op jit(solution)/shard_map/pallas_call | solution.py:671
  139.4 4.1 %shard_map.339.refs_7_ = f32[2,180,1,768]{3,2,1,0:T(1,128)} custom-call(s32[2,1,2]{2,1,0:T(1,128)} %refs_0_.9, s32[1]{0:T(128)} %bitcast.refs_1_, bf16[8,2,96,128]{3,2,1,0:T(8,128)(2,1)S(1)} %bitcast.80, bf16[2,180,768]{2,1,0:T(8,128)(2,1)S(1)} %bitcast.78, f32[2,180,768]{2,1,0:T(8,128)} %get-tuple-element.91.refs_4_, s32[2,1,180]{2,1,0:T(1,128)} %bitcast.106, ...), custom_call_target="tpu_custom_call" | custom-call | flops 70778880 | bytes 3208628 | tf_op jit(solution)/shard_map/pallas_call | solution.py:671
  144.6 4.1 %collective-permute-done.19.refs_3_.refs_5_ = bf16[96,384]{1,0:T(8,128)(2,1)} collective-permute-done((bf16[96,384]{1,0:T(8,128)(2,1)}, bf16[96,384]{1,0:T(8,128)(2,1)}, u32[]{:S(2)}, u32[]{:S(2)}) %collective-permute-start.19) | collective-permute-done | bytes 73760 | tf_op jit(solution)/shard_map/ppermute | solution.py:698
  (68 shorter events, 30.8 us)
Async XLA Ops:
  4.7 19.0 %all-to-all-start = ((bf16[8,192,128]{2,1,0:T(8,128)(2,1)}), bf16[8,192,128]{2,1,0:T(8,128)(2,1)S(1)}, u32[]{:S(2)}, u32[]{:S(2)}) async-start(bf16[8,192,128]{2,1,0:T(8,128)(2,1)} %bitcast.3), calls=%async_computation | async-start | bytes 786432 | tf_op jit(solution)/shard_map/all_to_all | solution.py:760
  28.1 15.2 %all-to-all-start.1 = ((bf16[8,192,128]{2,1,0:T(8,128)(2,1)}), bf16[8,192,128]{2,1,0:T(8,128)(2,1)S(1)}, u32[]{:S(2)}, u32[]{:S(2)}) async-start(bf16[8,192,128]{2,1,0:T(8,128)(2,1)} %bitcast.9), calls=%async_computation.1 | async-start | bytes 786432 | tf_op jit(solution)/shard_map/all_to_all | solution.py:763
  31.9 14.6 %collective-permute-start.1 = (bf16[384,768]{1,0:T(8,128)(2,1)S(1)}, bf16[384,768]{1,0:T(8,128)(2,1)}, u32[]{:S(2)}, u32[]{:S(2)}) collective-permute-start(bf16[384,768]{1,0:T(8,128)(2,1)S(1)} %bitcast.90), channel_id=1, source_target_pairs={{0,8},{8,0},{16,24},{24,16},{1,9},{9,1},{17,25},{25,17},{2,10},{10... | collective-permute-start | bytes 1769480 | tf_op jit(solution)/shard_map/ppermute | solution.py:698
  46.2 2.2 %collective-permute-start = (bf16[384,768]{1,0:T(8,128)(2,1)S(1)}, bf16[384,768]{1,0:T(8,128)(2,1)}, u32[]{:S(2)}, u32[]{:S(2)}) collective-permute-start(bf16[384,768]{1,0:T(8,128)(2,1)S(1)} %bitcast.88), channel_id=1, source_target_pairs={{0,8},{8,0},{16,24},{24,16},{1,9},{9,1},{17,25},{25,17},{2,10},{10... | collective-permute-start | bytes 1769480 | tf_op jit(solution)/shard_map/ppermute | solution.py:698
  66.0 24.2 %collective-permute-start.4 = (bf16[768,640]{1,0:T(8,128)(2,1)}, bf16[768,640]{1,0:T(8,128)(2,1)}, u32[]{:S(2)}, u32[]{:S(2)}) collective-permute-start(bf16[768,640]{1,0:T(8,128)(2,1)} %get-tuple-element.84), channel_id=1, source_target_pairs={{0,16},{8,24},{16,0},{24,8},{1,17},{9,25},{17,1},{25,9},{2,18},{10... | collective-permute-start | bytes 2949128 | tf_op jit(solution)/shard_map/ppermute | solution.py:698
  67.6 22.3 %collective-permute-start.5 = (bf16[768,512]{1,0:T(8,128)(2,1)}, bf16[768,512]{1,0:T(8,128)(2,1)}, u32[]{:S(2)}, u32[]{:S(2)}) collective-permute-start(bf16[768,512]{1,0:T(8,128)(2,1)} %get-tuple-element.86), channel_id=1, source_target_pairs={{0,1},{1,0},{2,3},{3,2},{4,5},{5,4},{6,7},{7,6},{8,9},{9,8},{10,11... | collective-permute-start | bytes 2359304 | tf_op jit(solution)/shard_map/ppermute | solution.py:698
  69.0 20.4 %collective-permute-start.6 = (bf16[768,384]{1,0:T(8,128)(2,1)}, bf16[768,384]{1,0:T(8,128)(2,1)}, u32[]{:S(2)}, u32[]{:S(2)}) collective-permute-start(bf16[768,384]{1,0:T(8,128)(2,1)} %get-tuple-element.88), channel_id=1, source_target_pairs={{0,2},{1,3},{2,0},{3,1},{4,6},{5,7},{6,4},{7,5},{8,10},{9,11},{10,... | collective-permute-start | bytes 1769480 | tf_op jit(solution)/shard_map/ppermute | solution.py:698
  75.8 21.4 %all-to-all-start.2 = ((bf16[8,192,128]{2,1,0:T(8,128)(2,1)}), bf16[8,192,128]{2,1,0:T(8,128)(2,1)S(1)}, u32[]{:S(2)}, u32[]{:S(2)}) async-start(bf16[8,192,128]{2,1,0:T(8,128)(2,1)} %bitcast.26), calls=%async_computation.2 | async-start | bytes 786432 | tf_op jit(solution)/shard_map/all_to_all | solution.py:760
  94.0 13.6 %collective-permute-start.9 = (bf16[384,640]{1,0:T(8,128)(2,1)}, bf16[384,640]{1,0:T(8,128)(2,1)}, u32[]{:S(2)}, u32[]{:S(2)}) collective-permute-start(bf16[384,640]{1,0:T(8,128)(2,1)} %bitcast.96), channel_id=1, source_target_pairs={{0,1},{1,0},{2,3},{3,2},{4,5},{5,4},{6,7},{7,6},{8,9},{9,8},{10,11... | collective-permute-start | bytes 1474568 | tf_op jit(solution)/shard_map/ppermute | solution.py:698
  96.2 11.4 %collective-permute-start.10 = (bf16[384,512]{1,0:T(8,128)(2,1)}, bf16[384,512]{1,0:T(8,128)(2,1)}, u32[]{:S(2)}, u32[]{:S(2)}) collective-permute-start(bf16[384,512]{1,0:T(8,128)(2,1)} %bitcast.107), channel_id=1, source_target_pairs={{0,2},{1,3},{2,0},{3,1},{4,6},{5,7},{6,4},{7,5},{8,10},{9,11},{10,... | collective-permute-start | bytes 1179656 | tf_op jit(solution)/shard_map/ppermute | solution.py:698
  96.2 8.6 %collective-permute-start.7 = (bf16[384,384]{1,0:T(8,128)(2,1)}, bf16[384,384]{1,0:T(8,128)(2,1)S(1)}, u32[]{:S(2)}, u32[]{:S(2)}) collective-permute-start(bf16[384,384]{1,0:T(8,128)(2,1)} %bitcast.108), channel_id=1, source_target_pairs={{0,16},{8,24},{16,0},{24,8},{1,17},{9,25},{17,1},{25,9},{2,18},{10... | collective-permute-start | bytes 884744 | tf_op jit(solution)/shard_map/ppermute | solution.py:698
  101.1 19.0 %all-to-all-start.3 = ((bf16[8,192,128]{2,1,0:T(8,128)(2,1)}), bf16[8,192,128]{2,1,0:T(8,128)(2,1)S(1)}, u32[]{:S(2)}, u32[]{:S(2)}) async-start(bf16[8,192,128]{2,1,0:T(8,128)(2,1)} %bitcast.35), calls=%async_computation.3 | async-start | bytes 786432 | tf_op jit(solution)/shard_map/all_to_all | solution.py:763
  110.6 17.3 %collective-permute-start.12 = (bf16[192,640]{1,0:T(8,128)(2,1)}, bf16[192,640]{1,0:T(8,128)(2,1)}, u32[]{:S(2)}, u32[]{:S(2)}) collective-permute-start(bf16[192,640]{1,0:T(8,128)(2,1)} %bitcast.98), channel_id=1, source_target_pairs={{0,2},{1,3},{2,0},{3,1},{4,6},{5,7},{6,4},{7,5},{8,10},{9,11},{10,... | collective-permute-start | bytes 737288 | tf_op jit(solution)/shard_map/ppermute | solution.py:698
  112.7 15.2 %collective-permute-start.13 = (bf16[192,512]{1,0:T(8,128)(2,1)}, bf16[192,512]{1,0:T(8,128)(2,1)}, u32[]{:S(2)}, u32[]{:S(2)}) collective-permute-start(bf16[192,512]{1,0:T(8,128)(2,1)} %bitcast.109), channel_id=1, source_target_pairs={{0,16},{8,24},{16,0},{24,8},{1,17},{9,25},{17,1},{25,9},{2,18},{10... | collective-permute-start | bytes 589832 | tf_op jit(solution)/shard_map/ppermute | solution.py:698
  113.9 14.0 %collective-permute-start.14 = (bf16[192,384]{1,0:T(8,128)(2,1)}, bf16[192,384]{1,0:T(8,128)(2,1)}, u32[]{:S(2)}, u32[]{:S(2)}) collective-permute-start(bf16[192,384]{1,0:T(8,128)(2,1)} %bitcast.110), channel_id=1, source_target_pairs={{0,1},{1,0},{2,3},{3,2},{4,5},{5,4},{6,7},{7,6},{8,9},{9,8},{10,11... | collective-permute-start | bytes 442376 | tf_op jit(solution)/shard_map/ppermute | solution.py:698
  116.0 4.2 %collective-permute-start.11 = (f32[96,128]{1,0:T(8,128)S(1)}, f32[96,128]{1,0:T(8,128)S(1)}, u32[]{:S(2)}, u32[]{:S(2)}) collective-permute-start(f32[96,128]{1,0:T(8,128)S(1)} %get-tuple-element.108), channel_id=1, source_target_pairs={{0,16},{8,24},{16,0},{24,8},{1,17},{9,25},{17,1},{25,9},{2,18},{10... | collective-permute-start | bytes 147464 | tf_op jit(solution)/shard_map/ppermute | solution.py:698
  116.8 19.7 %collective-permute-start.2 = (bf16[384,768]{1,0:T(8,128)(2,1)S(1)}, bf16[384,768]{1,0:T(8,128)(2,1)S(1)}, u32[]{:S(2)}, u32[]{:S(2)}) collective-permute-start(bf16[384,768]{1,0:T(8,128)(2,1)S(1)} %get-tuple-element.77), channel_id=1, source_target_pairs={{0,8},{8,0},{16,24},{24,16},{1,9},{9,1},{17,25},{25,17},{2,10},{10... | collective-permute-start | bytes 1769480 | tf_op jit(solution)/shard_map/ppermute | solution.py:698
  123.5 20.0 %all-to-all-start.4 = ((bf16[8,112,128]{2,1,0:T(8,128)(2,1)}), bf16[8,112,128]{2,1,0:T(8,128)(2,1)S(1)}, u32[]{:S(2)}, u32[]{:S(2)}) async-start(bf16[8,112,128]{2,1,0:T(8,128)(2,1)} %shard_map.338.refs_8_.refs_7_), calls=%async_computation.4 | async-start | bytes 458752 | tf_op jit(solution)/shard_map/all_to_all | solution.py:1010
  130.6 18.1 %collective-permute-start.17 = (bf16[96,640]{1,0:T(8,128)(2,1)}, bf16[96,640]{1,0:T(8,128)(2,1)}, u32[]{:S(2)}, u32[]{:S(2)}) collective-permute-start(bf16[96,640]{1,0:T(8,128)(2,1)} %bitcast.100), channel_id=1, source_target_pairs={{0,4},{1,5},{2,6},{3,7},{4,0},{5,1},{6,2},{7,3},{8,12},{9,13},{10,... | collective-permute-start | bytes 368648 | tf_op jit(solution)/shard_map/ppermute | solution.py:698
  133.6 15.1 %collective-permute-start.18 = (bf16[96,512]{1,0:T(8,128)(2,1)}, bf16[96,512]{1,0:T(8,128)(2,1)}, u32[]{:S(2)}, u32[]{:S(2)}) collective-permute-start(bf16[96,512]{1,0:T(8,128)(2,1)} %bitcast.111), channel_id=1, source_target_pairs={{0,4},{1,5},{2,6},{3,7},{4,0},{5,1},{6,2},{7,3},{8,12},{9,13},{10,... | collective-permute-start | bytes 294920 | tf_op jit(solution)/shard_map/ppermute | solution.py:698
  133.7 15.0 %collective-permute-start.19 = (bf16[96,384]{1,0:T(8,128)(2,1)}, bf16[96,384]{1,0:T(8,128)(2,1)}, u32[]{:S(2)}, u32[]{:S(2)}) collective-permute-start(bf16[96,384]{1,0:T(8,128)(2,1)} %bitcast.112), channel_id=1, source_target_pairs={{0,4},{1,5},{2,6},{3,7},{4,0},{5,1},{6,2},{7,3},{8,12},{9,13},{10,... | collective-permute-start | bytes 221192 | tf_op jit(solution)/shard_map/ppermute | solution.py:698
  143.6 5.7 %collective-permute-start.15 = (bf16[656,128]{1,0:T(8,128)(2,1)S(1)}, bf16[656,128]{1,0:T(8,128)(2,1)S(1)}, u32[]{:S(2)}, u32[]{:S(2)}) collective-permute-start(bf16[656,128]{1,0:T(8,128)(2,1)S(1)} %shard_map.341.refs_1_), channel_id=1, source_target_pairs={{0,16},{8,24},{16,0},{24,8},{1,17},{9,25},{17,1},{25,9},{2,18},{10... | collective-permute-start | bytes 503816 | tf_op jit(solution)/shard_map/ppermute | solution.py:698
  149.2 2.7 %collective-permute-start.16 = (bf16[656,128]{1,0:T(8,128)(2,1)S(1)}, bf16[656,128]{1,0:T(8,128)(2,1)S(1)}, u32[]{:S(2)}, u32[]{:S(2)}) collective-permute-start(bf16[656,128]{1,0:T(8,128)(2,1)S(1)} %shard_map.341.refs_1_), channel_id=1, source_target_pairs={{0,8},{8,0},{16,24},{24,16},{1,9},{9,1},{17,25},{25,17},{2,10},{10... | collective-permute-start | bytes 503816 | tf_op jit(solution)/shard_map/ppermute | solution.py:698
  149.3 2.6 %collective-permute-start.20 = (bf16[656,128]{1,0:T(8,128)(2,1)S(1)}, bf16[656,128]{1,0:T(8,128)(2,1)S(1)}, u32[]{:S(2)}, u32[]{:S(2)}) collective-permute-start(bf16[656,128]{1,0:T(8,128)(2,1)S(1)} %shard_map.343), channel_id=1, source_target_pairs={{0,8},{8,0},{16,24},{24,16},{1,9},{9,1},{17,25},{25,17},{2,10},{10... | collective-permute-start | bytes 503816 | tf_op jit(solution)/shard_map/ppermute | solution.py:698
  (6 other events, 53.1 us)
